TPU v7x, 256 devices: a whole 4x4x8 slice. The times are simulated.
256 devices in a mesh: tm: 8 (over y, core), doc: 32 (over x, z).
Axes of the slice: x: 4, y: 4, z: 8, core: 2. Of those that a mesh axis runs over, the one named last changes fastest.
Arguments:
- beta_mean: float32 [16, 65536, 200], P('tm', 'doc'), may hold values from -9 to 230
- word_ids: int32 [8192, 128], P(('tm', 'doc')), may hold values from 0 to 65535, as said below
- word_counts: int32 [8192, 128], P(('tm', 'doc')), may hold values from 0 to 8
- doc_slice: int32 [8192], P(('tm', 'doc')), may hold values from 0 to 15, as said below
- dirichlet: float32 [200], replicated, may hold values from 0.05 to 0.5
- drift_var: float32 [200], replicated, may hold values from 0.002 to 0.5
- obs_var: float32 [200], replicated, may hold values from 0.05 to 1
Outputs:
- smoothed_mean: float32 [16, 65536, 200], P('tm', 'doc')
- doc_topics: float32 [8192, 200], P(('tm', 'doc'))
Inputs may be any that keep to these rules, and one draw needn't show every extreme that they name: `word_ids`: vocabulary range b holds the words b * 2048 to (b + 1) * 2048 - 1. Over the 4096 slots of each aligned block of 32 documents, at most 160 hold words of one range; in every block some range holds exactly 160, the same range for all blocks of the same 1024 documents. A word may fill several slots of a document. `doc_slice`: the documents of rows i * 1024 to (i + 1) * 1024 - 1 belong to slices i * 2 to (i + 1) * 2 - 1.
All inputs are finite; a program needn't handle non-finite values.
Results may differ from a plain program's by a relative error of at most 0.0034.
Values may be sent and summed in bfloat16 or wider, within the bound.
No kernel may reach another device: no remote copies, remote signals or barrier semaphores. Data moves between devices by JAX's collectives and lax.ppermute only.
A program may use at most 128 MiB of HBM per device.

v0:
```python
import jax
import jax.numpy as jnp
from jax import lax
from jax.sharding import PartitionSpec as P

E_ITERS = 4


pseudo_count = 0.1
prior_var = 1.0


def carried_in(value, axis, join, neutral):
    place = lax.axis_index(axis)
    gathered = jax.tree.map(
        lambda a, kind: lax.all_gather(a.astype(kind), axis), value, (jnp.bfloat16, jnp.bfloat16)
    )
    state = jax.tree.map(lambda a, e: jnp.zeros_like(a) + jnp.asarray(e, a.dtype), value, neutral)

    def one(hop, state):
        return join(
            state,
            jax.tree.map(
                lambda a, own: lax.dynamic_index_in_dim(a, hop, 0, False).astype(own.dtype),
                gathered,
                value,
            ),
        )

    return lax.fori_loop(0, place, one, state)


def entering(value, axis, join, neutral):
    count, mine = (lax.axis_size(axis), lax.axis_index(axis))
    pieces = jax.tree.map(lambda part: lax.all_gather(part, axis), value)
    pieces = jax.tree.map(lambda part: part[::-1], pieces)
    mine = count - 1 - mine
    total = jax.tree.map(
        lambda part, zero: jnp.full_like(part, 0) + jnp.asarray(zero, part.dtype), value, neutral
    )

    def hop(position, total):
        longer = join(total, jax.tree.map(lambda part: part[position], pieces))
        return jax.tree.map(lambda new, old: jnp.where(position < mine, new, old), longer, total)

    return lax.fori_loop(0, count - 1, hop, total)


def digamma_series(value):
    correction = jnp.zeros_like(value)
    for shift_step in range(6):
        correction = correction + 1.0 / (value + float(shift_step))
    shifted = value + 6.0
    inverse = 1.0 / shifted
    inverse_square = inverse * inverse
    series = inverse_square * (
        1.0 / 12.0 - inverse_square * (1.0 / 120.0 - inverse_square * (1.0 / 252.0))
    )
    return jnp.log(shifted) - 0.5 * inverse - series - correction


def expectation(tok_beta, tok_count, dirichlet):
    doc_gamma = dirichlet[None, :] + jnp.sum(tok_count, axis=1, keepdims=True) / dirichlet.shape[0]
    for iteration in range(E_ITERS):
        log_theta = digamma_series(doc_gamma) - digamma_series(
            jnp.sum(doc_gamma, axis=1, keepdims=True)
        )
        theta_exp = jnp.exp(log_theta)
        norm_tok = jnp.einsum(
            "dk,dnk->dn",
            theta_exp,
            tok_beta,
            precision=lax.Precision.HIGHEST,
            preferred_element_type=jnp.float32,
        )
        slot_ratio = tok_count / norm_tok
        doc_gamma = dirichlet[None, :] + theta_exp * jnp.einsum(
            "dn,dnk->dk",
            slot_ratio,
            tok_beta,
            precision=lax.Precision.HIGHEST,
            preferred_element_type=jnp.float32,
        )
    return (doc_gamma, theta_exp, slot_ratio)


def variances(drift_var, obs_var, length):

    def advance(filt_prev, placeholder):
        predicted = filt_prev + drift_var
        gain_now = predicted / (predicted + obs_var)
        filt_now = (1.0 - gain_now) * predicted
        return (filt_now, (gain_now, filt_now))

    initial = jnp.full(drift_var.shape, prior_var, jnp.float32)
    final_var, outputs = lax.scan(advance, initial, None, length=length)
    return outputs


def compose_maps(earlier, latter):
    return (latter[0] * earlier[0], latter[0][None, :] * earlier[1] + latter[1])


def per_device(beta_mean, word_ids, word_counts, doc_slice, dirichlet, drift_var, obs_var):
    slice_dev, vocab_shard, topics = beta_mean.shape
    doc_dev, token_width = word_ids.shape
    doc_peers = lax.axis_size("doc")
    time_peers = lax.axis_size("tm")
    time_index = lax.axis_index("tm")
    table_rows = slice_dev * vocab_shard
    vocab_top = lax.pmax(jnp.max(beta_mean, axis=1), "doc")
    vocab_total = lax.psum(jnp.sum(jnp.exp(beta_mean - vocab_top[:, None, :]), axis=1), "doc")
    log_norm = vocab_top + jnp.log(vocab_total)
    expected_beta = (
        jnp.exp(beta_mean - log_norm[:, None, :]).astype(jnp.bfloat16).reshape(table_rows, topics)
    )
    slot_count = doc_dev * token_width
    capacity = slot_count * 5 // (4 * doc_peers)
    flat_words = word_ids.reshape(slot_count)
    owners = flat_words // vocab_shard
    local_slice = doc_slice - time_index * slice_dev
    slot_row = jnp.repeat(local_slice, token_width) * vocab_shard + flat_words % vocab_shard
    slot_doc = jnp.repeat(jnp.arange(doc_dev, dtype=jnp.int32), token_width)
    request_code = slot_doc * table_rows + slot_row
    ordering = jnp.argsort(owners, stable=True)
    owners_sorted = owners[ordering]
    owner_load = jnp.sum(
        (owners[:, None] == jnp.arange(doc_peers, dtype=jnp.int32)[None, :]).astype(jnp.int32),
        axis=0,
    )
    owner_start = jnp.cumsum(owner_load) - owner_load
    place_sorted = (
        owners_sorted * capacity
        + jnp.arange(slot_count, dtype=jnp.int32)
        - owner_start[owners_sorted]
    )
    placement = jnp.zeros((slot_count,), jnp.int32).at[ordering].set(place_sorted)
    request = (
        jnp.full((doc_peers * capacity,), -1, jnp.int32)
        .at[placement]
        .set(request_code)
        .reshape(doc_peers, capacity)
    )
    received = lax.all_to_all(request, "doc", split_axis=0, concat_axis=0, tiled=True)
    rows_wanted = jnp.where(received >= 0, received % table_rows, 0)
    fetched = expected_beta[rows_wanted]
    replies = lax.all_to_all(fetched, "doc", split_axis=0, concat_axis=0, tiled=True)
    replies, received, fetched = (replies, received, fetched)
    tok_beta = replies.reshape(doc_peers * capacity, topics)[placement].reshape(
        doc_dev, token_width, topics
    )
    tok_count = word_counts.astype(jnp.float32)
    doc_gamma, theta_exp, slot_ratio = expectation(tok_beta, tok_count, dirichlet)
    slot_terms = (theta_exp[:, None, :] * slot_ratio[:, :, None]).reshape(slot_count, topics)
    outgoing = (
        jnp.zeros((doc_peers * capacity, topics), jnp.float32)
        .at[placement]
        .set(slot_terms)
        .reshape(doc_peers, capacity, topics)
    )
    arrived = lax.all_to_all(
        outgoing.astype(jnp.bfloat16), "doc", split_axis=0, concat_axis=0, tiled=True
    ).astype(outgoing.dtype)
    contrib = arrived * fetched
    target_row = jnp.where(received >= 0, received % table_rows, table_rows)
    word_stats = jax.ops.segment_sum(
        contrib.reshape(doc_peers * capacity, topics),
        target_row.reshape(doc_peers * capacity),
        num_segments=table_rows + 1,
    )
    word_stats = word_stats[:table_rows].reshape(slice_dev, vocab_shard, topics)
    total_slices = slice_dev * time_peers
    gain_all, var_all = variances(drift_var, obs_var, total_slices)
    first_slice = time_index * slice_dev
    gain_here = lax.dynamic_slice_in_dim(gain_all, first_slice, slice_dev, 0)
    var_here = lax.dynamic_slice_in_dim(var_all, first_slice, slice_dev, 0)
    slice_number = first_slice + jnp.arange(slice_dev, dtype=jnp.int32)
    smooth_gain = jnp.where(
        (slice_number == total_slices - 1)[:, None], 0.0, var_here / (var_here + drift_var[None, :])
    )
    pseudo = jnp.log(word_stats + pseudo_count)
    slope_now = jnp.ones((topics,), jnp.float32)
    offset = jnp.zeros((vocab_shard, topics), jnp.float32)
    slopes = []
    offsets = []
    for position in range(slice_dev):
        retained = 1.0 - gain_here[position]
        slope_now = retained * slope_now
        offset = retained[None, :] * offset + gain_here[position][None, :] * pseudo[position]
        slopes.append(slope_now)
        offsets.append(offset)
    identity = (jnp.ones((topics,), jnp.float32), jnp.zeros((vocab_shard, topics), jnp.float32))
    carried = carried_in((slope_now, offset), "tm", compose_maps, identity)
    filtered = [
        offsets[position] + slopes[position][None, :] * carried[1] for position in range(slice_dev)
    ]
    factor = jnp.ones((topics,), jnp.float32)
    constant = jnp.zeros((vocab_shard, topics), jnp.float32)
    factors = [None] * slice_dev
    constants = [None] * slice_dev
    for position in reversed(range(slice_dev)):
        weight = smooth_gain[position]
        factor = weight * factor
        constant = (1.0 - weight)[None, :] * filtered[position] + weight[None, :] * constant
        factors[position] = factor
        constants[position] = constant
    from_ahead = entering((factor, constant), "tm", compose_maps, identity)
    smoothed = jnp.stack(
        [
            constants[position] + factors[position][None, :] * from_ahead[1]
            for position in range(slice_dev)
        ]
    )
    return (smoothed, doc_gamma)


def solution(mesh):
    return jax.shard_map(
        per_device,
        mesh=mesh,
        in_specs=(
            P("tm", "doc", None),
            P(("tm", "doc"), None),
            P(("tm", "doc"), None),
            P(("tm", "doc")),
            P(),
            P(),
            P(),
        ),
        out_specs=(P("tm", "doc", None), P(("tm", "doc"), None)),
        check_vma=False,
    )
```

profile of v0, /device:TPU:1, one launch (start us, length us, event | category | flops | bytes accessed | tf_op | source)
XLA Modules:
  0.0 693.7 jit_solution(11381500754262118763)
XLA Ops:
  10.5 5.8 sort.17
  16.3 23.0 %gather_fusion = s32[4096]{0:T(1024)S(1)} fusion(s32[4096]{0:T(1024)S(1)} %get-tuple-element.318, s32[4096]{0:T(1024)S(1)} %get-tuple-element.319), kind=kCustom, calls=%fused_computation | custom fusion | bytes 49152 | tf_op jit(solution)/shard_map/gather | solution.py:126
  39.3 4.4 compare_select_fusion.8
  45.0 15.8 %select_subtract_fusion = s32[4096]{0:T(1024)S(1)} fusion(pred[4096]{0:T(1024)(128)(4,1)S(1)} %get-tuple-element.270, pred[4096]{0:T(1024)(128)(4,1)S(1)} %get-tuple-element.269, pred[4096]{0:T(1024)(128)(4,1)S(1)} %get-tuple-element.268, pred[4096]{0:T(1024)(128)(4,1)S(1)} %get-tuple-element.267, pred[4096]{0:T(1024)(128)(4,1)S(1)} %get-tuple-element.266, ...), kind=kLoop, calls=%fused_computation.139 | loop fusion | flops 114688 | bytes 151652 | tf_op jit(solution)/shard_map/sub | solution.py:133
  60.8 15.5 %scatter_custom_fusion = s32[4096]{0:T(1024)S(1)} fusion(s32[4096]{0:T(1024)S(1)} %get-tuple-element.320, s32[4096]{0:T(1024)S(1)} %select_subtract_fusion, s32[]{:T(128)} %constant.143.clone.1), kind=kCustom, calls=%fused_computation.157 | custom fusion | bytes 16388 | tf_op jit(solution)/shard_map/scatter | solution.py:137
  76.3 15.5 %scatter_custom_fusion.1 = s32[5120]{0:T(1024)S(1)} fusion(s32[4096]{0:T(1024)S(1)} %get-tuple-element.316, s32[4096]{0:T(1024)S(1)} %get-tuple-element.317, s32[]{:T(128)} %constant.145.clone.1), kind=kCustom, calls=%fused_computation.150 | custom fusion | bytes 20484 | tf_op jit(solution)/shard_map/scatter | solution.py:141
  92.6 11.9 %all-to-all-start = ((s32[32,1,160]{2,1,0:T(1,128)}), s32[32,1,160]{2,1,0:T(1,128)S(1)}, u32[]{:S(2)}, u32[]{:S(2)}) async-start(s32[32,1,160]{2,1,0:T(1,128)} %all_to_all.16), calls=%async_computation | async-start | bytes 65536 | tf_op jit(solution)/shard_map/all_to_all | solution.py:144
  104.7 60.5 %pmax.7 = f32[2,200]{1,0:T(2,128)S(1)} all-reduce(f32[2,200]{1,0:T(2,128)S(1)} %reduce_max.9), channel_id=1, replica_groups=mesh['tm'=8,'doc'=32] {'doc'}, use_global_device_ids=true, to_apply=%region_10.11 | all-reduce | flops 400 | bytes 3200 | tf_op jit(solution)/shard_map/pmax | solution.py:111
  165.8 55.7 %psum.7 = f32[2,200]{1,0:T(2,128)S(1)} all-reduce(f32[2,200]{1,0:T(2,128)S(1)} %exponential_reduce_fusion), channel_id=1, replica_groups=mesh['tm'=8,'doc'=32] {'doc'}, use_global_device_ids=true, to_apply=%region_12.13 | all-reduce | flops 400 | bytes 3200 | tf_op jit(solution)/shard_map/psum | solution.py:112
  226.3 21.1 %gather_fusion.1 = bf16[5120,200]{1,0:T(8,128)(2,1)} fusion(bf16[4096,200]{1,0:T(8,128)(2,1)S(1)} %bitcast.213, s32[5120]{0:T(1024)S(1)} %broadcast_clamp_fusion), kind=kCustom, calls=%fused_computation.1 | custom fusion | bytes 4116480 | tf_op jit(solution)/shard_map/gather | solution.py:146
  247.4 4.4 all-to-all-start.1
  252.3 32.8 %all-to-all-done.1 = bf16[32,160,200]{2,1,0:T(8,128)(2,1)S(1)} async-done(((bf16[32,160,200]{2,1,0:T(8,128)(2,1)}), bf16[32,160,200]{2,1,0:T(8,128)(2,1)S(1)}, u32[]{:S(2)}, u32[]{:S(2)}) %all-to-all-start.1) | async-done | bytes 2048032 | tf_op jit(solution)/shard_map/all_to_all | solution.py:147
  286.7 15.1 %gather_fusion.2 = bf16[4096,200]{1,0:T(8,128)(2,1)S(1)} fusion(bf16[5120,200]{1,0:T(8,128)(2,1)} %bitcast.222, s32[4096]{0:T(1024)S(1)} %get-tuple-element.315), kind=kCustom, calls=%fused_computation.2 | custom fusion | bytes 3293184 | tf_op jit(solution)/shard_map/gather | solution.py:149
  315.1 20.4 %scatter_custom_fusion.2 = f32[5120,200]{1,0:T(8,128)} fusion(s32[4096]{0:T(1024)S(1)} %get-tuple-element.316, f32[4096,200]{1,0:T(8,128)} %bitcast_multiply_fusion, f32[]{:T(128)} %constant.142.clone.1), kind=kCustom, calls=%fused_computation.23 | custom fusion | bytes 4096512 | tf_op jit(solution)/shard_map/scatter | solution.py:158
  335.5 4.3 convert_element_type.42
  339.8 6.6 all-to-all-start.2
  349.2 30.7 %all-to-all-done.2 = bf16[32,160,200]{2,1,0:T(8,128)(2,1)} async-done(((bf16[32,160,200]{2,1,0:T(8,128)(2,1)}), bf16[32,160,200]{2,1,0:T(8,128)(2,1)}, u32[]{:S(2)}, u32[]{:S(2)}) %all-to-all-start.2) | async-done | bytes 2048032 | tf_op jit(solution)/shard_map/all_to_all | solution.py:161
  379.9 5.7 convert_multiply_fusion
  385.6 33.3 %scatter_custom_fusion.3 = f32[4097,200]{1,0:T(8,128)} fusion(s32[5120]{0:T(1024)S(1)} %bitcast.253, f32[5120,200]{1,0:T(8,128)} %bitcast.227, f32[]{:T(128)} %constant.142.clone.1), kind=kCustom, calls=%fused_computation.25 | custom fusion | flops 1024000 | bytes 3278112 | tf_op jit(solution)/shard_map/scatter-add | solution.py:166
  425.4 42.1 %all-gather.1 = bf16[8,1,200]{2,1,0:T(2,128)(2,1)S(1)} all-gather(bf16[1,1,200]{2,1,0:T(2,128)(2,1)S(1)} %get-tuple-element.311), channel_id=1, replica_groups=mesh['tm'=8,'doc'=32] {'tm'}, dimensions={0}, use_global_device_ids=true | all-gather | bytes 3600 | tf_op jit(solution)/shard_map/all_gather | solution.py:16
  467.5 29.7 %all-gather.6.cloned.1.call-done = bf16[8,2048,200]{1,2,0:T(8,128)(2,1)} async-done(((bf16[1,2048,200]{1,2,0:T(8,128)(2,1)}), bf16[8,2048,200]{1,2,0:T(8,128)(2,1)}) %all-gather.6.cloned.1.call-update) | async-done | bytes 6553616 | tf_op jit(solution)/shard_map/all_gather | solution.py:16
  498.7 6.7 while.41
  505.4 5.1 multiply_add_fusion
  510.6 46.9 %all-gather.2 = f32[8,1,200]{2,1,0:T(1,128)S(1)} all-gather(f32[1,1,200]{2,1,0:T(1,128)S(1)} %bitcast.257), channel_id=1, replica_groups=mesh['tm'=8,'doc'=32] {'tm'}, dimensions={0}, use_global_device_ids=true | all-gather | bytes 7200 | tf_op jit(solution)/shard_map/all_gather | solution.py:35
  559.0 78.5 %all-gather.8.cloned.1.call-done = f32[16384,200]{1,0:T(8,128)} async-done(((f32[2048,200]{1,0:T(8,128)}), f32[16384,200]{1,0:T(8,128)}) %all-gather.8.cloned.1.call-update) | async-done | bytes 13107216 | tf_op jit(solution)/shard_map/all_gather | solution.py:35
  637.6 11.3 %rev.7 = f32[8,2048,200]{2,1,0:T(8,128)} reverse(f32[8,2048,200]{2,1,0:T(8,128)} %bitcast.225), dimensions={0} | reverse | bytes 26214400 | tf_op jit(solution)/shard_map/rev | solution.py:36
  648.8 26.2 %while.43 = (s32[]{:T(128)}, f32[2048,200]{1,0:T(8,128)}, s32[]{:T(128)}, f32[8,200]{1,0:T(8,128)S(1)}, f32[8,2048,200]{2,1,0:T(8,128)}, /*index=5*/s32[]{:T(128)}, s32[]{:T(128)}) while((s32[]{:T(128)}, f32[2048,200]{1,0:T(8,128)}, s32[]{:T(128)}, f32[8,200]{1,0:T(8,128)S(1)}, f32[8,2048,200]{2,1,0:T(8,128)}, ...), condition=%wide.region_21.22_spmd.clone, body=%wide.region_20.21_spmd.clone.sunk | while | flops 1638404 | bytes 4917713 | solution.py:46
  652.2 3.8 fusion.80
  656.0 3.8 fusion.80
  663.6 3.8 fusion.80
  675.0 4.4 add_bitcast_fusion.1
  681.6 5.2 copy.35
  (156 shorter events, 63.6 us)
Async XLA Ops:
  16.3 88.2 %copy-start.3 = (f32[2,2048,200]{1,2,0:T(8,128)S(1)}, f32[2,2048,200]{1,2,0:T(8,128)}, u32[]{:S(2)}) copy-start(f32[2,2048,200]{1,2,0:T(8,128)} %param.13) | copy-start | bytes 9830404
  92.6 133.4 %all-to-all-start = ((s32[32,1,160]{2,1,0:T(1,128)}), s32[32,1,160]{2,1,0:T(1,128)S(1)}, u32[]{:S(2)}, u32[]{:S(2)}) async-start(s32[32,1,160]{2,1,0:T(1,128)} %all_to_all.16), calls=%async_computation | async-start | bytes 65536 | tf_op jit(solution)/shard_map/all_to_all | solution.py:144
  247.4 4.4 copy-start.4
  247.4 4.6 copy-start.5
  247.4 37.7 %all-to-all-start.1 = ((bf16[32,160,200]{2,1,0:T(8,128)(2,1)}), bf16[32,160,200]{2,1,0:T(8,128)(2,1)S(1)}, u32[]{:S(2)}, u32[]{:S(2)}) async-start(bf16[32,160,200]{2,1,0:T(8,128)(2,1)} %bitcast.223), calls=%async_computation.1 | async-start | bytes 5242880 | tf_op jit(solution)/shard_map/all_to_all | solution.py:147
  285.2 1.5 copy-start
  339.8 6.9 copy-start.6
  339.8 6.9 copy-start.7
  339.8 40.1 %all-to-all-start.2 = ((bf16[32,160,200]{2,1,0:T(8,128)(2,1)}), bf16[32,160,200]{2,1,0:T(8,128)(2,1)}, u32[]{:S(2)}, u32[]{:S(2)}) async-start(bf16[32,160,200]{2,1,0:T(8,128)(2,1)} %bitcast.226), calls=%async_computation.2 | async-start | bytes 5242880 | tf_op jit(solution)/shard_map/all_to_all | solution.py:161
  346.4 150.9 %all-gather.6.cloned.1.call-start = ((), (), s32[]{:S(2)}) async-start(), calls=%async_computation.3 | async-start | bytes 7372800 | tf_op jit(solution)/shard_map/all_gather | solution.py:16
  421.6 2.0 copy-start.2
  425.4 212.2 %all-gather.8.cloned.1.call-start = ((), (), s32[]{:S(2)}) async-start(), calls=%async_computation.4 | async-start | bytes 18874368 | tf_op jit(solution)/shard_map/all_gather | solution.py:35
  648.8 26.2 %copy-start.1 = (f32[2048,200]{1,0:T(8,128)S(1)}, f32[2048,200]{1,0:T(8,128)}, u32[]{:S(2)}) copy-start(f32[2048,200]{1,0:T(8,128)} %get-tuple-element.177) | copy-start | bytes 4915204
Sparse Core Ops, SparseCore 0:
  425.5 71.7 all-gather.5
  510.7 126.8 all-gather.7
where the time goes:
time: 695 us; the launch traced here: 694 us
  blocking collectives  205 us (29%)
  waiting for transfers between devices  172 us (25%)
  local copies, waits for them, and re-layouts  144 us (21%)
  other arithmetic  124 us (18%)
  starting transfers between devices  23.1 us (3%)
  between operations  14.4 us (2%)
  matrix products  10.6 us (2%)
    all_gather x1, waiting for transfers between devices, entering(): pieces = jax.tree.map(lambda part: lax.all_gather(part, axis), value)  78.5 us
    pmax x1, blocking collectives, per_device(): vocab_top = lax.pmax(jnp.max(beta_mean, axis=1), 'doc')  60.5 us
    psum x1, blocking collectives, per_device(): lax.psum(jnp.sum(jnp.exp(beta_mean - vocab_top[:, None, :]), axis=1), 'doc')  55.7 us
    all_gather x1, blocking collectives, entering(): pieces = jax.tree.map(lambda part: lax.all_gather(part, axis), value)  46.9 us
    all_gather x1, blocking collectives, carried_in(): lax.all_gather(a.astype(kind), axis)  42.1 us
    scatter-add x1, other arithmetic, per_device(): jax.ops.segment_sum(contrib.reshape(doc_peers * capacity, topics), target...  33.3 us
    all_to_all x1, waiting for transfers between devices, per_device(): lax.all_to_all(fetched, 'doc', split_axis=0, concat_axis=0, tiled=True)  32.8 us
    all_to_all x1, waiting for transfers between devices, per_device(): lax.all_to_all(outgoing.astype(jnp.bfloat16), 'doc', split_axis=0, concat...  30.7 us
  transfers between devices with their start and end apart: 5, of which 4 were waited for; matrix products, arithmetic and copies ran while one was open for 1% of the time, Pallas kernels for 0%

commit v1 on v0

v1 whole, which is shorter than its diff:
```python
import functools
import math

import jax
import jax.numpy as jnp
from jax import lax
from jax.experimental import pallas as pl
from jax.experimental.pallas import tpu as pltpu
from jax.sharding import PartitionSpec as P

E_ITERS = 4
PSEUDO = 0.1
PRIOR_VAR = 1.0
LOG_PSEUDO = math.log(PSEUDO)
F32, BF16, I32 = jnp.float32, jnp.bfloat16, jnp.int32
NT = (((1,), (1,)), ((), ()))
TN = (((0,), (0,)), ((), ()))
SMEM = pl.BlockSpec(memory_space=pltpu.SMEM)


def iota(shape, axis):
    return lax.broadcasted_iota(I32, shape, axis)


def mm(a, b):
    return jnp.dot(a, b, preferred_element_type=F32)


def mmg(a, b, dims):
    return lax.dot_general(a, b, dims, preferred_element_type=F32)


def call(kernel, out_shape, *args, specs=None, scratch=()):
    specs = specs or [pl.BlockSpec()] * len(args)
    return pl.pallas_call(kernel, out_shape=out_shape, in_specs=specs, scratch_shapes=scratch)(*args)


def shape(dims, dtype):
    return jax.ShapeDtypeStruct(dims, dtype)


def place_kernel(peers, capacity, shift, ids_ref, counts_ref, slice_ref, code_ref, doc_ref, count_ref):
    docs, width = ids_ref.shape
    ids = ids_ref[...]
    owner = lax.shift_right_logical(ids, shift)
    word = ids & ((1 << shift) - 1)
    low = (word & 255).astype(F32)
    high = (lax.shift_right_logical(word, 8) + (slice_ref[...] << (shift - 8)) + 1).astype(F32)
    counts = counts_ref[...].astype(F32)
    before = (iota((width, width), 0) < iota((width, width), 1)).astype(F32).astype(BF16)
    owners = iota((peers, width), 0)
    ranks = iota((capacity, width), 0).astype(F32)
    hot = [(owners == owner[d : d + 1, :]).astype(F32) for d in range(docs)]
    inside = mm(jnp.concatenate(hot, axis=0).astype(BF16), before)
    start = jnp.zeros((peers, 1), F32)
    left, right = [], []
    for d in range(docs):
        mine = hot[d]
        rank = jnp.sum(mine * (inside[d * peers : (d + 1) * peers] + start), axis=0, keepdims=True)
        start = start + jnp.sum(mine, axis=1, keepdims=True)
        right.append((ranks == rank).astype(F32).astype(BF16))
        left.append(
            jnp.concatenate(
                [
                    mine * low[d : d + 1],
                    mine * high[d : d + 1],
                    mine * float(d),
                    mine * counts[d : d + 1],
                ],
                axis=0,
            ).astype(BF16)
        )
    placed = mmg(jnp.concatenate(left, axis=1), jnp.concatenate(right, axis=1), NT)
    low_p, high_p, doc_p, count_p = (placed[i * peers : (i + 1) * peers] for i in range(4))
    code_ref[...] = doc_p * 8192.0 + high_p * 256.0 + low_p
    doc_ref[...] = jnp.where(high_p > 0.5, doc_p, -1.0)
    count_ref[...] = count_p


def row_of(code, shift):
    at = (code & 8191) - 256
    return at & ((1 << shift) - 1), lax.shift_right_logical(at, shift) & 1


def fetch_kernel(shift, beta_ref, norm_ref, code_ref, table_ref, out_ref):
    rows, words = beta_ref.shape
    topics = rows // 2
    step = 16

    def fill(i, carry):
        at = pl.ds(pl.multiple_of(i * step, step), step)
        table_ref[at, :] = jnp.exp(beta_ref[at, :] - norm_ref[at, :]).astype(BF16)
        return carry

    lax.fori_loop(0, rows // step, fill, 0)
    chunk = code_ref.shape[1]

    def one(i, carry):
        word, part = row_of(code_ref[pl.ds(i, 1), :].astype(I32), shift)
        hot = (iota((words, chunk), 0) == word).astype(F32).astype(BF16)
        both = mm(table_ref[...], hot)
        picked = jnp.where(part == 0, both[:topics], both[topics:])
        out_ref[pl.ds(pl.multiple_of(i * chunk, chunk), chunk), :] = jnp.transpose(picked).astype(BF16)
        return carry

    lax.fori_loop(0, code_ref.shape[0], one, 0)


def digamma(value):
    correction = jnp.zeros_like(value)
    for j in range(6):
        correction = correction + 1.0 / (value + float(j))
    shifted = value + 6.0
    inverse = 1.0 / shifted
    square = inverse * inverse
    series = square * (1.0 / 12.0 - square * (1.0 / 120.0 - square * (1.0 / 252.0)))
    return jnp.log(shifted) - 0.5 * inverse - series - correction


def split(value):
    high = value.astype(BF16)
    return high, (value - high.astype(F32)).astype(BF16)


def estep_kernel(tok_ref, doc_ref, count_ref, counts_ref, dirichlet_ref, gamma_ref, theta_ref, ratio_ref):
    docs = counts_ref.shape[0]
    topics = dirichlet_ref.shape[1]
    places = tok_ref.shape[0]
    dirichlet = dirichlet_ref[...]
    total = jnp.sum(counts_ref[...].astype(F32), axis=1, keepdims=True)
    gamma = dirichlet + total / float(topics)
    doc = doc_ref[...]
    mask = iota((docs, places), 0) == doc.astype(I32)
    for step in range(E_ITERS):
        theta = jnp.exp(digamma(gamma) - digamma(jnp.sum(gamma, axis=1, keepdims=True)))
        norm = mmg(jnp.concatenate(split(theta), axis=0), tok_ref[...], NT)
        norm = norm[:docs] + norm[docs:]
        norm = jnp.sum(jnp.where(mask, norm, 0.0), axis=0, keepdims=True)
        ratio = jnp.where(doc >= 0.0, count_ref[...] / norm, 0.0)
        high, low = split(ratio)
        spread = jnp.concatenate(
            [jnp.where(mask, high.astype(F32), 0.0), jnp.where(mask, low.astype(F32), 0.0)], axis=0
        ).astype(BF16)
        part = mm(spread, tok_ref[...])
        gamma = dirichlet + theta * (part[:docs] + part[docs:])
    gamma_ref[...] = gamma
    theta_ref[...] = theta.astype(BF16)
    ratio_ref[0:1, :] = high.astype(F32)
    ratio_ref[1:2, :] = low.astype(F32)


def stats_kernel(
    shift, per, docs, core_ref, theta_ref, code_ref, high_ref, low_ref, table_ref, keep_ref, send_ref, total_ref
):
    groups, places = code_ref.shape
    rows, words = table_ref.shape
    topics = rows // 2
    sources = theta_ref.shape[0] // groups
    capacity = places // sources
    lane = iota((1, places), 1)
    offset = jnp.zeros((1, places), I32)
    for s in range(1, sources):
        offset = offset + jnp.where(lane >= s * capacity, docs, 0)
    for g in range(groups):
        code = code_ref[g : g + 1, :].astype(I32)
        word, part = row_of(code, shift)
        key = lax.shift_right_logical(code, 13) + offset
        theta = theta_ref[g * sources : (g + 1) * sources, :docs, :].reshape(sources * docs, topics)
        mask = iota((sources * docs, places), 0) == key
        high = jnp.where(mask, high_ref[g : g + 1, :], 0.0).astype(BF16)
        low = jnp.where(mask, low_ref[g : g + 1, :], 0.0).astype(BF16)
        factor = mmg(theta, high, TN) + mmg(theta, low, TN)
        factor = jnp.concatenate(
            [jnp.where(part == 0, factor, 0.0), jnp.where(part == 1, factor, 0.0)], axis=0
        ).astype(BF16)
        column = jnp.transpose(jnp.broadcast_to(word.astype(F32), (8, places)))[:, 0:1].astype(I32)

        def one(j, carry):
            at = pl.ds(pl.multiple_of(j * per, per), per)
            hot = (iota((places, per), 1) + j * per == column).astype(F32).astype(BF16)
            new = mm(factor, hot)
            if g == 0:
                total_ref[:, at] = new
            else:
                total_ref[:, at] = total_ref[:, at] + new
            return carry

        lax.fori_loop(0, words // per, one, 0)
    half = words // 2
    first = core_ref[0] == 0
    step = 16

    def finish(i, carry):
        at = pl.ds(pl.multiple_of(i * step, step), step)
        shifted = jnp.log(1.0 + (1.0 / PSEUDO) * (table_ref[at, :].astype(F32) * total_ref[at, :]))
        left, right = shifted[:, :half], shifted[:, half:]
        keep_ref[at, :] = jnp.where(first, left, right)
        send_ref[at, :] = jnp.where(first, right, left)
        return carry

    lax.fori_loop(0, rows // step, finish, 0)


G0, S0, H0, B0, PHI0, QK, KNEXT, PHI, WF0, WQ0, NCOEF = 0, 4, 8, 12, 16, 20, 21, 22, 23, 27, 32


def coef_kernel(chips, chip_ref, drift_ref, obs_ref, out_ref):
    per = 4
    length = chips * per
    drift, obs = drift_ref[...], obs_ref[...]
    one, zero = jnp.ones_like(drift), jnp.zeros_like(drift)
    var = one * PRIOR_VAR
    gain, smooth = [], []
    for t in range(length):
        pred = var + drift
        now = pred / (pred + obs)
        var = (1.0 - now) * pred
        gain.append(now)
        smooth.append(var / (var + drift) if t < length - 1 else zero)
    level, forward = zero, []
    for t in range(length):
        level = (1.0 - gain[t]) * level + gain[t]
        forward.append(level)
    ones_smoothed = [None] * length
    level = zero
    for t in reversed(range(length)):
        level = (1.0 - smooth[t]) * forward[t] + smooth[t] * level
        ones_smoothed[t] = level
    beta, phi, sigma, kappa = [], [], [], []
    for c in range(chips):
        run, back, k = one, one, zero
        for t in range(c * per, (c + 1) * per):
            run = run * (1.0 - gain[t])
            phi.append(run)
            beta.append(back * (1.0 - smooth[t]))
            k = k + beta[t] * run
            back = back * smooth[t]
        sigma.append(back)
        kappa.append(k)
    total = [phi[c * per + per - 1] for c in range(chips)]
    lead = [zero] * (chips + 1)
    for c in reversed(range(chips)):
        lead[c] = kappa[c] + sigma[c] * lead[c + 1] * total[c]
    chip = chip_ref[0]
    for c in range(chips):
        rows = [None] * NCOEF
        for u in range(per):
            t = c * per + u
            rows[G0 + u], rows[S0 + u], rows[H0 + u] = gain[t], smooth[t], ones_smoothed[t] * LOG_PSEUDO
            rows[B0 + u], rows[PHI0 + u] = beta[t], phi[t]
        rows[QK], rows[KNEXT], rows[PHI] = sigma[c] * lead[c + 1], lead[c + 1], total[c]
        for j in range(chips):
            behind, ahead = zero, zero
            if j < c:
                behind = one
                for m in range(j + 1, c):
                    behind = behind * total[m]
            if j > c:
                ahead = one
                for m in range(c + 1, j):
                    ahead = ahead * sigma[m]
            rows[WF0 + j], rows[WQ0 + j] = behind, ahead

        @pl.when(chip == c)
        def _():
            for r in range(NCOEF):
                out_ref[r : r + 1, :] = zero if rows[r] is None else rows[r]


def local_filter(coef, values):
    out, level = [], None
    for u in range(4):
        gain = coef[:, G0 + u : G0 + u + 1]
        level = gain * values[u] if level is None else (1.0 - gain) * level + gain * values[u]
        out.append(level)
    return out


def four(first, keep_ref, recv_ref, topics, at):
    own = [keep_ref[pl.ds(u * topics + at, 8), :] for u in range(2)]
    other = [recv_ref[pl.ds(u * topics + at, 8), :] for u in range(2)]
    return [jnp.where(first, own[u], other[u]) for u in range(2)] + [
        jnp.where(first, other[u], own[u]) for u in range(2)
    ]


def combine_kernel(where_ref, coef_ref, keep_ref, recv_ref, out_ref):
    chips, topics, _ = out_ref.shape
    first, chip = where_ref[1] == 0, where_ref[0]

    def block(i, carry):
        at = pl.multiple_of(i * 8, 8)
        coef = coef_ref[pl.ds(at, 8), :]
        local = local_filter(coef, four(first, keep_ref, recv_ref, topics, at))
        back = coef[:, QK : QK + 1] * local[3]
        for u in range(4):
            back = back + coef[:, B0 + u : B0 + u + 1] * local[u]
        for j in range(chips):
            out_ref[j, pl.ds(at, 8), :] = jnp.where(j > chip, local[3], back).astype(BF16)
        return carry

    lax.fori_loop(0, topics // 8, block, 0)


def smooth_kernel(where_ref, coef_ref, keep_ref, recv_ref, far_ref, own_ref, other_ref):
    chips, topics, _ = far_ref.shape
    first = where_ref[1] == 0

    def block(i, carry):
        at = pl.multiple_of(i * 8, 8)
        coef = coef_ref[pl.ds(at, 8), :]

        def take(r):
            return coef[:, r : r + 1]

        local = local_filter(coef, four(first, keep_ref, recv_ref, topics, at))
        entering = jnp.zeros_like(local[0])
        ahead = jnp.zeros_like(local[0])
        for j in range(chips):
            far = far_ref[j, pl.ds(at, 8), :].astype(F32)
            entering = entering + take(WF0 + j) * far
            ahead = ahead + take(WQ0 + j) * far
        level = ahead + take(KNEXT) * (local[3] + take(PHI) * entering)
        means = [None] * 4
        for u in reversed(range(4)):
            weight = take(S0 + u)
            level = (1.0 - weight) * (local[u] + take(PHI0 + u) * entering) + weight * level
            means[u] = level + take(H0 + u)
        for u in range(2):
            own_ref[u, pl.ds(at, 8), :] = jnp.where(first, means[u], means[u + 2])
            other_ref[u, pl.ds(at, 8), :] = jnp.where(first, means[u + 2], means[u])
        return carry

    lax.fori_loop(0, topics // 8, block, 0)


def per_device(beta_mean, word_ids, word_counts, doc_slice, dirichlet, drift_var, obs_var):
    slice_dev, vocab_shard, topics = beta_mean.shape
    docs, width = word_ids.shape
    peers = lax.axis_size("doc")
    time_peers = lax.axis_size("tm")
    here = lax.axis_index("tm")
    chip, core = here // 2, here % 2
    chips = time_peers // 2
    shift = vocab_shard.bit_length() - 1
    slots = docs * width
    capacity = slots * 5 // (4 * peers)
    places = peers * capacity
    half = vocab_shard // 2
    where = jnp.stack([chip, core]).astype(I32)

    beta = jnp.swapaxes(beta_mean, 1, 2)
    local_slice = (doc_slice - here * slice_dev).astype(I32).reshape(docs, 1)
    code, doc, count = call(
        functools.partial(place_kernel, peers, capacity, shift),
        [shape((peers, capacity), F32)] * 3,
        word_ids,
        word_counts,
        local_slice,
    )
    top = jnp.max(beta, axis=2)
    mass = jnp.sum(jnp.exp(beta - top[:, :, None]), axis=2)
    stats = jnp.concatenate([top.reshape(1, 1, -1), mass.reshape(1, 1, -1)], axis=2)
    outgoing = jnp.concatenate(
        [code.reshape(peers, 1, capacity), jnp.broadcast_to(stats, (peers, 1, stats.shape[2]))], axis=2
    )
    arrived = lax.all_to_all(outgoing, "doc", split_axis=0, concat_axis=0, tiled=True)
    coef = call(
        functools.partial(coef_kernel, chips),
        shape((NCOEF, topics), F32),
        where,
        drift_var.reshape(1, topics),
        obs_var.reshape(1, topics),
        specs=[SMEM, pl.BlockSpec(), pl.BlockSpec()],
    )
    coef = coef.T
    asked = arrived[:, 0, :capacity]
    tops = arrived[:, 0, capacity : capacity + slice_dev * topics]
    masses = arrived[:, 0, capacity + slice_dev * topics :]
    highest = jnp.max(tops, axis=0)
    log_norm = highest + jnp.log(jnp.sum(masses * jnp.exp(tops - highest), axis=0))
    chunk = 256
    table, fetched = call(
        functools.partial(fetch_kernel, shift),
        [shape((slice_dev * topics, vocab_shard), BF16), shape((places, topics), BF16)],
        beta.reshape(slice_dev * topics, vocab_shard),
        log_norm.reshape(-1, 1),
        asked.reshape(places // chunk, chunk),
    )
    replies = lax.all_to_all(
        fetched.reshape(peers, capacity, topics), "doc", split_axis=0, concat_axis=0, tiled=True
    )
    gamma, theta, ratio = call(
        estep_kernel,
        [shape((docs, topics), F32), shape((docs, topics), BF16), shape((2, places), F32)],
        replies.reshape(places, topics),
        doc.reshape(1, places),
        count.reshape(1, places),
        word_counts,
        dirichlet.reshape(1, topics),
    )
    ratio = jnp.swapaxes(ratio.reshape(2, peers, capacity), 0, 1).reshape(peers, 2 * capacity).astype(BF16)
    ratio = jnp.pad(ratio, ((0, 0), (0, 2 * topics - 2 * capacity))).reshape(peers, 2, topics)
    factors = jnp.concatenate([jnp.broadcast_to(theta[None], (peers, docs, topics)), ratio], axis=1)
    factors = lax.all_to_all(factors, "doc", split_axis=0, concat_axis=0, tiled=True)
    group = 4
    ratios = factors[:, docs:, :].reshape(peers, 2 * topics).astype(F32)
    keep, send = call(
        functools.partial(stats_kernel, shift, 256, docs),
        [shape((slice_dev * topics, half), F32)] * 2,
        core.astype(I32).reshape(1),
        factors,
        asked.reshape(group, places // group),
        ratios[:, :capacity].reshape(group, places // group),
        ratios[:, capacity : 2 * capacity].reshape(group, places // group),
        table,
        specs=[SMEM] + [pl.BlockSpec()] * 5,
        scratch=[pltpu.VMEM((slice_dev * topics, vocab_shard), F32)],
    )
    swap = [(i, i ^ 1) for i in range(time_peers)]
    recv = lax.ppermute(send, "tm", swap)
    combined = call(
        combine_kernel,
        shape((chips, topics, half), BF16),
        where,
        coef,
        keep,
        recv,
        specs=[SMEM] + [pl.BlockSpec()] * 3,
    )
    far = lax.all_to_all(
        combined,
        "tm",
        split_axis=0,
        concat_axis=0,
        tiled=True,
        axis_index_groups=[[2 * i + c for i in range(chips)] for c in range(2)],
    )
    own, other = call(
        smooth_kernel,
        [shape((slice_dev, topics, half), F32)] * 2,
        where,
        coef,
        keep,
        recv,
        far,
        specs=[SMEM] + [pl.BlockSpec()] * 4,
    )
    partner = lax.ppermute(other, "tm", swap)
    first = core == 0
    means = jnp.concatenate([jnp.where(first, own, partner), jnp.where(first, partner, own)], axis=2)
    return jnp.swapaxes(means, 1, 2), gamma


def solution(mesh):
    return jax.shard_map(
        per_device,
        mesh=mesh,
        in_specs=(
            P("tm", "doc", None),
            P(("tm", "doc"), None),
            P(("tm", "doc"), None),
            P(("tm", "doc")),
            P(),
            P(),
            P(),
        ),
        out_specs=(P("tm", "doc", None), P(("tm", "doc"), None)),
        check_vma=False,
    )
```

time: 695 us -> 234 us (0.34)
  blocking collectives: 205 us -> 46.5 us
  local copies, waits for them, and re-layouts: 144 us -> 12.9 us
  other arithmetic: 124 us -> 9.63 us
  waiting for transfers between devices: 172 us -> 77.4 us
  Pallas kernels: 0 us -> 69.3 us
  between operations: 14.4 us -> 0.77 us
  matrix products: 10.6 us -> 0 us
    all_gather x2 -> x0, waiting for transfers between devices: 108 us -> none  [the longest x1 78.5 us: entering(): pieces = jax.tree.map(lambda part: lax.all_gather(part, axis), value)]
    all_gather x2 -> x0, blocking collectives: 89 us -> none  [the longest x1 46.9 us: entering(): pieces = jax.tree.map(lambda part: lax.all_gather(part, axis), value)]
    pallas_call x0 -> x7, Pallas kernels: none -> 69.3 us  [call(): pl.pallas_call(kernel, out_shape=out_shape, in_specs=specs, scratch_shape...]
    gather x5 -> x0, local copies, waits for them, and re-layouts: 60.7 us -> none  [the longest x1 23 us: per_device(): owners_sorted = owners[ordering]]
    pmax x1 -> x0, blocking collectives: 60.5 us -> none  [per_device(): vocab_top = lax.pmax(jnp.max(beta_mean, axis=1), 'doc')]
    psum x1 -> x0, blocking collectives: 55.7 us -> none  [per_device(): lax.psum(jnp.sum(jnp.exp(beta_mean - vocab_top[:, None, :]), axis=1), 'doc')]
    scatter x3 -> x0, local copies, waits for them, and re-layouts: 51.5 us -> none  [the longest x1 20.4 us: per_device(): outgoing = jnp.zeros((doc_peers * capacity, topics), jnp.float32).at[plac...]
    all_to_all x0 -> x2, blocking collectives: none -> 46.5 us  [the longest x1 25.7 us: per_device(): lax.all_to_all(combined, 'tm', split_axis=0, concat_axis=0, tiled=True, a...]
  transfers between devices with their start and end apart: 5 -> 4, of which waited for: 4 -> 3; matrix products, arithmetic and copies ran while one was open for 1% -> 2% of each run, Pallas kernels for 0% -> 1%
where the time goes in v1:
time: 234 us
  waiting for transfers between devices  77.4 us (33%)
  Pallas kernels  69.3 us (30%)
  blocking collectives  46.5 us (20%)
  starting transfers between devices  17.1 us (7%)
  local copies, waits for them, and re-layouts  12.9 us (6%)
  other arithmetic  9.63 us (4%)
    pallas_call x7, Pallas kernels, call(): pl.pallas_call(kernel, out_shape=out_shape, in_specs=specs, scratch_shape...  69.3 us
    all_to_all x1, waiting for transfers between devices, per_device(): lax.all_to_all(fetched.reshape(peers, capacity, topics), 'doc', split_axi...  58.6 us
    all_to_all x1, blocking collectives, per_device(): lax.all_to_all(combined, 'tm', split_axis=0, concat_axis=0, tiled=True, a...  25.7 us
    all_to_all x1, blocking collectives, per_device(): lax.all_to_all(outgoing, 'doc', split_axis=0, concat_axis=0, tiled=True)  20.8 us
    all_to_all x1, waiting for transfers between devices, per_device(): lax.all_to_all(factors, 'doc', split_axis=0, concat_axis=0, tiled=True)  15.5 us
    all_to_all x1, starting transfers between devices, per_device(): lax.all_to_all(factors, 'doc', split_axis=0, concat_axis=0, tiled=True)  6.81 us
    ppermute x1, starting transfers between devices, per_device(): recv = lax.ppermute(send, 'tm', swap)  5 us
  transfers between devices with their start and end apart: 4, of which 3 were waited for; matrix products, arithmetic and copies ran while one was open for 2% of the time, Pallas kernels for 1%

profile of v1, /device:TPU:1, one launch (start us, length us, event | category | flops | bytes accessed | tf_op | source)
XLA Modules:
  0.0 233.7 jit_solution(5171946596353264196)
XLA Ops:
  0.6 2.3 bitcast_reduce_fusion
  4.3 0.7 copy.17.slice_ref
  5.0 2.2 shard_map.87
  7.2 0.8 copy.18
  8.2 20.8 %all_to_all.20 = f32[32,1,960]{2,1,0:T(1,128)S(1)} all-to-all(f32[32,1,960]{2,1,0:T(1,128)S(1)} %pad_maximum_fusion.1), channel_id=1, replica_groups=mesh['tm'=8,'doc'=32] {'doc'}, dimensions={0} | all-to-all | bytes 245760 | tf_op jit(solution)/shard_map/all_to_all | solution.py:367
  29.5 0.7 reshape_squeeze.6.code_ref
  30.2 0.8 copy.20.norm_ref
  31.1 19.7 %shard_map.88 = (bf16[400,2048]{1,0:T(8,128)(2,1)}, bf16[5120,200]{1,0:T(8,128)(2,1)}) custom-call(f32[400,2048]{1,0:T(8,128)} %bitcast.36, f32[400,1]{1,0:T(8,128)} %copy.20.norm_ref, f32[20,256]{1,0:T(8,128)} %reshape_squeeze.6.code_ref), custom_call_target="tpu_custom_call" | custom-call | tf_op jit(solution)/shard_map/pallas_call | solution.py:35
  50.7 4.2 %all-to-all-start.1 = ((bf16[32,160,200]{2,1,0:T(8,128)(2,1)}), bf16[32,160,200]{2,1,0:T(8,128)(2,1)S(1)}, u32[]{:S(2)}, u32[]{:S(2)}) async-start(bf16[32,160,200]{2,1,0:T(8,128)(2,1)} %bitcast.38), calls=%async_computation.1 | async-start | bytes 5242880 | tf_op jit(solution)/shard_map/all_to_all | solution.py:390
  55.0 0.7 reshape.88.doc_ref
  55.7 0.7 reshape.89.count_ref
  56.4 58.6 %all-to-all-done.1 = bf16[32,160,200]{2,1,0:T(8,128)(2,1)S(1)} async-done(((bf16[32,160,200]{2,1,0:T(8,128)(2,1)}), bf16[32,160,200]{2,1,0:T(8,128)(2,1)S(1)}, u32[]{:S(2)}, u32[]{:S(2)}) %all-to-all-start.1) | async-done | bytes 2048032 | tf_op jit(solution)/shard_map/all_to_all | solution.py:390
  115.0 1.5 copy-done.1
  116.5 8.6 %shard_map.89 = (f32[32,200]{1,0:T(8,128)}, bf16[32,200]{1,0:T(8,128)(2,1)}, f32[2,5120]{1,0:T(2,128)}) custom-call(bf16[5120,200]{1,0:T(8,128)(2,1)} %bitcast.37, f32[1,5120]{1,0:T(1,128)} %reshape.88.doc_ref, f32[1,5120]{1,0:T(1,128)} %reshape.89.count_ref, s32[32,128]{1,0:T(8,128)} %counts_ref.3, f32[1,200]{1,0:T(1,128)} %bitcast.44), custom_call_target="tpu_custom_call" | custom-call | tf_op jit(solution)/shard_map/pallas_call | solution.py:35
  125.1 0.8 convert_element_type.20
  126.3 0.8 broadcast_in_dim.8
  127.0 1.0 pad_maximum_fusion
  128.0 6.8 %all-to-all-start.2 = ((bf16[32,34,200]{2,1,0:T(8,128)(2,1)}), bf16[32,34,200]{2,1,0:T(8,128)(2,1)S(1)}, u32[]{:S(2)}, u32[]{:S(2)}) async-start(bf16[32,34,200]{2,1,0:T(8,128)(2,1)} %pad_maximum_fusion), calls=%async_computation.2 | async-start | bytes 1310720 | tf_op jit(solution)/shard_map/all_to_all | solution.py:405
  135.5 15.5 %all-to-all-done.2.theta_ref = bf16[32,34,200]{2,1,0:T(8,128)(2,1)S(1)} async-done(((bf16[32,34,200]{2,1,0:T(8,128)(2,1)}), bf16[32,34,200]{2,1,0:T(8,128)(2,1)S(1)}, u32[]{:S(2)}, u32[]{:S(2)}) %all-to-all-start.2) | async-done | bytes 435232 | tf_op jit(solution)/shard_map/all_to_all | solution.py:405
  152.0 0.7 reshape.92.high_ref
  152.6 23.8 %shard_map.90 = (f32[400,1024]{1,0:T(8,128)}, f32[400,1024]{1,0:T(8,128)}) custom-call(s32[1]{0:T(128)} %bitcast.1.core_ref, bf16[32,34,200]{2,1,0:T(8,128)(2,1)} %copy-done.3, f32[4,1280]{1,0:T(4,128)} %reshape_squeeze.7.code_ref, f32[4,1280]{1,0:T(4,128)} %reshape.92.high_ref, f32[4,1280]{1,0:T(4,128)} %reshape.93.low_ref, ...), custom_call_target="tpu_custom_call" | custom-call | tf_op jit(solution)/shard_map/pallas_call | solution.py:35
  176.5 5.0 %collective-permute-start = (f32[400,1024]{1,0:T(8,128)}, f32[400,1024]{1,0:T(8,128)S(1)}, u32[]{:S(2)}, u32[]{:S(2)}) collective-permute-start(f32[400,1024]{1,0:T(8,128)} %get-tuple-element.22), channel_id=1, source_target_pairs={{0,32},{32,0},{64,96},{96,64},{128,160},{160,128},{192,224},{224,1... | collective-permute-start | bytes 4915208 | tf_op jit(solution)/shard_map/ppermute | solution.py:421
  182.1 1.5 shard_map.86
  183.6 1.5 copy.16
  185.1 1.2 copy-done.2
  186.3 5.6 %shard_map.91 = bf16[4,200,1024]{2,1,0:T(8,128)(2,1)} custom-call(s32[2]{0:T(128)} %pad_add_fusion.chip_ref.where_ref, f32[200,32]{1,0:T(8,128)} %bitcast.39, f32[400,1024]{1,0:T(8,128)} %get-tuple-element.21.keep_ref, f32[400,1024]{1,0:T(8,128)} %copy-done.2), custom_call_target="tpu_custom_call" | custom-call | tf_op jit(solution)/shard_map/pallas_call | solution.py:35
  191.9 25.7 %all_to_all.21.far_ref = bf16[4,200,1024]{2,1,0:T(8,128)(2,1)} all-to-all(bf16[4,200,1024]{2,1,0:T(8,128)(2,1)} %shard_map.91), channel_id=1, replica_groups={{0,64,128,192},{32,96,160,224},{1,65,129,193},{33,97,161,225},{2,66,130..., dimensions={0} | all-to-all | bytes 3276800 | tf_op jit(solution)/shard_map/all_to_all | solution.py:431
  217.6 7.8 %shard_map.92 = (f32[2,200,1024]{2,1,0:T(8,128)}, f32[2,200,1024]{2,1,0:T(8,128)}) custom-call(s32[2]{0:T(128)} %pad_add_fusion.chip_ref.where_ref, f32[200,32]{1,0:T(8,128)} %bitcast.40, f32[400,1024]{1,0:T(8,128)} %get-tuple-element.21.keep_ref, f32[400,1024]{1,0:T(8,128)} %copy-done.2, bf16[4,200,1024]{2,1,0:T(8,128)(2,1)} %all_to_all.21.far_ref), custom_call_target="tpu_custom_call" | custom-call | tf_op jit(solution)/shard_map/pallas_call | solution.py:35
  225.4 1.1 collective-permute-start.1
  226.5 3.3 %collective-permute-done.1 = f32[2,200,1024]{2,1,0:T(8,128)S(1)} collective-permute-done((f32[2,200,1024]{2,1,0:T(8,128)}, f32[2,200,1024]{2,1,0:T(8,128)S(1)}, u32[]{:S(2)}, u32[]{:S(2)}) %collective-permute-start.1) | collective-permute-done | bytes 1638432 | tf_op jit(solution)/shard_map/ppermute | solution.py:449
  229.8 1.9 broadcast_select_fusion.1
  231.7 1.9 maximum_bitcast_fusion
  (35 shorter events, 4.6 us)
Async XLA Ops:
  0.6 2.9 %copy-start = (f32[2,2048,200]{1,2,0:T(8,128)S(1)}, f32[2,2048,200]{1,2,0:T(8,128)}, u32[]{:S(2)}) copy-start(f32[2,2048,200]{1,2,0:T(8,128)} %param.7) | copy-start | bytes 9830404
  3.5 0.8 copy-start.6
  50.7 4.2 %copy-start.5 = (f32[32,160]{1,0:T(8,128)S(1)}, f32[32,160]{1,0:T(8,128)}, u32[]{:S(2)}) copy-start(f32[32,160]{1,0:T(8,128)} %get-tuple-element.16) | copy-start | bytes 61444
  50.7 4.9 %copy-start.4 = (f32[32,160]{1,0:T(8,128)S(1)}, f32[32,160]{1,0:T(8,128)}, u32[]{:S(2)}) copy-start(f32[32,160]{1,0:T(8,128)} %get-tuple-element.17) | copy-start | bytes 61444
  50.7 64.2 %all-to-all-start.1 = ((bf16[32,160,200]{2,1,0:T(8,128)(2,1)}), bf16[32,160,200]{2,1,0:T(8,128)(2,1)S(1)}, u32[]{:S(2)}, u32[]{:S(2)}) async-start(bf16[32,160,200]{2,1,0:T(8,128)(2,1)} %bitcast.38), calls=%async_computation.1 | async-start | bytes 5242880 | tf_op jit(solution)/shard_map/all_to_all | solution.py:390
  115.0 1.5 copy-start.1
  128.0 23.0 %all-to-all-start.2 = ((bf16[32,34,200]{2,1,0:T(8,128)(2,1)}), bf16[32,34,200]{2,1,0:T(8,128)(2,1)S(1)}, u32[]{:S(2)}, u32[]{:S(2)}) async-start(bf16[32,34,200]{2,1,0:T(8,128)(2,1)} %pad_maximum_fusion), calls=%async_computation.2 | async-start | bytes 1310720 | tf_op jit(solution)/shard_map/all_to_all | solution.py:405
  151.0 1.6 copy-start.3
  176.5 8.6 %collective-permute-start = (f32[400,1024]{1,0:T(8,128)}, f32[400,1024]{1,0:T(8,128)S(1)}, u32[]{:S(2)}, u32[]{:S(2)}) collective-permute-start(f32[400,1024]{1,0:T(8,128)} %get-tuple-element.22), channel_id=1, source_target_pairs={{0,32},{32,0},{64,96},{96,64},{128,160},{160,128},{192,224},{224,1... | collective-permute-start | bytes 4915208 | tf_op jit(solution)/shard_map/ppermute | solution.py:421
  185.1 1.2 copy-start.2
  225.4 4.4 %collective-permute-start.1 = (f32[2,200,1024]{2,1,0:T(8,128)}, f32[2,200,1024]{2,1,0:T(8,128)S(1)}, u32[]{:S(2)}, u32[]{:S(2)}) collective-permute-start(f32[2,200,1024]{2,1,0:T(8,128)} %get-tuple-element.24), channel_id=1, source_target_pairs={{0,32},{32,0},{64,96},{96,64},{128,160},{160,128},{192,224},{224,1... | collective-permute-start | bytes 4915208 | tf_op jit(solution)/shard_map/ppermute | solution.py:449

commit v2 on v1

v2 whole, which is shorter than its diff:
```python
import functools
import math

import jax
import jax.numpy as jnp
from jax import lax
from jax.experimental import pallas as pl
from jax.experimental.pallas import tpu as pltpu
from jax.sharding import PartitionSpec as P

E_ITERS = 4
PSEUDO = 0.1
PRIOR_VAR = 1.0
LOG_PSEUDO = math.log(PSEUDO)
F32, BF16, I32 = jnp.float32, jnp.bfloat16, jnp.int32
NT = (((1,), (1,)), ((), ()))
TN = (((0,), (0,)), ((), ()))
SMEM = pl.BlockSpec(memory_space=pltpu.SMEM)


def iota(shape, axis):
    return lax.broadcasted_iota(I32, shape, axis)


def mm(a, b):
    return jnp.dot(a, b, preferred_element_type=F32)


def mmg(a, b, dims):
    return lax.dot_general(a, b, dims, preferred_element_type=F32)


def call(kernel, out_shape, *args, specs=None, scratch=()):
    specs = specs or [pl.BlockSpec()] * len(args)
    return pl.pallas_call(kernel, out_shape=out_shape, in_specs=specs, scratch_shapes=scratch)(*args)


def shape(dims, dtype):
    return jax.ShapeDtypeStruct(dims, dtype)


def place_kernel(peers, capacity, shift, per, slice_ref, where_ref, ids_ref, counts_ref, code_ref, doc_ref, count_ref):
    docs, width = ids_ref.shape
    ids = ids_ref[...]
    owner = lax.shift_right_logical(ids, shift)
    word = ids & ((1 << shift) - 1)
    low = (word & 255).astype(F32)
    high = (lax.shift_right_logical(word, 8) + 1).astype(F32)
    counts = counts_ref[...].astype(F32)
    base = (where_ref[0] * 2 + where_ref[1]) * per
    before = (iota((width, width), 0) < iota((width, width), 1)).astype(F32).astype(BF16)
    owners = iota((peers, width), 0)
    ranks = iota((capacity, width), 0).astype(F32)
    hot = [(owners == owner[d : d + 1, :]).astype(F32) for d in range(docs)]
    inside = mm(jnp.concatenate(hot, axis=0).astype(BF16), before)
    start = jnp.zeros((peers, 1), F32)
    left, right = [], []
    for d in range(docs):
        mine = hot[d]
        part = ((slice_ref[d] - base) << (shift - 8)).astype(F32)
        rank = jnp.sum(mine * (inside[d * peers : (d + 1) * peers] + start), axis=0, keepdims=True)
        start = start + jnp.sum(mine, axis=1, keepdims=True)
        right.append((ranks == rank).astype(F32).astype(BF16))
        left.append(
            jnp.concatenate(
                [
                    mine * low[d : d + 1],
                    mine * (high[d : d + 1] + part),
                    mine * float(d),
                    mine * counts[d : d + 1],
                ],
                axis=0,
            ).astype(BF16)
        )
    placed = mmg(jnp.concatenate(left, axis=1), jnp.concatenate(right, axis=1), NT)
    low_p, high_p, doc_p, count_p = (placed[i * peers : (i + 1) * peers] for i in range(4))
    code_ref[...] = doc_p * 8192.0 + high_p * 256.0 + low_p
    doc_ref[...] = jnp.where(high_p > 0.5, doc_p, -1.0)
    count_ref[...] = count_p


HEAD = 128


def at_of(code):
    return (code & 8191) - 256


def word_of(code, shift):
    return at_of(code) & ((1 << shift) - 1)


def part_of(code, shift):
    return lax.shift_right_logical(at_of(code), shift) & 1


def flatten(flat_ref, rows_ref, group):
    capacity = rows_ref.shape[1]
    for s in range(rows_ref.shape[0]):
        g, i = divmod(s, group)
        flat_ref[g : g + 1, i * capacity : (i + 1) * capacity] = rows_ref[s : s + 1, :]


def tiles(count, grid, low, high):
    return [jnp.where(grid == jnp.where(high == float(h), low, -1.0).astype(BF16), 1.0, 0.0).astype(BF16) for h in range(count)]


def columns(source, code, shift):
    rows, words = source.shape[0] // 2, source.shape[1]
    chunk = 256
    grid = iota((256, chunk), 0).astype(F32).astype(BF16)
    out = []
    for c in range(code.shape[1] // chunk):
        mine = code[:, c * chunk : (c + 1) * chunk]
        word = word_of(mine, shift)
        low, high = (word & 255).astype(F32), lax.shift_right_logical(word, 8).astype(F32)
        both = mm(source[...], jnp.concatenate(tiles(words // 256, grid, low, high), axis=0))
        out.append(jnp.where(part_of(mine, shift) == 0, both[:rows], both[rows:]))
    return jnp.concatenate(out, axis=1)


def fetch_kernel(shift, beta_ref, norm_ref, asked_ref, table_ref, out_ref, flat_ref):
    rows, words = beta_ref.shape
    topics = rows // 2
    tail = topics - HEAD
    peers, capacity = asked_ref.shape
    groups = flat_ref.shape[0]
    group = peers // groups
    norm = jnp.transpose(jnp.broadcast_to(norm_ref[...], (8, norm_ref.shape[1])))[:, 0:1]
    step = 40
    for r in range(0, rows, step):
        table_ref[r : r + step, :] = jnp.exp(beta_ref[r : r + step, :] - norm[r : r + step]).astype(BF16)
    flatten(flat_ref, asked_ref, group)
    third = tail // 3
    spare = capacity - HEAD

    def one(g, carry):
        got = columns(table_ref, flat_ref[pl.ds(g, 1), :].astype(I32), shift)
        wide = jnp.transpose(got[:HEAD]).astype(BF16)
        for i in range(group):
            mine = got[HEAD:, i * capacity : (i + 1) * capacity]
            rest = [mine[b * third : (b + 1) * third, HEAD:] for b in range(3)]
            rest.append(jnp.zeros((third, HEAD - 3 * spare), F32))
            out_ref[g * group + i, 0:capacity, :] = wide[i * capacity : (i + 1) * capacity]
            out_ref[g * group + i, capacity : capacity + tail, :] = mine[:, :HEAD].astype(BF16)
            out_ref[g * group + i, capacity + tail :, :] = jnp.concatenate(rest, axis=1).astype(BF16)
        return carry

    lax.fori_loop(0, groups, one, 0)


def hot_kernel(shift, docs, asked_ref, hot_ref, mask_ref, flat_ref):
    peers, capacity = asked_ref.shape
    groups, places = flat_ref.shape
    group = peers // groups
    step = pl.program_id(0)

    @pl.when(step == 0)
    def _():
        flatten(flat_ref, asked_ref, group)

    code = flat_ref[pl.ds(step, 1), :].astype(I32)
    lane = iota((1, places), 1)
    key = jnp.where(code == 0, -1, lax.shift_right_logical(code, 13))
    for s in range(1, group):
        key = key + jnp.where(lane >= s * capacity, jnp.where(code == 0, 0, docs), 0)
    mask_ref[...] = (iota((group * docs, places), 0) == key).astype(F32).astype(BF16)
    word = word_of(code, shift).astype(F32)
    column = jnp.transpose(jnp.broadcast_to(word, (8, places)))[:, 0:1].astype(I32)
    chunk = 256

    def one(j, carry):
        at = pl.ds(pl.multiple_of(j * chunk, chunk), chunk)
        hot_ref[:, at] = (iota((places, chunk), 1) + j * chunk == column).astype(F32).astype(BF16)
        return carry

    lax.fori_loop(0, hot_ref.shape[1] // chunk, one, 0)


def digamma(value):
    correction = jnp.zeros_like(value)
    for j in range(6):
        correction = correction + 1.0 / (value + float(j))
    shifted = value + 6.0
    inverse = 1.0 / shifted
    square = inverse * inverse
    series = square * (1.0 / 12.0 - square * (1.0 / 120.0 - square * (1.0 / 252.0)))
    return jnp.log(shifted) - 0.5 * inverse - series - correction


def split(value):
    high = value.astype(BF16)
    return high, (value - high.astype(F32)).astype(BF16)


def estep_kernel(
    got_ref, doc_rows, count_rows, counts_ref, dirichlet_ref, gamma_ref, out_ref, head_ref, wide_ref, tail_ref, doc_ref, count_ref
):
    docs = counts_ref.shape[0]
    topics = dirichlet_ref.shape[1]
    tail = topics - HEAD
    third = tail // 3
    peers, capacity = doc_rows.shape
    spare = capacity - HEAD
    flatten(doc_ref, doc_rows, peers)
    flatten(count_ref, count_rows, peers)
    for s in range(peers):
        at = s * capacity
        head_ref[at : at + capacity, :] = got_ref[s, :capacity, :]
        wide_ref[:, at : at + HEAD] = got_ref[s, capacity : capacity + tail, :].astype(F32)
        left = got_ref[s, capacity + tail :, :].astype(F32)
        for b in range(3):
            wide_ref[b * third : (b + 1) * third, at + HEAD : at + capacity] = left[:, b * spare : (b + 1) * spare]
    tail_ref[...] = wide_ref[...].astype(BF16)
    dirichlet = dirichlet_ref[...]
    total = jnp.sum(counts_ref[...].astype(F32), axis=1, keepdims=True)
    gamma = dirichlet + total / float(topics)
    doc = doc_ref[...]
    mask = iota((docs, doc.shape[1]), 0) == doc.astype(I32)
    for step in range(E_ITERS):
        theta = jnp.exp(digamma(gamma) - digamma(jnp.sum(gamma, axis=1, keepdims=True)))
        both = jnp.concatenate(split(theta), axis=0)
        norm = mmg(both[:, :HEAD], head_ref[...], NT) + mm(both[:, HEAD:], tail_ref[...])
        norm = norm[:docs] + norm[docs:]
        norm = jnp.sum(jnp.where(mask, norm, 0.0), axis=0, keepdims=True)
        ratio = jnp.where(doc >= 0.0, count_ref[...] / norm, 0.0)
        high, low = split(ratio)
        high, low = high.astype(F32), low.astype(F32)
        spread = jnp.concatenate([jnp.where(mask, high, 0.0), jnp.where(mask, low, 0.0)], axis=0).astype(BF16)
        part = jnp.concatenate([mm(spread, head_ref[...]), mmg(spread, tail_ref[...], NT)], axis=1)
        gamma = dirichlet + theta * (part[:docs] + part[docs:])
    gamma_ref[...] = gamma
    turned = jnp.transpose(jnp.concatenate([theta[:, HEAD:], jnp.zeros((docs, 2 * HEAD - topics), F32)], axis=1))
    turned = [turned[b * third : (b + 1) * third, :] for b in range(3)]
    turned.append(jnp.zeros((third, HEAD - 3 * docs), F32))
    common = jnp.concatenate([theta[:, :HEAD], jnp.concatenate(turned, axis=1)], axis=0).astype(BF16)
    pad = jnp.zeros((1, HEAD - spare), F32)
    blank = jnp.zeros((4, HEAD), F32)
    for s in range(peers):
        at = s * capacity
        rows = []
        for piece in (high, low):
            rows.append(piece[:, at : at + HEAD])
            rows.append(jnp.concatenate([piece[:, at + HEAD : at + capacity], pad], axis=1))
        out_ref[s, 0 : docs + third, :] = common
        out_ref[s, docs + third : docs + third + 8, :] = jnp.concatenate(rows + [blank], axis=0).astype(BF16)


def stats_kernel(
    shift, docs, core_ref, factor_ref, asked_ref, table_ref, hot_ref, mask_ref, keep_ref, send_ref, total_ref, part_ref, ratio_ref
):
    step = pl.program_id(0)
    steps = pl.num_programs(0)
    group, capacity = asked_ref.shape
    rows, words = table_ref.shape
    topics = rows // 2
    tail = topics - HEAD
    third = tail // 3
    spare = capacity - HEAD
    flatten(part_ref, asked_ref, group)
    turned = []
    for s in range(group):
        block = factor_ref[s, docs : docs + third + 8, :].astype(F32)
        turned.append(jnp.concatenate([block[:third, b * docs : (b + 1) * docs] for b in range(3)], axis=0))
        ratio = block[third : third + 2] + block[third + 2 : third + 4]
        ratio_ref[0:1, s * capacity : s * capacity + HEAD] = ratio[0:1]
        ratio_ref[0:1, s * capacity + HEAD : (s + 1) * capacity] = ratio[1:2, :spare]
    mask = mask_ref[...]
    top = factor_ref[:, :docs, :].reshape(group * docs, HEAD)
    bottom = jnp.concatenate(turned, axis=1).astype(BF16)
    factor = jnp.concatenate([mmg(top, mask, TN), mm(bottom, mask)], axis=0) * ratio_ref[...]
    part = part_of(part_ref[...].astype(I32), shift)
    factor = jnp.concatenate([jnp.where(part == 0, factor, 0.0), jnp.where(part == 1, factor, 0.0)], axis=0).astype(BF16)
    chunk = 256
    for j in range(words // chunk):
        new = mm(factor, hot_ref[:, j * chunk : (j + 1) * chunk])

        @pl.when(step == 0)
        def _():
            total_ref[:, j * chunk : (j + 1) * chunk] = new

        @pl.when(step > 0)
        def _():
            total_ref[:, j * chunk : (j + 1) * chunk] += new

    @pl.when(step == steps - 1)
    def _():
        half = words // 2
        first = core_ref[0] == 0
        size = 16

        def finish(i, carry):
            at = pl.ds(pl.multiple_of(i * size, size), size)
            shifted = jnp.log(1.0 + (1.0 / PSEUDO) * (table_ref[at, :].astype(F32) * total_ref[at, :]))
            left, right = shifted[:, :half], shifted[:, half:]
            keep_ref[at, :] = jnp.where(first, left, right)
            send_ref[at, :] = jnp.where(first, right, left)
            return carry

        lax.fori_loop(0, rows // size, finish, 0)


G0, S0, H0, B0, PHI0, QK, KNEXT, PHI, WF0, WQ0, NCOEF = 0, 4, 8, 12, 16, 20, 21, 22, 23, 27, 32


def coef_kernel(chips, chip_ref, drift_ref, obs_ref, out_ref, rows_ref):
    per = 4
    length = chips * per
    drift, obs = drift_ref[...], obs_ref[...]
    one, zero = jnp.ones_like(drift), jnp.zeros_like(drift)
    var = one * PRIOR_VAR
    gain, smooth = [], []
    for t in range(length):
        pred = var + drift
        now = pred / (pred + obs)
        var = (1.0 - now) * pred
        gain.append(now)
        smooth.append(var / (var + drift) if t < length - 1 else zero)
    level, forward = zero, []
    for t in range(length):
        level = (1.0 - gain[t]) * level + gain[t]
        forward.append(level)
    ones_smoothed = [None] * length
    level = zero
    for t in reversed(range(length)):
        level = (1.0 - smooth[t]) * forward[t] + smooth[t] * level
        ones_smoothed[t] = level
    beta, phi, sigma, kappa = [], [], [], []
    for c in range(chips):
        run, back, k = one, one, zero
        for t in range(c * per, (c + 1) * per):
            run = run * (1.0 - gain[t])
            phi.append(run)
            beta.append(back * (1.0 - smooth[t]))
            k = k + beta[t] * run
            back = back * smooth[t]
        sigma.append(back)
        kappa.append(k)
    total = [phi[c * per + per - 1] for c in range(chips)]
    lead = [zero] * (chips + 1)
    for c in reversed(range(chips)):
        lead[c] = kappa[c] + sigma[c] * lead[c + 1] * total[c]
    chip = chip_ref[0]
    for c in range(chips):
        rows = [None] * NCOEF
        for u in range(per):
            t = c * per + u
            rows[G0 + u], rows[S0 + u], rows[H0 + u] = gain[t], smooth[t], ones_smoothed[t] * LOG_PSEUDO
            rows[B0 + u], rows[PHI0 + u] = beta[t], phi[t]
        rows[QK], rows[KNEXT], rows[PHI] = sigma[c] * lead[c + 1], lead[c + 1], total[c]
        for j in range(chips):
            behind, ahead = zero, zero
            if j < c:
                behind = one
                for m in range(j + 1, c):
                    behind = behind * total[m]
            if j > c:
                ahead = one
                for m in range(c + 1, j):
                    ahead = ahead * sigma[m]
            rows[WF0 + j], rows[WQ0 + j] = behind, ahead

        @pl.when(chip == c)
        def _():
            for r in range(NCOEF):
                rows_ref[r : r + 1, : drift.shape[1]] = zero if rows[r] is None else rows[r]

    out_ref[...] = jnp.transpose(rows_ref[...])[: out_ref.shape[0]]


def local_filter(coef, values):
    out, level = [], None
    for u in range(4):
        gain = coef[:, G0 + u : G0 + u + 1]
        level = gain * values[u] if level is None else (1.0 - gain) * level + gain * values[u]
        out.append(level)
    return out


def four(first, keep_ref, recv_ref, topics, at):
    own = [keep_ref[pl.ds(u * topics + at, 8), :] for u in range(2)]
    other = [recv_ref[pl.ds(u * topics + at, 8), :] for u in range(2)]
    return [jnp.where(first, own[u], other[u]) for u in range(2)] + [
        jnp.where(first, other[u], own[u]) for u in range(2)
    ]


def combine_kernel(where_ref, coef_ref, keep_ref, recv_ref, out_ref):
    chips, topics, _ = out_ref.shape
    first, chip = where_ref[1] == 0, where_ref[0]

    def block(i, carry):
        at = pl.multiple_of(i * 8, 8)
        coef = coef_ref[pl.ds(at, 8), :]
        local = local_filter(coef, four(first, keep_ref, recv_ref, topics, at))
        back = coef[:, QK : QK + 1] * local[3]
        for u in range(4):
            back = back + coef[:, B0 + u : B0 + u + 1] * local[u]
        for j in range(chips):
            out_ref[j, pl.ds(at, 8), :] = jnp.where(j > chip, local[3], back).astype(BF16)
        return carry

    lax.fori_loop(0, topics // 8, block, 0)


def edges_kernel(where_ref, coef_ref, keep_ref, recv_ref, far_ref, own_ref, other_ref):
    chips, topics, _ = far_ref.shape
    first = where_ref[1] == 0

    def block(i, carry):
        at = pl.multiple_of(i * 8, 8)
        coef = coef_ref[pl.ds(at, 8), :]

        def take(r):
            return coef[:, r : r + 1]

        local = local_filter(coef, four(first, keep_ref, recv_ref, topics, at))
        entering = jnp.zeros_like(local[0])
        ahead = jnp.zeros_like(local[0])
        for j in range(chips):
            far = far_ref[j, pl.ds(at, 8), :].astype(F32)
            entering = entering + take(WF0 + j) * far
            ahead = ahead + take(WQ0 + j) * far
        after = ahead + take(KNEXT) * (local[3] + take(PHI) * entering)
        middle = after
        for u in (3, 2):
            weight = take(S0 + u)
            middle = (1.0 - weight) * (local[u] + take(PHI0 + u) * entering) + weight * middle
        half = local[1] + take(PHI0 + 1) * entering
        own_ref[0, pl.ds(at, 8), :] = jnp.where(first, entering, half)
        own_ref[1, pl.ds(at, 8), :] = jnp.where(first, middle, after)
        other_ref[0, pl.ds(at, 8), :] = jnp.where(first, half, entering)
        other_ref[1, pl.ds(at, 8), :] = jnp.where(first, after, middle)
        return carry

    lax.fori_loop(0, topics // 8, block, 0)


def means_kernel(where_ref, coef_ref, keep_ref, send_ref, own_ref, other_ref, out_ref):
    _, topics, words = out_ref.shape
    half = words // 2
    first = where_ref[1] == 0

    def block(i, carry):
        at = pl.multiple_of(i * 8, 8)
        coef = coef_ref[pl.ds(at, 8), :]

        def take(r):
            return jnp.where(first, coef[:, r : r + 1], coef[:, r + 2 : r + 3])

        gain, weight, level = ([take(r + u) for u in range(2)] for r in (G0, S0, H0))
        sides = []
        for value_ref, edge_ref in ((keep_ref, own_ref), (send_ref, other_ref)):
            values = [value_ref[pl.ds(u * topics + at, 8), :] for u in range(2)]
            early = (1.0 - gain[0]) * edge_ref[0, pl.ds(at, 8), :] + gain[0] * values[0]
            late = (1.0 - gain[1]) * early + gain[1] * values[1]
            late = (1.0 - weight[1]) * late + weight[1] * edge_ref[1, pl.ds(at, 8), :]
            early = (1.0 - weight[0]) * early + weight[0] * late
            sides.append((early + level[0], late + level[1]))
        for u in range(2):
            out_ref[u, pl.ds(at, 8), :half] = jnp.where(first, sides[0][u], sides[1][u])
            out_ref[u, pl.ds(at, 8), half:] = jnp.where(first, sides[1][u], sides[0][u])
        return carry

    lax.fori_loop(0, topics // 8, block, 0)


def per_device(beta_mean, word_ids, word_counts, doc_slice, dirichlet, drift_var, obs_var):
    slice_dev, vocab_shard, topics = beta_mean.shape
    docs, width = word_ids.shape
    peers = lax.axis_size("doc")
    time_peers = lax.axis_size("tm")
    here = lax.axis_index("tm")
    chip, core = here // 2, here % 2
    chips = time_peers // 2
    shift = vocab_shard.bit_length() - 1
    slots = docs * width
    capacity = slots * 5 // (4 * peers)
    places = peers * capacity
    half = vocab_shard // 2
    rows = slice_dev * topics
    tail = topics - HEAD
    packed = capacity + tail + tail // 3
    groups = 4
    group = peers // groups
    where = jnp.stack([chip, core]).astype(I32)
    vmem = pl.BlockSpec()

    beta = jnp.swapaxes(beta_mean, 1, 2)
    code, doc, count = call(
        functools.partial(place_kernel, peers, capacity, shift, slice_dev),
        [shape((peers, capacity), F32)] * 3,
        doc_slice,
        where,
        word_ids,
        word_counts,
        specs=[SMEM, SMEM, vmem, vmem],
    )
    top = jnp.max(beta, axis=2)
    mass = jnp.sum(jnp.exp(beta - top[:, :, None]), axis=2)
    stats = jnp.concatenate([top.reshape(1, 1, -1), mass.reshape(1, 1, -1)], axis=2)
    outgoing = jnp.concatenate(
        [code.reshape(peers, 1, capacity), jnp.broadcast_to(stats, (peers, 1, stats.shape[2]))], axis=2
    )
    arrived = lax.all_to_all(outgoing, "doc", split_axis=0, concat_axis=0, tiled=True)
    coef = call(
        functools.partial(coef_kernel, chips),
        shape((topics, NCOEF), F32),
        where,
        drift_var.reshape(1, topics),
        obs_var.reshape(1, topics),
        specs=[SMEM, vmem, vmem],
        scratch=[pltpu.VMEM((NCOEF, 2 * HEAD), F32)],
    )
    asked = arrived[:, 0, :capacity]
    tops = arrived[:, 0, capacity : capacity + rows]
    masses = arrived[:, 0, capacity + rows :]
    highest = jnp.max(tops, axis=0)
    log_norm = highest + jnp.log(jnp.sum(masses * jnp.exp(tops - highest), axis=0))
    log_norm = jnp.pad(log_norm, (0, 4 * HEAD - rows)).reshape(1, -1)
    flat = pltpu.VMEM((groups, places // groups), F32)
    table, fetched = call(
        functools.partial(fetch_kernel, shift),
        [shape((rows, vocab_shard), BF16), shape((peers, packed, HEAD), BF16)],
        beta.reshape(rows, vocab_shard),
        log_norm,
        asked,
        scratch=[flat],
    )

    def exchange(value):
        return lax.all_to_all(value, "doc", split_axis=0, concat_axis=0, tiled=True)

    asked_late, fetched = lax.optimization_barrier((asked, fetched))
    got = exchange(fetched)
    hot, mask = pl.pallas_call(
        functools.partial(hot_kernel, shift, docs),
        grid=(groups,),
        out_shape=[shape((places, vocab_shard), BF16), shape((peers * docs, places // groups), BF16)],
        in_specs=[pl.BlockSpec((peers, capacity), lambda g: (0, 0))],
        out_specs=[
            pl.BlockSpec((places // groups, vocab_shard), lambda g: (g, 0)),
            pl.BlockSpec((group * docs, places // groups), lambda g: (g, 0)),
        ],
        scratch_shapes=[flat],
    )(asked_late)
    got, hot, mask = lax.optimization_barrier((got, hot, mask))
    line = pltpu.VMEM((1, places), F32)
    gamma, factors = call(
        estep_kernel,
        [shape((docs, topics), F32), shape((peers, docs + tail // 3 + 8, HEAD), BF16)],
        got,
        doc,
        count,
        word_counts,
        dirichlet.reshape(1, topics),
        scratch=[pltpu.VMEM((places, HEAD), BF16), pltpu.VMEM((tail, places), F32), pltpu.VMEM((tail, places), BF16), line, line],
    )
    factors = exchange(factors)
    line = pltpu.VMEM((1, places // groups), F32)
    keep, send = pl.pallas_call(
        functools.partial(stats_kernel, shift, docs),
        grid=(groups,),
        out_shape=[shape((rows, half), F32)] * 2,
        in_specs=[
            SMEM,
            pl.BlockSpec((group,) + factors.shape[1:], lambda g: (g, 0, 0)),
            pl.BlockSpec((group, capacity), lambda g: (g, 0)),
            pl.BlockSpec((rows, vocab_shard), lambda g: (0, 0)),
            pl.BlockSpec((places // groups, vocab_shard), lambda g: (g, 0)),
            pl.BlockSpec((group * docs, places // groups), lambda g: (g, 0)),
        ],
        out_specs=[pl.BlockSpec((rows, half), lambda g: (0, 0))] * 2,
        scratch_shapes=[pltpu.VMEM((rows, vocab_shard), F32), line, line],
    )(core.astype(I32).reshape(1), factors, asked, table, hot, mask)
    swap = [(i, i ^ 1) for i in range(time_peers)]
    recv = lax.ppermute(send, "tm", swap)
    combined = call(
        combine_kernel,
        shape((chips, topics, half), BF16),
        where,
        coef,
        keep,
        recv,
        specs=[SMEM] + [vmem] * 3,
    )
    far = lax.all_to_all(
        combined,
        "tm",
        split_axis=0,
        concat_axis=0,
        tiled=True,
        axis_index_groups=[[2 * i + c for i in range(chips)] for c in range(2)],
    )
    own, other = call(
        edges_kernel,
        [shape((slice_dev, topics, half), F32)] * 2,
        where,
        coef,
        keep,
        recv,
        far,
        specs=[SMEM] + [vmem] * 4,
    )
    partner = lax.ppermute(other, "tm", swap)
    means = call(
        means_kernel,
        shape((slice_dev, topics, vocab_shard), F32),
        where,
        coef,
        keep,
        send,
        own,
        partner,
        specs=[SMEM] + [vmem] * 5,
    )
    return jnp.swapaxes(means, 1, 2), gamma


def solution(mesh):
    return jax.shard_map(
        per_device,
        mesh=mesh,
        in_specs=(
            P("tm", "doc", None),
            P(("tm", "doc"), None),
            P(("tm", "doc"), None),
            P(("tm", "doc")),
            P(),
            P(),
            P(),
        ),
        out_specs=(P("tm", "doc", None), P(("tm", "doc"), None)),
        check_vma=False,
    )
```

time: 234 us -> 225 us (0.962)
  waiting for transfers between devices: 77.4 us -> 41.4 us
  Pallas kernels: 69.3 us -> 95.2 us
  blocking collectives: 46.5 us -> 66 us
  starting transfers between devices: 17.1 us -> 10 us
  local copies, waits for them, and re-layouts: 12.9 us -> 6.5 us
  other arithmetic: 9.63 us -> 4.08 us
    pallas_call x0 -> x2, Pallas kernels: none -> 43.2 us  [the longest x1 30.1 us: per_device(): pl.pallas_call(functools.partial(stats_kernel, shift, docs), grid=(groups...]
    all_to_all x2 -> x1, waiting for transfers between devices: 74.1 us -> 36.4 us  [exchange(): return lax.all_to_all(value, 'doc', split_axis=0, concat_axis=0, tiled=True)]
    all_to_all x0 -> x1, blocking collectives: none -> 19.9 us  [exchange(): return lax.all_to_all(value, 'doc', split_axis=0, concat_axis=0, tiled=True)]
    pallas_call x7, Pallas kernels: 69.3 us -> 52.1 us  [call(): pl.pallas_call(kernel, out_shape=out_shape, in_specs=specs, scratch_shape...]
    all_to_all x2 -> x1, starting transfers between devices: 11 us -> 4.01 us  [exchange(): return lax.all_to_all(value, 'doc', split_axis=0, concat_axis=0, tiled=True)]
    reshape x6 -> x0, local copies, waits for them, and re-layouts: 3.59 us -> none  [the longest x1 0.71 us: per_device(): count.reshape(1, places)]
    unnamed x14 -> x9, local copies, waits for them, and re-layouts: 3.27 us -> 4.86 us
  transfers between devices with their start and end apart: 4 -> 3, of which waited for: 3 -> 3; matrix products, arithmetic and copies ran while one was open for 2% -> 0% of each run, Pallas kernels for 1% -> 7%
where the time goes in v2:
time: 225 us; the launch traced here: 224 us
  Pallas kernels  95.2 us (42%)
  blocking collectives  66 us (29%)
  waiting for transfers between devices  41.4 us (18%)
  starting transfers between devices  10 us (4%)
  local copies, waits for them, and re-layouts  6.5 us (3%)
  other arithmetic  4.08 us (2%)
    pallas_call x7, Pallas kernels, call(): pl.pallas_call(kernel, out_shape=out_shape, in_specs=specs, scratch_shape...  52.1 us
    all_to_all x1, waiting for transfers between devices, exchange(): return lax.all_to_all(value, 'doc', split_axis=0, concat_axis=0, tiled=True)  36.4 us
    pallas_call x1, Pallas kernels, per_device(): pl.pallas_call(functools.partial(stats_kernel, shift, docs), grid=(groups...  30.1 us
    all_to_all x1, blocking collectives, per_device(): lax.all_to_all(combined, 'tm', split_axis=0, concat_axis=0, tiled=True, a...  25.3 us
    all_to_all x1, blocking collectives, per_device(): lax.all_to_all(outgoing, 'doc', split_axis=0, concat_axis=0, tiled=True)  20.8 us
    all_to_all x1, blocking collectives, exchange(): return lax.all_to_all(value, 'doc', split_axis=0, concat_axis=0, tiled=True)  19.9 us
    pallas_call x1, Pallas kernels, per_device(): pl.pallas_call(functools.partial(hot_kernel, shift, docs), grid=(groups,)...  13 us
    unnamed x9, local copies, waits for them, and re-layouts  4.86 us
  transfers between devices with their start and end apart: 3, of which 3 were waited for; matrix products, arithmetic and copies ran while one was open for 0% of the time, Pallas kernels for 7%

profile of v2, /device:TPU:1, one launch (start us, length us, event | category | flops | bytes accessed | tf_op | source)
XLA Modules:
  0.0 223.9 jit_solution(15914903320985243403)
XLA Ops:
  0.7 2.3 %bitcast_reduce_fusion = f32[2,200]{1,0:T(2,128)S(1)} fusion(f32[2,2048,200]{1,2,0:T(8,128)} %param.7), kind=kLoop, calls=%fused_computation.1 | loop fusion | flops 818800 | bytes 3278400 | tf_op jit(solution)/shard_map/reduce_max | solution.py:499
  3.0 0.6 copy-done
  3.5 0.6 fusion.1
  4.1 0.1 reshape.36
  4.3 0.6 pad_add_fusion.chip_ref.where_ref
  4.9 2.1 shard_map.87
  7.1 0.8 copy.9
  7.9 0.1 maximum_reduce_fusion
  8.0 0.1 pad_maximum_fusion
  8.1 20.8 %all_to_all.20 = f32[32,1,960]{2,1,0:T(1,128)S(1)} all-to-all(f32[32,1,960]{2,1,0:T(1,128)S(1)} %pad_maximum_fusion), channel_id=1, replica_groups=mesh['tm'=8,'doc'=32] {'doc'}, dimensions={0} | all-to-all | bytes 245760 | tf_op jit(solution)/shard_map/all_to_all | solution.py:505
  29.0 0.6 copy.27
  29.6 0.3 fusion.6
  30.0 0.6 pad.4
  30.6 16.2 %shard_map.88 = (bf16[400,2048]{1,0:T(8,128)(2,1)}, bf16[32,256,128]{2,1,0:T(8,128)(2,1)}) custom-call(f32[400,2048]{1,0:T(8,128)} %bitcast.32, f32[1,512]{1,0:T(1,128)} %bitcast.38, f32[32,160]{1,0:T(8,128)} %bitcast.34), custom_call_target="tpu_custom_call" | custom-call | tf_op jit(solution)/shard_map/pallas_call | solution.py:35
  46.8 4.0 %all-to-all-start.1 = ((bf16[32,256,128]{2,1,0:T(8,128)(2,1)}), bf16[32,256,128]{2,1,0:T(8,128)(2,1)S(1)}, u32[]{:S(2)}, u32[]{:S(2)}) async-start(bf16[32,256,128]{2,1,0:T(8,128)(2,1)} %get-tuple-element.22), calls=%async_computation.1 | async-start | bytes 4194304 | tf_op jit(solution)/shard_map/all_to_all | solution.py:532
  50.8 13.0 %shard_map.89 = (bf16[5120,2048]{1,0:T(8,128)(2,1)}, bf16[1024,1280]{1,0:T(8,128)(2,1)}) custom-call(f32[32,160]{1,0:T(8,128)} %bitcast.35), custom_call_target="tpu_custom_call" | custom-call | tf_op jit(solution)/shard_map/pallas_call | solution.py:536
  63.8 36.4 %all-to-all-done.1.got_ref = bf16[32,256,128]{2,1,0:T(8,128)(2,1)S(1)} async-done(((bf16[32,256,128]{2,1,0:T(8,128)(2,1)}), bf16[32,256,128]{2,1,0:T(8,128)(2,1)S(1)}, u32[]{:S(2)}, u32[]{:S(2)}) %all-to-all-start.1) | async-done | bytes 2097184 | tf_op jit(solution)/shard_map/all_to_all | solution.py:532
  100.2 1.3 copy-done.1
  101.5 9.9 %shard_map.90 = (f32[32,200]{1,0:T(8,128)}, bf16[32,64,128]{2,1,0:T(8,128)(2,1)}) custom-call(bf16[32,256,128]{2,1,0:T(8,128)(2,1)} %copy-done.1, f32[32,160]{1,0:T(8,128)} %get-tuple-element.27.doc_rows, f32[32,160]{1,0:T(8,128)} %get-tuple-element.28.count_rows, s32[32,128]{1,0:T(8,128)} %counts_ref.3, f32[1,200]{1,0:T(1,128)} %bitcast.39), custom_call_target="tpu_custom_call" | custom-call | tf_op jit(solution)/shard_map/pallas_call | solution.py:35
  111.4 19.9 %all_to_all.21.factor_ref = bf16[32,64,128]{2,1,0:T(8,128)(2,1)} all-to-all(bf16[32,64,128]{2,1,0:T(8,128)(2,1)} %get-tuple-element.29), channel_id=1, replica_groups=mesh['tm'=8,'doc'=32] {'doc'}, dimensions={0} | all-to-all | bytes 1048576 | tf_op jit(solution)/shard_map/all_to_all | solution.py:532
  131.3 30.1 %shard_map.91 = (f32[400,1024]{1,0:T(8,128)}, f32[400,1024]{1,0:T(8,128)}) custom-call(s32[1]{0:T(128)} %bitcast.1.core_ref, bf16[32,64,128]{2,1,0:T(8,128)(2,1)} %all_to_all.21.factor_ref, f32[32,160]{1,0:T(8,128)} %bitcast.36, bf16[400,2048]{1,0:T(8,128)(2,1)} %get-tuple-element.30.table_ref, bf16[5120,2048]{1,0:T(8,128)(2,1)} %get-tuple-element.31.hot_ref, ...), custom_call_target="tpu_custom_call" | custom-call | tf_op jit(solution)/shard_map/pallas_call | solution.py:561
  161.5 4.5 %collective-permute-start = (f32[400,1024]{1,0:T(8,128)}, f32[400,1024]{1,0:T(8,128)S(1)}, u32[]{:S(2)}, u32[]{:S(2)}) collective-permute-start(f32[400,1024]{1,0:T(8,128)} %get-tuple-element.34.send_ref), channel_id=1, source_target_pairs={{0,32},{32,0},{64,96},{96,64},{128,160},{160,128},{192,224},{224,1... | collective-permute-start | bytes 4915208 | tf_op jit(solution)/shard_map/ppermute | solution.py:577
  166.0 1.7 shard_map.86.coef_ref
  167.6 1.7 collective-permute-done.recv_ref
  169.3 1.2 copy-done.2
  170.5 5.6 %shard_map.92 = bf16[4,200,1024]{2,1,0:T(8,128)(2,1)} custom-call(s32[2]{0:T(128)} %pad_add_fusion.chip_ref.where_ref, f32[200,32]{1,0:T(8,128)} %shard_map.86.coef_ref, f32[400,1024]{1,0:T(8,128)} %get-tuple-element.33.keep_ref, f32[400,1024]{1,0:T(8,128)} %copy-done.2), custom_call_target="tpu_custom_call" | custom-call | tf_op jit(solution)/shard_map/pallas_call | solution.py:35
  176.1 25.3 %all_to_all.22.far_ref = bf16[4,200,1024]{2,1,0:T(8,128)(2,1)} all-to-all(bf16[4,200,1024]{2,1,0:T(8,128)(2,1)} %shard_map.92), channel_id=1, replica_groups={{0,64,128,192},{32,96,160,224},{1,65,129,193},{33,97,161,225},{2,66,130..., dimensions={0} | all-to-all | bytes 3276800 | tf_op jit(solution)/shard_map/all_to_all | solution.py:587
  201.4 7.5 %shard_map.93 = (f32[2,200,1024]{2,1,0:T(8,128)}, f32[2,200,1024]{2,1,0:T(8,128)}) custom-call(s32[2]{0:T(128)} %pad_add_fusion.chip_ref.where_ref, f32[200,32]{1,0:T(8,128)} %shard_map.86.coef_ref, f32[400,1024]{1,0:T(8,128)} %get-tuple-element.33.keep_ref, f32[400,1024]{1,0:T(8,128)} %copy-done.2, bf16[4,200,1024]{2,1,0:T(8,128)(2,1)} %all_to_all.22.far_ref), custom_call_target="tpu_custom_call" | custom-call | tf_op jit(solution)/shard_map/pallas_call | solution.py:35
  208.8 1.5 collective-permute-start.1
  210.3 3.3 %collective-permute-done.1.other_ref = f32[2,200,1024]{2,1,0:T(8,128)S(1)} collective-permute-done((f32[2,200,1024]{2,1,0:T(8,128)}, f32[2,200,1024]{2,1,0:T(8,128)S(1)}, u32[]{:S(2)}, u32[]{:S(2)}) %collective-permute-start.1) | collective-permute-done | bytes 1638432 | tf_op jit(solution)/shard_map/ppermute | solution.py:605
  213.7 1.2 copy-done.3
  214.8 9.1 %shard_map.94 = f32[2,200,2048]{2,1,0:T(8,128)} custom-call(s32[2]{0:T(128)} %pad_add_fusion.chip_ref.where_ref, f32[200,32]{1,0:T(8,128)} %shard_map.86.coef_ref, f32[400,1024]{1,0:T(8,128)} %get-tuple-element.33.keep_ref, f32[400,1024]{1,0:T(8,128)} %get-tuple-element.34.send_ref, f32[2,200,1024]{2,1,0:T(8,128)} %get-tuple-element.35.own_ref, ...), custom_call_target="tpu_custom_call" | custom-call | tf_op jit(solution)/shard_map/pallas_call | solution.py:35
  (9 shorter events, 0.2 us)
Async XLA Ops:
  0.6 2.9 %copy-start = (f32[2,2048,200]{1,2,0:T(8,128)S(1)}, f32[2,2048,200]{1,2,0:T(8,128)}, u32[]{:S(2)}) copy-start(f32[2,2048,200]{1,2,0:T(8,128)} %param.7) | copy-start | bytes 9830404
  46.8 53.4 %all-to-all-start.1 = ((bf16[32,256,128]{2,1,0:T(8,128)(2,1)}), bf16[32,256,128]{2,1,0:T(8,128)(2,1)S(1)}, u32[]{:S(2)}, u32[]{:S(2)}) async-start(bf16[32,256,128]{2,1,0:T(8,128)(2,1)} %get-tuple-element.22), calls=%async_computation.1 | async-start | bytes 4194304 | tf_op jit(solution)/shard_map/all_to_all | solution.py:532
  100.2 1.3 copy-start.1
  161.5 7.8 %collective-permute-start = (f32[400,1024]{1,0:T(8,128)}, f32[400,1024]{1,0:T(8,128)S(1)}, u32[]{:S(2)}, u32[]{:S(2)}) collective-permute-start(f32[400,1024]{1,0:T(8,128)} %get-tuple-element.34.send_ref), channel_id=1, source_target_pairs={{0,32},{32,0},{64,96},{96,64},{128,160},{160,128},{192,224},{224,1... | collective-permute-start | bytes 4915208 | tf_op jit(solution)/shard_map/ppermute | solution.py:577
  169.3 1.2 copy-start.2
  208.8 4.8 %collective-permute-start.1 = (f32[2,200,1024]{2,1,0:T(8,128)}, f32[2,200,1024]{2,1,0:T(8,128)S(1)}, u32[]{:S(2)}, u32[]{:S(2)}) collective-permute-start(f32[2,200,1024]{2,1,0:T(8,128)} %get-tuple-element.36), channel_id=1, source_target_pairs={{0,32},{32,0},{64,96},{96,64},{128,160},{160,128},{192,224},{224,1... | collective-permute-start | bytes 4915208 | tf_op jit(solution)/shard_map/ppermute | solution.py:605
  213.7 1.2 copy-start.3

commit v3 on v2

--- a/solution.py
+++ b/solution.py
@@ -30,13 +30,23 @@
     return lax.dot_general(a, b, dims, preferred_element_type=F32)
 
 
-def call(kernel, out_shape, *args, specs=None, scratch=()):
-    specs = specs or [pl.BlockSpec()] * len(args)
-    return pl.pallas_call(kernel, out_shape=out_shape, in_specs=specs, scratch_shapes=scratch)(*args)
+VMEM = pl.BlockSpec(memory_space=pltpu.VMEM)
 
 
 def shape(dims, dtype):
     return jax.ShapeDtypeStruct(dims, dtype)
+
+
+def call(kernel, outs, *args, scalars=0, scratch=()):
+    args = args[:scalars] + tuple(pltpu.with_memory_space_constraint(a, pltpu.VMEM) for a in args[scalars:])
+    return pl.pallas_call(
+        kernel,
+        out_shape=outs,
+        in_specs=[SMEM] * scalars + [VMEM] * (len(args) - scalars),
+        out_specs=[VMEM if isinstance(o, pl.MemoryRef) else pl.BlockSpec() for o in outs],
+        scratch_shapes=scratch,
+        compiler_params=pltpu.CompilerParams(vmem_limit_bytes=36 << 20),
+    )(*args)
 
 
 def place_kernel(peers, capacity, shift, per, slice_ref, where_ref, ids_ref, counts_ref, code_ref, doc_ref, count_ref):
@@ -149,32 +159,27 @@
     lax.fori_loop(0, groups, one, 0)
 
 
-def hot_kernel(shift, docs, asked_ref, hot_ref, mask_ref, flat_ref):
+def index_kernel(shift, docs, asked_ref, low_ref, block_ref, mask_ref, flat_ref):
     peers, capacity = asked_ref.shape
     groups, places = flat_ref.shape
     group = peers // groups
-    step = pl.program_id(0)
-
-    @pl.when(step == 0)
-    def _():
-        flatten(flat_ref, asked_ref, group)
-
-    code = flat_ref[pl.ds(step, 1), :].astype(I32)
+    flatten(flat_ref, asked_ref, group)
     lane = iota((1, places), 1)
-    key = jnp.where(code == 0, -1, lax.shift_right_logical(code, 13))
-    for s in range(1, group):
-        key = key + jnp.where(lane >= s * capacity, jnp.where(code == 0, 0, docs), 0)
-    mask_ref[...] = (iota((group * docs, places), 0) == key).astype(F32).astype(BF16)
-    word = word_of(code, shift).astype(F32)
-    column = jnp.transpose(jnp.broadcast_to(word, (8, places)))[:, 0:1].astype(I32)
-    chunk = 256
-
-    def one(j, carry):
-        at = pl.ds(pl.multiple_of(j * chunk, chunk), chunk)
-        hot_ref[:, at] = (iota((places, chunk), 1) + j * chunk == column).astype(F32).astype(BF16)
-        return carry
-
-    lax.fori_loop(0, hot_ref.shape[1] // chunk, one, 0)
+    chunk = low_ref.shape[1]
+    grid = iota((places, chunk), 1).astype(F32).astype(BF16)
+    for g in range(groups):
+        code = flat_ref[g : g + 1, :].astype(I32)
+        key = jnp.where(code == 0, -1, lax.shift_right_logical(code, 13))
+        for s in range(1, group):
+            key = key + jnp.where(lane >= s * capacity, jnp.where(code == 0, 0, docs), 0)
+        mask_ref[g * group * docs : (g + 1) * group * docs, :] = (
+            (iota((group * docs, places), 0) == key).astype(F32).astype(BF16)
+        )
+        at = at_of(code) & ((2 << shift) - 1)
+        low = (at & (chunk - 1)).astype(F32)
+        block_ref[:, g * places : (g + 1) * places] = lax.shift_right_logical(at, chunk.bit_length() - 1).astype(F32)
+        column = jnp.transpose(jnp.broadcast_to(low, (8, places)))[:, 0:1].astype(BF16)
+        low_ref[g * places : (g + 1) * places, :] = jnp.where(grid == column, 1.0, 0.0).astype(BF16)
 
 
 def digamma(value):
@@ -246,58 +251,56 @@
         out_ref[s, docs + third : docs + third + 8, :] = jnp.concatenate(rows + [blank], axis=0).astype(BF16)
 
 
-def stats_kernel(
-    shift, docs, core_ref, factor_ref, asked_ref, table_ref, hot_ref, mask_ref, keep_ref, send_ref, total_ref, part_ref, ratio_ref
+def factor_of(docs, capacity, factor_in, mask_ref, ratio_ref, out_ref):
+    peers = factor_in.shape[0]
+    topics, places = out_ref.shape[0], mask_ref.shape[1]
+    group = places // capacity
+    third = (topics - HEAD) // 3
+    spare = capacity - HEAD
+    for g in range(peers // group):
+        turned = []
+        for i in range(group):
+            block = factor_in[g * group + i, docs : docs + third + 8, :].astype(F32)
+            turned.append(jnp.concatenate([block[:third, b * docs : (b + 1) * docs] for b in range(3)], axis=0))
+            ratio = block[third : third + 2] + block[third + 2 : third + 4]
+            ratio_ref[0:1, i * capacity : i * capacity + HEAD] = ratio[0:1]
+            ratio_ref[0:1, i * capacity + HEAD : (i + 1) * capacity] = ratio[1:2, :spare]
+        mask = mask_ref[g * group * docs : (g + 1) * group * docs, :]
+        top = factor_in[g * group : (g + 1) * group, :docs, :].reshape(group * docs, HEAD)
+        bottom = jnp.concatenate(turned, axis=1).astype(BF16)
+        at = slice(g * places, (g + 1) * places)
+        ratio = ratio_ref[...]
+        out_ref[:HEAD, at] = (mmg(top, mask, TN) * ratio).astype(BF16)
+        out_ref[HEAD:, at] = (mm(bottom, mask) * ratio).astype(BF16)
+
+
+def half_stats(half, factor_ref, low_ref, block_ref, table_ref, out_ref):
+    topics = factor_ref.shape[0]
+    parts = table_ref.shape[0] // topics
+    chunk = low_ref.shape[1]
+    blocks = table_ref.shape[1] // chunk
+    block = block_ref[...]
+    for t in range(parts):
+        for q in range(blocks // 2):
+            h = half * (blocks // 2) + q
+            here = jnp.where(block == (t * blocks + h).astype(F32), 1.0, 0.0).astype(BF16)
+            total = mm(factor_ref[...] * here, low_ref[...])
+            words = pl.ds(pl.multiple_of(h * chunk, chunk), chunk)
+            table = table_ref[t * topics : (t + 1) * topics, words].astype(F32)
+            out_ref[t * topics : (t + 1) * topics, q * chunk : (q + 1) * chunk] = jnp.log(
+                1.0 + (1.0 / PSEUDO) * (table * total)
+            )
+
+
+def send_kernel(
+    docs, capacity, where_ref, factor_in, mask_ref, low_ref, block_ref, table_ref, out_ref, factor_ref, ratio_ref
 ):
-    step = pl.program_id(0)
-    steps = pl.num_programs(0)
-    group, capacity = asked_ref.shape
-    rows, words = table_ref.shape
-    topics = rows // 2
-    tail = topics - HEAD
-    third = tail // 3
-    spare = capacity - HEAD
-    flatten(part_ref, asked_ref, group)
-    turned = []
-    for s in range(group):
-        block = factor_ref[s, docs : docs + third + 8, :].astype(F32)
-        turned.append(jnp.concatenate([block[:third, b * docs : (b + 1) * docs] for b in range(3)], axis=0))
-        ratio = block[third : third + 2] + block[third + 2 : third + 4]
-        ratio_ref[0:1, s * capacity : s * capacity + HEAD] = ratio[0:1]
-        ratio_ref[0:1, s * capacity + HEAD : (s + 1) * capacity] = ratio[1:2, :spare]
-    mask = mask_ref[...]
-    top = factor_ref[:, :docs, :].reshape(group * docs, HEAD)
-    bottom = jnp.concatenate(turned, axis=1).astype(BF16)
-    factor = jnp.concatenate([mmg(top, mask, TN), mm(bottom, mask)], axis=0) * ratio_ref[...]
-    part = part_of(part_ref[...].astype(I32), shift)
-    factor = jnp.concatenate([jnp.where(part == 0, factor, 0.0), jnp.where(part == 1, factor, 0.0)], axis=0).astype(BF16)
-    chunk = 256
-    for j in range(words // chunk):
-        new = mm(factor, hot_ref[:, j * chunk : (j + 1) * chunk])
-
-        @pl.when(step == 0)
-        def _():
-            total_ref[:, j * chunk : (j + 1) * chunk] = new
-
-        @pl.when(step > 0)
-        def _():
-            total_ref[:, j * chunk : (j + 1) * chunk] += new
-
-    @pl.when(step == steps - 1)
-    def _():
-        half = words // 2
-        first = core_ref[0] == 0
-        size = 16
-
-        def finish(i, carry):
-            at = pl.ds(pl.multiple_of(i * size, size), size)
-            shifted = jnp.log(1.0 + (1.0 / PSEUDO) * (table_ref[at, :].astype(F32) * total_ref[at, :]))
-            left, right = shifted[:, :half], shifted[:, half:]
-            keep_ref[at, :] = jnp.where(first, left, right)
-            send_ref[at, :] = jnp.where(first, right, left)
-            return carry
-
-        lax.fori_loop(0, rows // size, finish, 0)
+    factor_of(docs, capacity, factor_in, mask_ref, ratio_ref, factor_ref)
+    half_stats(1 - where_ref[1], factor_ref, low_ref, block_ref, table_ref, out_ref)
+
+
+def keep_kernel(where_ref, factor_ref, low_ref, block_ref, table_ref, out_ref):
+    half_stats(where_ref[1], factor_ref, low_ref, block_ref, table_ref, out_ref)
 
 
 G0, S0, H0, B0, PHI0, QK, KNEXT, PHI, WF0, WQ0, NCOEF = 0, 4, 8, 12, 16, 20, 21, 22, 23, 27, 32
@@ -400,7 +403,7 @@
             out_ref[j, pl.ds(at, 8), :] = jnp.where(j > chip, local[3], back).astype(BF16)
         return carry
 
-    lax.fori_loop(0, topics // 8, block, 0)
+    lax.fori_loop(0, topics // 8, block, 0, unroll=5)
 
 
 def edges_kernel(where_ref, coef_ref, keep_ref, recv_ref, far_ref, own_ref, other_ref):
@@ -433,7 +436,7 @@
         other_ref[1, pl.ds(at, 8), :] = jnp.where(first, after, middle)
         return carry
 
-    lax.fori_loop(0, topics // 8, block, 0)
+    lax.fori_loop(0, topics // 8, block, 0, unroll=5)
 
 
 def means_kernel(where_ref, coef_ref, keep_ref, send_ref, own_ref, other_ref, out_ref):
@@ -462,7 +465,7 @@
             out_ref[u, pl.ds(at, 8), half:] = jnp.where(first, sides[1][u], sides[0][u])
         return carry
 
-    lax.fori_loop(0, topics // 8, block, 0)
+    lax.fori_loop(0, topics // 8, block, 0, unroll=5)
 
 
 def per_device(beta_mean, word_ids, word_counts, doc_slice, dirichlet, drift_var, obs_var):
@@ -484,17 +487,19 @@
     groups = 4
     group = peers // groups
     where = jnp.stack([chip, core]).astype(I32)
-    vmem = pl.BlockSpec()
+
+    def local(*dims, dtype=F32):
+        return pltpu.VMEM(dims, dtype)
 
     beta = jnp.swapaxes(beta_mean, 1, 2)
     code, doc, count = call(
         functools.partial(place_kernel, peers, capacity, shift, slice_dev),
-        [shape((peers, capacity), F32)] * 3,
+        [local(peers, capacity)] * 3,
         doc_slice,
         where,
         word_ids,
         word_counts,
-        specs=[SMEM, SMEM, vmem, vmem],
+        scalars=2,
     )
     top = jnp.max(beta, axis=2)
     mass = jnp.sum(jnp.exp(beta - top[:, :, None]), axis=2)
@@ -502,15 +507,19 @@
     outgoing = jnp.concatenate(
         [code.reshape(peers, 1, capacity), jnp.broadcast_to(stats, (peers, 1, stats.shape[2]))], axis=2
     )
-    arrived = lax.all_to_all(outgoing, "doc", split_axis=0, concat_axis=0, tiled=True)
-    coef = call(
+
+    def exchange(value):
+        return lax.all_to_all(value, "doc", split_axis=0, concat_axis=0, tiled=True)
+
+    arrived = exchange(outgoing)
+    (coef,) = call(
         functools.partial(coef_kernel, chips),
-        shape((topics, NCOEF), F32),
+        [local(topics, NCOEF)],
         where,
         drift_var.reshape(1, topics),
         obs_var.reshape(1, topics),
-        specs=[SMEM, vmem, vmem],
-        scratch=[pltpu.VMEM((NCOEF, 2 * HEAD), F32)],
+        scalars=1,
+        scratch=[local(NCOEF, 2 * HEAD)],
     )
     asked = arrived[:, 0, :capacity]
     tops = arrived[:, 0, capacity : capacity + rows]
@@ -518,34 +527,28 @@
     highest = jnp.max(tops, axis=0)
     log_norm = highest + jnp.log(jnp.sum(masses * jnp.exp(tops - highest), axis=0))
     log_norm = jnp.pad(log_norm, (0, 4 * HEAD - rows)).reshape(1, -1)
-    flat = pltpu.VMEM((groups, places // groups), F32)
+    flat = local(groups, places // groups)
     table, fetched = call(
         functools.partial(fetch_kernel, shift),
-        [shape((rows, vocab_shard), BF16), shape((peers, packed, HEAD), BF16)],
+        [local(rows, vocab_shard, dtype=BF16), shape((peers, packed, HEAD), BF16)],
         beta.reshape(rows, vocab_shard),
         log_norm,
         asked,
         scratch=[flat],
     )
-
-    def exchange(value):
-        return lax.all_to_all(value, "doc", split_axis=0, concat_axis=0, tiled=True)
-
     asked_late, fetched = lax.optimization_barrier((asked, fetched))
     got = exchange(fetched)
-    hot, mask = pl.pallas_call(
-        functools.partial(hot_kernel, shift, docs),
-        grid=(groups,),
-        out_shape=[shape((places, vocab_shard), BF16), shape((peers * docs, places // groups), BF16)],
-        in_specs=[pl.BlockSpec((peers, capacity), lambda g: (0, 0))],
-        out_specs=[
-            pl.BlockSpec((places // groups, vocab_shard), lambda g: (g, 0)),
-            pl.BlockSpec((group * docs, places // groups), lambda g: (g, 0)),
+    low, block, mask = call(
+        functools.partial(index_kernel, shift, docs),
+        [
+            local(places, 2 * HEAD, dtype=BF16),
+            local(1, places),
+            local(peers * docs, places // groups, dtype=BF16),
         ],
-        scratch_shapes=[flat],
-    )(asked_late)
-    got, hot, mask = lax.optimization_barrier((got, hot, mask))
-    line = pltpu.VMEM((1, places), F32)
+        asked_late,
+        scratch=[flat],
+    )
+    got, low, block, mask = lax.optimization_barrier((got, low, block, mask))
     gamma, factors = call(
         estep_kernel,
         [shape((docs, topics), F32), shape((peers, docs + tail // 3 + 8, HEAD), BF16)],
@@ -554,35 +557,32 @@
         count,
         word_counts,
         dirichlet.reshape(1, topics),
-        scratch=[pltpu.VMEM((places, HEAD), BF16), pltpu.VMEM((tail, places), F32), pltpu.VMEM((tail, places), BF16), line, line],
+        scratch=[
+            local(places, HEAD, dtype=BF16),
+            local(tail, places),
+            local(tail, places, dtype=BF16),
+            local(1, places),
+            local(1, places),
+        ],
     )
     factors = exchange(factors)
-    line = pltpu.VMEM((1, places // groups), F32)
-    keep, send = pl.pallas_call(
-        functools.partial(stats_kernel, shift, docs),
-        grid=(groups,),
-        out_shape=[shape((rows, half), F32)] * 2,
-        in_specs=[
-            SMEM,
-            pl.BlockSpec((group,) + factors.shape[1:], lambda g: (g, 0, 0)),
-            pl.BlockSpec((group, capacity), lambda g: (g, 0)),
-            pl.BlockSpec((rows, vocab_shard), lambda g: (0, 0)),
-            pl.BlockSpec((places // groups, vocab_shard), lambda g: (g, 0)),
-            pl.BlockSpec((group * docs, places // groups), lambda g: (g, 0)),
-        ],
-        out_specs=[pl.BlockSpec((rows, half), lambda g: (0, 0))] * 2,
-        scratch_shapes=[pltpu.VMEM((rows, vocab_shard), F32), line, line],
-    )(core.astype(I32).reshape(1), factors, asked, table, hot, mask)
+    send, factor = call(
+        functools.partial(send_kernel, docs, capacity),
+        [local(rows, half), local(topics, places, dtype=BF16)],
+        where,
+        factors,
+        mask,
+        low,
+        block,
+        table,
+        scalars=1,
+        scratch=[local(1, places // groups)],
+    )
     swap = [(i, i ^ 1) for i in range(time_peers)]
     recv = lax.ppermute(send, "tm", swap)
-    combined = call(
-        combine_kernel,
-        shape((chips, topics, half), BF16),
-        where,
-        coef,
-        keep,
-        recv,
-        specs=[SMEM] + [vmem] * 3,
+    (keep,) = call(keep_kernel, [local(rows, half)], where, factor, low, block, table, scalars=1)
+    (combined,) = call(
+        combine_kernel, [shape((chips, topics, half), BF16)], where, coef, keep, recv, scalars=1
     )
     far = lax.all_to_all(
         combined,
@@ -593,26 +593,19 @@
         axis_index_groups=[[2 * i + c for i in range(chips)] for c in range(2)],
     )
     own, other = call(
-        edges_kernel,
-        [shape((slice_dev, topics, half), F32)] * 2,
-        where,
-        coef,
-        keep,
-        recv,
-        far,
-        specs=[SMEM] + [vmem] * 4,
+        edges_kernel, [local(slice_dev, topics, half)] * 2, where, coef, keep, recv, far, scalars=1
     )
     partner = lax.ppermute(other, "tm", swap)
-    means = call(
+    (means,) = call(
         means_kernel,
-        shape((slice_dev, topics, vocab_shard), F32),
+        [shape((slice_dev, topics, vocab_shard), F32)],
         where,
         coef,
         keep,
         send,
         own,
         partner,
-        specs=[SMEM] + [vmem] * 5,
+        scalars=1,
     )
     return jnp.swapaxes(means, 1, 2), gamma
 

time: 225 us -> 183 us (0.81)
  Pallas kernels: 95.2 us -> 47.4 us
  waiting for transfers between devices: 41.4 us -> 48.3 us
    pallas_call x9 -> x10, Pallas kernels: 95.2 us -> 47.4 us  [call(): pl.pallas_call(kernel, out_shape=outs, in_specs=[SMEM] * scalars + [VMEM]...]
    all_to_all x1 -> x0, blocking collectives: 20.8 us -> none  [per_device(): lax.all_to_all(outgoing, 'doc', split_axis=0, concat_axis=0, tiled=True)]
    all_to_all x1 -> x2, blocking collectives: 19.9 us -> 40.4 us  [exchange(): return lax.all_to_all(value, 'doc', split_axis=0, concat_axis=0, tiled=True)]
    all_to_all x1, waiting for transfers between devices: 36.4 us -> 45.1 us  [exchange(): return lax.all_to_all(value, 'doc', split_axis=0, concat_axis=0, tiled=True)]
    unnamed x9 -> x25, local copies, waits for them, and re-layouts: 4.86 us -> 6.32 us
  transfers between devices with their start and end apart: 3 -> 3, of which waited for: 3 -> 2; matrix products, arithmetic and copies ran while one was open for 0% -> 0% of each run, Pallas kernels for 7% -> 5%
where the time goes in v3:
time: 183 us
  blocking collectives  65.4 us (36%)
  waiting for transfers between devices  48.3 us (26%)
  Pallas kernels  47.4 us (26%)
  starting transfers between devices  11.2 us (6%)
  local copies, waits for them, and re-layouts  6.62 us (4%)
  other arithmetic  3.51 us (2%)
    pallas_call x10, Pallas kernels, call(): pl.pallas_call(kernel, out_shape=outs, in_specs=[SMEM] * scalars + [VMEM]...  47.4 us
    all_to_all x1, waiting for transfers between devices, exchange(): return lax.all_to_all(value, 'doc', split_axis=0, concat_axis=0, tiled=True)  45.1 us
    all_to_all x2, blocking collectives, exchange(): return lax.all_to_all(value, 'doc', split_axis=0, concat_axis=0, tiled=True)  40.4 us
    all_to_all x1, blocking collectives, per_device(): lax.all_to_all(combined, 'tm', split_axis=0, concat_axis=0, tiled=True, a...  24.9 us
    unnamed x25, local copies, waits for them, and re-layouts  6.32 us
    all_to_all x1, starting transfers between devices, exchange(): return lax.all_to_all(value, 'doc', split_axis=0, concat_axis=0, tiled=True)  5.09 us
    ppermute x1, starting transfers between devices, per_device(): recv = lax.ppermute(send, 'tm', swap)  4.61 us
  transfers between devices with their start and end apart: 3, of which 2 were waited for; matrix products, arithmetic and copies ran while one was open for 0% of the time, Pallas kernels for 5%

profile of v3, /device:TPU:1, one launch (start us, length us, event | category | flops | bytes accessed | tf_op | source)
XLA Modules:
  0.0 183.2 jit_solution(8668282064598501809)
XLA Ops:
  0.7 2.3 %bitcast_reduce_fusion = f32[2,200]{1,0:T(2,128)S(1)} fusion(f32[2,2048,200]{1,2,0:T(8,128)} %param.7), kind=kLoop, calls=%fused_computation.1 | loop fusion | flops 818800 | bytes 3278400 | tf_op jit(solution)/shard_map/reduce_max | solution.py:504
  3.0 0.6 copy-done
  3.5 0.6 fusion.1
  4.1 0.1 reshape.35
  4.2 0.1 reshape.36
  4.3 0.1 pad_add_fusion.chip_ref.where_ref
  4.4 1.3 shard_map.87
  5.8 0.1 maximum_reduce_fusion
  5.9 0.1 pad.6.clone
  5.9 0.1 pad_maximum_fusion
  6.0 20.8 %all_to_all.20 = f32[32,1,960]{2,1,0:T(1,128)S(1)} all-to-all(f32[32,1,960]{2,1,0:T(1,128)S(1)} %pad_maximum_fusion), channel_id=1, replica_groups=mesh['tm'=8,'doc'=32] {'doc'}, dimensions={0} | all-to-all | bytes 245760 | tf_op jit(solution)/shard_map/all_to_all | solution.py:512
  26.9 0.3 fusion.6
  27.3 13.0 %shard_map.88 = (bf16[400,2048]{1,0:T(8,128)(2,1)S(1)}, bf16[32,256,128]{2,1,0:T(8,128)(2,1)S(1)}) custom-call(f32[400,2048]{1,0:T(8,128)S(1)} %bitcast.32, f32[1,512]{1,0:T(1,128)S(1)} %bitcast.36, f32[32,160]{1,0:T(8,128)S(1)} %bitcast.33), custom_call_target="tpu_custom_call" | custom-call | tf_op jit(solution)/shard_map/pallas_call | solution.py:42
  40.2 1.2 copy-done.1
  41.4 1.3 copy-done.5
  42.7 5.1 %all-to-all-start.1 = ((bf16[32,256,128]{2,1,0:T(8,128)(2,1)}), bf16[32,256,128]{2,1,0:T(8,128)(2,1)}, u32[]{:S(2)}, u32[]{:S(2)}) async-start(bf16[32,256,128]{2,1,0:T(8,128)(2,1)} %copy-done.5), calls=%async_computation.1 | async-start | bytes 4194304 | tf_op jit(solution)/shard_map/all_to_all | solution.py:512
  47.8 2.5 %shard_map.89 = (bf16[5120,256]{1,0:T(8,128)(2,1)S(1)}, f32[1,5120]{1,0:T(1,128)S(1)}, bf16[1024,1280]{1,0:T(8,128)(2,1)S(1)}) custom-call(f32[32,160]{1,0:T(8,128)S(1)} %bitcast.34), custom_call_target="tpu_custom_call" | custom-call | tf_op jit(solution)/shard_map/pallas_call | solution.py:42
  50.4 1.5 copy-done.3
  51.9 45.1 %all-to-all-done.1.got_ref = bf16[32,256,128]{2,1,0:T(8,128)(2,1)} async-done(((bf16[32,256,128]{2,1,0:T(8,128)(2,1)}), bf16[32,256,128]{2,1,0:T(8,128)(2,1)}, u32[]{:S(2)}, u32[]{:S(2)}) %all-to-all-start.1) | async-done | bytes 2097184 | tf_op jit(solution)/shard_map/all_to_all | solution.py:512
  97.0 10.0 %shard_map.90 = (f32[32,200]{1,0:T(8,128)}, bf16[32,64,128]{2,1,0:T(8,128)(2,1)S(1)}) custom-call(bf16[32,256,128]{2,1,0:T(8,128)(2,1)} %all-to-all-done.1.got_ref, f32[32,160]{1,0:T(8,128)S(1)} %get-tuple-element.30.doc_rows, f32[32,160]{1,0:T(8,128)S(1)} %get-tuple-element.31.count_rows, s32[32,128]{1,0:T(8,128)S(1)} %copy-done.6, f32[1,200]{1,0:T(1,128)S(1)} %bitcast.37), custom_call_target="tpu_custom_call" | custom-call | tf_op jit(solution)/shard_map/pallas_call | solution.py:42
  107.0 19.6 %all_to_all.21.factor_in = bf16[32,64,128]{2,1,0:T(8,128)(2,1)S(1)} all-to-all(bf16[32,64,128]{2,1,0:T(8,128)(2,1)S(1)} %get-tuple-element.32), channel_id=1, replica_groups=mesh['tm'=8,'doc'=32] {'doc'}, dimensions={0} | all-to-all | bytes 1048576 | tf_op jit(solution)/shard_map/all_to_all | solution.py:512
  126.6 1.7 copy-done.4
  128.3 6.2 %shard_map.91 = (f32[400,1024]{1,0:T(8,128)S(1)}, bf16[200,5120]{1,0:T(8,128)(2,1)S(1)}) custom-call(s32[2]{0:T(128)S(1)} %pad_add_fusion.chip_ref.where_ref, bf16[32,64,128]{2,1,0:T(8,128)(2,1)S(1)} %all_to_all.21.factor_in, bf16[1024,1280]{1,0:T(8,128)(2,1)S(1)} %copy-done.4, bf16[5120,256]{1,0:T(8,128)(2,1)S(1)} %get-tuple-element.34.low_ref, ...), custom_call_target="tpu_custom_call" | custom-call | tf_op jit(solution)/shard_map/pallas_call | solution.py:42
  134.6 4.6 %collective-permute-start = (f32[400,1024]{1,0:T(8,128)S(1)}, f32[400,1024]{1,0:T(8,128)S(1)}, u32[]{:S(2)}, u32[]{:S(2)}) collective-permute-start(f32[400,1024]{1,0:T(8,128)S(1)} %get-tuple-element.38.send_ref), channel_id=1, source_target_pairs={{0,32},{32,0},{64,96},{96,64},{128,160},{160,128},{192,224},{224,1... | collective-permute-start | bytes 4915208 | tf_op jit(solution)/shard_map/ppermute | solution.py:582
  139.2 0.9 shard_map.86.coef_ref
  140.1 5.2 %shard_map.92.keep_ref = f32[400,1024]{1,0:T(8,128)S(1)} custom-call(s32[2]{0:T(128)S(1)} %pad_add_fusion.chip_ref.where_ref, bf16[200,5120]{1,0:T(8,128)(2,1)S(1)} %get-tuple-element.37.factor_ref, bf16[5120,256]{1,0:T(8,128)(2,1)S(1)} %get-tuple-element.34.low_ref, f32[1,5120]{1,0:T(1,128)S(1)} %get-tuple-element.35.block_ref, bf16[400,2048]{1,0:T(8,128)(2,1)S(1)} %copy-done.2), custom_call_target="tpu_custom_call" | custom-call | tf_op jit(solution)/shard_map/pallas_call | solution.py:42
  145.3 1.7 shard_map.93
  147.1 24.9 %all_to_all.22.far_ref = bf16[4,200,1024]{2,1,0:T(8,128)(2,1)S(1)} all-to-all(bf16[4,200,1024]{2,1,0:T(8,128)(2,1)S(1)} %shard_map.93), channel_id=1, replica_groups={{0,64,128,192},{32,96,160,224},{1,65,129,193},{33,97,161,225},{2,66,130..., dimensions={0} | all-to-all | bytes 3276800 | tf_op jit(solution)/shard_map/all_to_all | solution.py:587
  172.0 2.6 %shard_map.94 = (f32[2,200,1024]{2,1,0:T(8,128)S(1)}, f32[2,200,1024]{2,1,0:T(8,128)S(1)}) custom-call(s32[2]{0:T(128)S(1)} %pad_add_fusion.chip_ref.where_ref, f32[200,32]{1,0:T(8,128)S(1)} %shard_map.86.coef_ref, f32[400,1024]{1,0:T(8,128)S(1)} %shard_map.92.keep_ref, f32[400,1024]{1,0:T(8,128)S(1)} %collective-permute-done.recv_ref, ...), custom_call_target="tpu_custom_call" | custom-call | tf_op jit(solution)/shard_map/pallas_call | solution.py:42
  174.5 1.5 collective-permute-start.1
  176.1 3.1 %collective-permute-done.1.other_ref = f32[2,200,1024]{2,1,0:T(8,128)S(1)} collective-permute-done((f32[2,200,1024]{2,1,0:T(8,128)S(1)}, f32[2,200,1024]{2,1,0:T(8,128)S(1)}, u32[]{:S(2)}, u32[]{:S(2)}) %collective-permute-start.1) | collective-permute-done | bytes 1638432 | tf_op jit(solution)/shard_map/ppermute | solution.py:598
  179.2 4.0 %shard_map.95 = f32[2,200,2048]{2,1,0:T(8,128)} custom-call(s32[2]{0:T(128)S(1)} %pad_add_fusion.chip_ref.where_ref, f32[200,32]{1,0:T(8,128)S(1)} %shard_map.86.coef_ref, f32[400,1024]{1,0:T(8,128)S(1)} %shard_map.92.keep_ref, f32[400,1024]{1,0:T(8,128)S(1)} %get-tuple-element.38.send_ref, f32[2,200,1024]{2,1,0:T(8,128)S(1)} %get-tuple-element.39.own_ref, ...), custom_call_target="tpu_custom_call" | custom-call | tf_op jit(solution)/shard_map/pallas_call | solution.py:42
  (26 shorter events, 0.1 us)
Async XLA Ops:
  0.6 2.9 %copy-start = (f32[2,2048,200]{1,2,0:T(8,128)S(1)}, f32[2,2048,200]{1,2,0:T(8,128)}, u32[]{:S(2)}) copy-start(f32[2,2048,200]{1,2,0:T(8,128)} %param.7) | copy-start | bytes 9830404
  3.5 0.8 copy-start.6
  3.5 0.8 copy-start.7
  3.5 0.8 copy-start.11
  40.2 1.2 copy-start.1
  41.4 1.3 copy-start.5
  42.7 54.3 %copy-start.8 = (f32[200]{0:T(256)S(1)}, f32[200]{0:T(256)}, u32[]{:S(2)}) copy-start(f32[200]{0:T(256)} %param.11) | copy-start | bytes 2404
  42.7 54.3 %all-to-all-start.1 = ((bf16[32,256,128]{2,1,0:T(8,128)(2,1)}), bf16[32,256,128]{2,1,0:T(8,128)(2,1)}, u32[]{:S(2)}, u32[]{:S(2)}) async-start(bf16[32,256,128]{2,1,0:T(8,128)(2,1)} %copy-done.5), calls=%async_computation.1 | async-start | bytes 4194304 | tf_op jit(solution)/shard_map/all_to_all | solution.py:512
  50.4 1.5 copy-start.3
  97.0 29.6 %copy-start.2 = (bf16[400,2048]{1,0:T(8,128)(2,1)S(1)}, bf16[400,2048]{1,0:T(8,128)(2,1)}, u32[]{:S(2)}) copy-start(bf16[400,2048]{1,0:T(8,128)(2,1)} %copy-done.1) | copy-start | bytes 4915204
  126.6 1.7 copy-start.4
  128.3 10.8 %copy-start.9 = (f32[200]{0:T(256)S(1)}, f32[200]{0:T(256)}, u32[]{:S(2)}) copy-start(f32[200]{0:T(256)} %param.12) | copy-start | bytes 2404
  128.3 10.8 %copy-start.10 = (f32[200]{0:T(256)S(1)}, f32[200]{0:T(256)}, u32[]{:S(2)}) copy-start(f32[200]{0:T(256)} %param.13) | copy-start | bytes 2404
  134.6 10.7 %collective-permute-start = (f32[400,1024]{1,0:T(8,128)S(1)}, f32[400,1024]{1,0:T(8,128)S(1)}, u32[]{:S(2)}, u32[]{:S(2)}) collective-permute-start(f32[400,1024]{1,0:T(8,128)S(1)} %get-tuple-element.38.send_ref), channel_id=1, source_target_pairs={{0,32},{32,0},{64,96},{96,64},{128,160},{160,128},{192,224},{224,1... | collective-permute-start | bytes 4915208 | tf_op jit(solution)/shard_map/ppermute | solution.py:582
  174.5 4.7 %collective-permute-start.1 = (f32[2,200,1024]{2,1,0:T(8,128)S(1)}, f32[2,200,1024]{2,1,0:T(8,128)S(1)}, u32[]{:S(2)}, u32[]{:S(2)}) collective-permute-start(f32[2,200,1024]{2,1,0:T(8,128)S(1)} %get-tuple-element.40), channel_id=1, source_target_pairs={{0,32},{32,0},{64,96},{96,64},{128,160},{160,128},{192,224},{224,1... | collective-permute-start | bytes 4915208 | tf_op jit(solution)/shard_map/ppermute | solution.py:598

commit v4 on v3

--- a/solution.py
+++ b/solution.py
@@ -37,13 +37,18 @@
     return jax.ShapeDtypeStruct(dims, dtype)
 
 
-def call(kernel, outs, *args, scalars=0, scratch=()):
-    args = args[:scalars] + tuple(pltpu.with_memory_space_constraint(a, pltpu.VMEM) for a in args[scalars:])
+def call(kernel, outs, *args, scalars=0, far=0, scratch=()):
+    near = len(args) - far
+    args = (
+        args[:scalars]
+        + tuple(pltpu.with_memory_space_constraint(a, pltpu.VMEM) for a in args[scalars:near])
+        + tuple(pltpu.with_memory_space_constraint(a, pltpu.HBM) for a in args[near:])
+    )
     return pl.pallas_call(
         kernel,
         out_shape=outs,
-        in_specs=[SMEM] * scalars + [VMEM] * (len(args) - scalars),
-        out_specs=[VMEM if isinstance(o, pl.MemoryRef) else pl.BlockSpec() for o in outs],
+        in_specs=[SMEM] * scalars + [VMEM] * (near - scalars) + [pl.BlockSpec(memory_space=pltpu.HBM)] * far,
+        out_specs=[VMEM if getattr(o, "memory_space", None) == pltpu.VMEM else pl.BlockSpec() for o in outs],
         scratch_shapes=scratch,
         compiler_params=pltpu.CompilerParams(vmem_limit_bytes=36 << 20),
     )(*args)
@@ -159,7 +164,7 @@
     lax.fori_loop(0, groups, one, 0)
 
 
-def index_kernel(shift, docs, asked_ref, low_ref, block_ref, mask_ref, flat_ref):
+def index_kernel(shift, docs, asked_ref, low_ref, block_ref, key_ref, flat_ref):
     peers, capacity = asked_ref.shape
     groups, places = flat_ref.shape
     group = peers // groups
@@ -172,11 +177,9 @@
         key = jnp.where(code == 0, -1, lax.shift_right_logical(code, 13))
         for s in range(1, group):
             key = key + jnp.where(lane >= s * capacity, jnp.where(code == 0, 0, docs), 0)
-        mask_ref[g * group * docs : (g + 1) * group * docs, :] = (
-            (iota((group * docs, places), 0) == key).astype(F32).astype(BF16)
-        )
         at = at_of(code) & ((2 << shift) - 1)
         low = (at & (chunk - 1)).astype(F32)
+        key_ref[:, g * places : (g + 1) * places] = key.astype(F32)
         block_ref[:, g * places : (g + 1) * places] = lax.shift_right_logical(at, chunk.bit_length() - 1).astype(F32)
         column = jnp.transpose(jnp.broadcast_to(low, (8, places)))[:, 0:1].astype(BF16)
         low_ref[g * places : (g + 1) * places, :] = jnp.where(grid == column, 1.0, 0.0).astype(BF16)
@@ -251,10 +254,11 @@
         out_ref[s, docs + third : docs + third + 8, :] = jnp.concatenate(rows + [blank], axis=0).astype(BF16)
 
 
-def factor_of(docs, capacity, factor_in, mask_ref, ratio_ref, out_ref):
+def factor_of(docs, capacity, factor_in, key_ref, ratio_ref, out_ref):
     peers = factor_in.shape[0]
-    topics, places = out_ref.shape[0], mask_ref.shape[1]
+    topics, places = out_ref.shape[0], ratio_ref.shape[1]
     group = places // capacity
+    grid = iota((group * docs, places), 0).astype(F32).astype(BF16)
     third = (topics - HEAD) // 3
     spare = capacity - HEAD
     for g in range(peers // group):
@@ -265,10 +269,10 @@
             ratio = block[third : third + 2] + block[third + 2 : third + 4]
             ratio_ref[0:1, i * capacity : i * capacity + HEAD] = ratio[0:1]
             ratio_ref[0:1, i * capacity + HEAD : (i + 1) * capacity] = ratio[1:2, :spare]
-        mask = mask_ref[g * group * docs : (g + 1) * group * docs, :]
+        at = slice(g * places, (g + 1) * places)
+        mask = jnp.where(grid == key_ref[:, at].astype(BF16), 1.0, 0.0).astype(BF16)
         top = factor_in[g * group : (g + 1) * group, :docs, :].reshape(group * docs, HEAD)
         bottom = jnp.concatenate(turned, axis=1).astype(BF16)
-        at = slice(g * places, (g + 1) * places)
         ratio = ratio_ref[...]
         out_ref[:HEAD, at] = (mmg(top, mask, TN) * ratio).astype(BF16)
         out_ref[HEAD:, at] = (mm(bottom, mask) * ratio).astype(BF16)
@@ -293,9 +297,24 @@
 
 
 def send_kernel(
-    docs, capacity, where_ref, factor_in, mask_ref, low_ref, block_ref, table_ref, out_ref, factor_ref, ratio_ref
+    docs,
+    capacity,
+    where_ref,
+    factor_in,
+    key_ref,
+    low_ref,
+    block_ref,
+    table_hbm,
+    out_ref,
+    factor_ref,
+    table_ref,
+    ratio_ref,
+    sem,
 ):
-    factor_of(docs, capacity, factor_in, mask_ref, ratio_ref, factor_ref)
+    load = pltpu.make_async_copy(table_hbm, table_ref, sem)
+    load.start()
+    factor_of(docs, capacity, factor_in, key_ref, ratio_ref, factor_ref)
+    load.wait()
     half_stats(1 - where_ref[1], factor_ref, low_ref, block_ref, table_ref, out_ref)
 
 
@@ -432,8 +451,8 @@
         half = local[1] + take(PHI0 + 1) * entering
         own_ref[0, pl.ds(at, 8), :] = jnp.where(first, entering, half)
         own_ref[1, pl.ds(at, 8), :] = jnp.where(first, middle, after)
-        other_ref[0, pl.ds(at, 8), :] = jnp.where(first, half, entering)
-        other_ref[1, pl.ds(at, 8), :] = jnp.where(first, after, middle)
+        other_ref[0, pl.ds(at, 8), :] = jnp.where(first, half, entering).astype(BF16)
+        other_ref[1, pl.ds(at, 8), :] = jnp.where(first, after, middle).astype(BF16)
         return carry
 
     lax.fori_loop(0, topics // 8, block, 0, unroll=5)
@@ -455,9 +474,9 @@
         sides = []
         for value_ref, edge_ref in ((keep_ref, own_ref), (send_ref, other_ref)):
             values = [value_ref[pl.ds(u * topics + at, 8), :] for u in range(2)]
-            early = (1.0 - gain[0]) * edge_ref[0, pl.ds(at, 8), :] + gain[0] * values[0]
+            early = (1.0 - gain[0]) * edge_ref[0, pl.ds(at, 8), :].astype(F32) + gain[0] * values[0]
             late = (1.0 - gain[1]) * early + gain[1] * values[1]
-            late = (1.0 - weight[1]) * late + weight[1] * edge_ref[1, pl.ds(at, 8), :]
+            late = (1.0 - weight[1]) * late + weight[1] * edge_ref[1, pl.ds(at, 8), :].astype(F32)
             early = (1.0 - weight[0]) * early + weight[0] * late
             sides.append((early + level[0], late + level[1]))
         for u in range(2):
@@ -530,25 +549,13 @@
     flat = local(groups, places // groups)
     table, fetched = call(
         functools.partial(fetch_kernel, shift),
-        [local(rows, vocab_shard, dtype=BF16), shape((peers, packed, HEAD), BF16)],
+        [pltpu.HBM((rows, vocab_shard), BF16), pltpu.HBM((peers, packed, HEAD), BF16)],
         beta.reshape(rows, vocab_shard),
         log_norm,
         asked,
         scratch=[flat],
     )
-    asked_late, fetched = lax.optimization_barrier((asked, fetched))
     got = exchange(fetched)
-    low, block, mask = call(
-        functools.partial(index_kernel, shift, docs),
-        [
-            local(places, 2 * HEAD, dtype=BF16),
-            local(1, places),
-            local(peers * docs, places // groups, dtype=BF16),
-        ],
-        asked_late,
-        scratch=[flat],
-    )
-    got, low, block, mask = lax.optimization_barrier((got, low, block, mask))
     gamma, factors = call(
         estep_kernel,
         [shape((docs, topics), F32), shape((peers, docs + tail // 3 + 8, HEAD), BF16)],
@@ -565,18 +572,27 @@
             local(1, places),
         ],
     )
+    asked_late, factors = lax.optimization_barrier((asked, factors))
     factors = exchange(factors)
-    send, factor = call(
+    low, block, key = call(
+        functools.partial(index_kernel, shift, docs),
+        [local(places, 2 * HEAD, dtype=BF16), local(1, places), local(1, places)],
+        asked_late,
+        scratch=[flat],
+    )
+    factors, low, block, key = lax.optimization_barrier((factors, low, block, key))
+    send, factor, table = call(
         functools.partial(send_kernel, docs, capacity),
-        [local(rows, half), local(topics, places, dtype=BF16)],
+        [local(rows, half), local(topics, places, dtype=BF16), local(rows, vocab_shard, dtype=BF16)],
         where,
         factors,
-        mask,
+        key,
         low,
         block,
         table,
         scalars=1,
-        scratch=[local(1, places // groups)],
+        far=1,
+        scratch=[local(1, places // groups), pltpu.SemaphoreType.DMA(())],
     )
     swap = [(i, i ^ 1) for i in range(time_peers)]
     recv = lax.ppermute(send, "tm", swap)
@@ -593,7 +609,14 @@
         axis_index_groups=[[2 * i + c for i in range(chips)] for c in range(2)],
     )
     own, other = call(
-        edges_kernel, [local(slice_dev, topics, half)] * 2, where, coef, keep, recv, far, scalars=1
+        edges_kernel,
+        [local(slice_dev, topics, half), local(slice_dev, topics, half, dtype=BF16)],
+        where,
+        coef,
+        keep,
+        recv,
+        far,
+        scalars=1,
     )
     partner = lax.ppermute(other, "tm", swap)
     (means,) = call(

time: 183 us -> 179 us (0.978)
  waiting for transfers between devices: 48.3 us -> 13.2 us
  blocking collectives: 65.4 us -> 96.8 us
  local copies, waits for them, and re-layouts: 6.62 us -> 0.91 us
  starting transfers between devices: 11.2 us -> 15.1 us
    all_to_all x1, waiting for transfers between devices: 45.1 us -> 11.2 us  [exchange(): return lax.all_to_all(value, 'doc', split_axis=0, concat_axis=0, tiled=True)]
    all_to_all x2, blocking collectives: 40.4 us -> 71.9 us  [exchange(): return lax.all_to_all(value, 'doc', split_axis=0, concat_axis=0, tiled=True)]
    unnamed x25 -> x15, local copies, waits for them, and re-layouts: 6.32 us -> 0.61 us
    all_to_all x1, starting transfers between devices: 5.09 us -> 8.35 us  [exchange(): return lax.all_to_all(value, 'doc', split_axis=0, concat_axis=0, tiled=True)]
  transfers between devices with their start and end apart: 3 -> 3, of which waited for: 2 -> 2; matrix products, arithmetic and copies ran while one was open for 0% -> 0% of each run, Pallas kernels for 5% -> 4%
where the time goes in v4:
time: 179 us
  blocking collectives  96.8 us (54%)
  Pallas kernels  48.6 us (27%)
  starting transfers between devices  15.1 us (8%)
  waiting for transfers between devices  13.2 us (7%)
  other arithmetic  3.51 us (2%)
    all_to_all x2, blocking collectives, exchange(): return lax.all_to_all(value, 'doc', split_axis=0, concat_axis=0, tiled=True)  71.9 us
    pallas_call x10, Pallas kernels, call(): pl.pallas_call(kernel, out_shape=outs, in_specs=[SMEM] * scalars + [VMEM]...  48.6 us
    all_to_all x1, blocking collectives, per_device(): lax.all_to_all(combined, 'tm', split_axis=0, concat_axis=0, tiled=True, a...  24.9 us
    all_to_all x1, waiting for transfers between devices, exchange(): return lax.all_to_all(value, 'doc', split_axis=0, concat_axis=0, tiled=True)  11.2 us
    all_to_all x1, starting transfers between devices, exchange(): return lax.all_to_all(value, 'doc', split_axis=0, concat_axis=0, tiled=True)  8.35 us
    ppermute x1, starting transfers between devices, per_device(): recv = lax.ppermute(send, 'tm', swap)  5.22 us
  transfers between devices with their start and end apart: 3, of which 2 were waited for; matrix products, arithmetic and copies ran while one was open for 0% of the time, Pallas kernels for 4%

profile of v4, /device:TPU:1, one launch (start us, length us, event | category | flops | bytes accessed | tf_op | source)
XLA Modules:
  0.0 178.8 jit_solution(9672810414770298027)
XLA Ops:
  0.6 0.0 copy-start
  0.7 2.3 %bitcast_reduce_fusion = f32[2,200]{1,0:T(2,128)S(1)} fusion(f32[2,2048,200]{1,2,0:T(8,128)} %param.7), kind=kLoop, calls=%fused_computation.1 | loop fusion | flops 818800 | bytes 3278400 | tf_op jit(solution)/shard_map/reduce_max | solution.py:523
  3.0 0.6 copy-done
  3.5 0.6 fusion.1
  4.1 0.1 reshape.35
  4.2 0.1 reshape.36
  4.3 0.1 pad_add_fusion.chip_ref.where_ref
  4.4 1.3 shard_map.87
  5.8 0.1 maximum_reduce_fusion
  5.9 0.1 pad.6.clone
  5.9 0.1 pad_maximum_fusion
  6.0 20.8 %all_to_all.20 = f32[32,1,960]{2,1,0:T(1,128)S(1)} all-to-all(f32[32,1,960]{2,1,0:T(1,128)S(1)} %pad_maximum_fusion), channel_id=1, replica_groups=mesh['tm'=8,'doc'=32] {'doc'}, dimensions={0} | all-to-all | bytes 245760 | tf_op jit(solution)/shard_map/all_to_all | solution.py:531
  26.9 0.3 fusion.6
  27.3 14.2 %shard_map.88 = (bf16[400,2048]{1,0:T(8,128)(2,1)}, bf16[32,256,128]{2,1,0:T(8,128)(2,1)}) custom-call(f32[400,2048]{1,0:T(8,128)S(1)} %bitcast.32, f32[1,512]{1,0:T(1,128)S(1)} %bitcast.36, f32[32,160]{1,0:T(8,128)S(1)} %bitcast.33), custom_call_target="tpu_custom_call" | custom-call | tf_op jit(solution)/shard_map/pallas_call | solution.py:47
  41.5 51.0 %all_to_all.21.got_ref = bf16[32,256,128]{2,1,0:T(8,128)(2,1)S(1)} all-to-all(bf16[32,256,128]{2,1,0:T(8,128)(2,1)} %get-tuple-element.24), channel_id=1, replica_groups=mesh['tm'=8,'doc'=32] {'doc'}, dimensions={0} | all-to-all | bytes 4194304 | tf_op jit(solution)/shard_map/all_to_all | solution.py:531
  92.6 0.0 copy-done.3
  92.6 8.3 %shard_map.89 = (f32[32,200]{1,0:T(8,128)}, bf16[32,64,128]{2,1,0:T(8,128)(2,1)}) custom-call(bf16[32,256,128]{2,1,0:T(8,128)(2,1)S(1)} %all_to_all.21.got_ref, f32[32,160]{1,0:T(8,128)S(1)} %get-tuple-element.25.doc_rows, f32[32,160]{1,0:T(8,128)S(1)} %get-tuple-element.26.count_rows, s32[32,128]{1,0:T(8,128)S(1)} %copy-done.1, f32[1,200]{1,0:T(1,128)S(1)} %bitcast.37), custom_call_target="tpu_custom_call" | custom-call | tf_op jit(solution)/shard_map/pallas_call | solution.py:47
  100.8 8.4 %all-to-all-start.2 = ((bf16[32,64,128]{2,1,0:T(8,128)(2,1)}), bf16[32,64,128]{2,1,0:T(8,128)(2,1)S(1)}, u32[]{:S(2)}, u32[]{:S(2)}) async-start(bf16[32,64,128]{2,1,0:T(8,128)(2,1)} %get-tuple-element.28), calls=%async_computation.2 | async-start | bytes 1048576 | tf_op jit(solution)/shard_map/all_to_all | solution.py:531
  109.2 1.6 shard_map.90
  110.8 11.2 %all-to-all-done.2.factor_in = bf16[32,64,128]{2,1,0:T(8,128)(2,1)S(1)} async-done(((bf16[32,64,128]{2,1,0:T(8,128)(2,1)}), bf16[32,64,128]{2,1,0:T(8,128)(2,1)S(1)}, u32[]{:S(2)}, u32[]{:S(2)}) %all-to-all-start.2) | async-done | bytes 524320 | tf_op jit(solution)/shard_map/all_to_all | solution.py:531
  122.0 8.5 %shard_map.91 = (f32[400,1024]{1,0:T(8,128)S(1)}, bf16[200,5120]{1,0:T(8,128)(2,1)S(1)}, bf16[400,2048]{1,0:T(8,128)(2,1)S(1)}) custom-call(s32[2]{0:T(128)S(1)} %pad_add_fusion.chip_ref.where_ref, bf16[32,64,128]{2,1,0:T(8,128)(2,1)S(1)} %all-to-all-done.2.factor_in, f32[1,5120]{1,0:T(1,128)S(1)} %get-tuple-element.34.key_ref, ...), custom_call_target="tpu_custom_call" | custom-call | tf_op jit(solution)/shard_map/pallas_call | solution.py:47
  130.5 5.2 %collective-permute-start = (f32[400,1024]{1,0:T(8,128)S(1)}, f32[400,1024]{1,0:T(8,128)S(1)}, u32[]{:S(2)}, u32[]{:S(2)}) collective-permute-start(f32[400,1024]{1,0:T(8,128)S(1)} %get-tuple-element.40.send_ref), channel_id=1, source_target_pairs={{0,32},{32,0},{64,96},{96,64},{128,160},{160,128},{192,224},{224,1... | collective-permute-start | bytes 4915208 | tf_op jit(solution)/shard_map/ppermute | solution.py:598
  135.7 0.0 copy-done.4
  135.7 1.1 shard_map.86.coef_ref
  136.8 5.2 %shard_map.92.keep_ref = f32[400,1024]{1,0:T(8,128)S(1)} custom-call(s32[2]{0:T(128)S(1)} %pad_add_fusion.chip_ref.where_ref, bf16[200,5120]{1,0:T(8,128)(2,1)S(1)} %get-tuple-element.38.factor_ref, bf16[5120,256]{1,0:T(8,128)(2,1)S(1)} %get-tuple-element.35.low_ref, f32[1,5120]{1,0:T(1,128)S(1)} %get-tuple-element.36.block_ref, ...), custom_call_target="tpu_custom_call" | custom-call | tf_op jit(solution)/shard_map/pallas_call | solution.py:47
  142.1 0.0 collective-permute-done.recv_ref
  142.1 1.7 shard_map.93
  143.8 24.9 %all_to_all.22.far_ref = bf16[4,200,1024]{2,1,0:T(8,128)(2,1)S(1)} all-to-all(bf16[4,200,1024]{2,1,0:T(8,128)(2,1)S(1)} %shard_map.93), channel_id=1, replica_groups={{0,64,128,192},{32,96,160,224},{1,65,129,193},{33,97,161,225},{2,66,130..., dimensions={0} | all-to-all | bytes 3276800 | tf_op jit(solution)/shard_map/all_to_all | solution.py:603
  168.8 2.6 %shard_map.94 = (f32[2,200,1024]{2,1,0:T(8,128)S(1)}, bf16[2,200,1024]{2,1,0:T(8,128)(2,1)S(1)}) custom-call(s32[2]{0:T(128)S(1)} %pad_add_fusion.chip_ref.where_ref, f32[200,32]{1,0:T(8,128)S(1)} %shard_map.86.coef_ref, f32[400,1024]{1,0:T(8,128)S(1)} %shard_map.92.keep_ref, f32[400,1024]{1,0:T(8,128)S(1)} %collective-permute-done.recv_ref, ...), custom_call_target="tpu_custom_call" | custom-call | tf_op jit(solution)/shard_map/pallas_call | solution.py:47
  171.3 1.5 collective-permute-start.1
  172.8 2.0 %collective-permute-done.1.other_ref = bf16[2,200,1024]{2,1,0:T(8,128)(2,1)S(1)} collective-permute-done((bf16[2,200,1024]{2,1,0:T(8,128)(2,1)S(1)}, bf16[2,200,1024]{2,1,0:T(8,128)(2,1)S(1)}, u32[]{:S(2)}, u32[]{:S(2)}) %collective-permute-start.1) | collective-permute-done | bytes 819232 | tf_op jit(solution)/shard_map/ppermute | solution.py:621
  174.8 4.0 %shard_map.95 = f32[2,200,2048]{2,1,0:T(8,128)} custom-call(s32[2]{0:T(128)S(1)} %pad_add_fusion.chip_ref.where_ref, f32[200,32]{1,0:T(8,128)S(1)} %shard_map.86.coef_ref, f32[400,1024]{1,0:T(8,128)S(1)} %shard_map.92.keep_ref, f32[400,1024]{1,0:T(8,128)S(1)} %get-tuple-element.40.send_ref, f32[2,200,1024]{2,1,0:T(8,128)S(1)} %get-tuple-element.41.own_ref, ...), custom_call_target="tpu_custom_call" | custom-call | tf_op jit(solution)/shard_map/pallas_call | solution.py:47
  (16 shorter events, 0.1 us)
Async XLA Ops:
  0.6 2.9 %copy-start = (f32[2,2048,200]{1,2,0:T(8,128)S(1)}, f32[2,2048,200]{1,2,0:T(8,128)}, u32[]{:S(2)}) copy-start(f32[2,2048,200]{1,2,0:T(8,128)} %param.7) | copy-start | bytes 9830404
  3.5 0.8 copy-start.1
  3.5 0.8 copy-start.2
  3.5 0.8 copy-start.6
  41.5 51.1 %copy-start.3 = (f32[200]{0:T(256)S(1)}, f32[200]{0:T(256)}, u32[]{:S(2)}) copy-start(f32[200]{0:T(256)} %param.11) | copy-start | bytes 2404
  100.8 21.2 %all-to-all-start.2 = ((bf16[32,64,128]{2,1,0:T(8,128)(2,1)}), bf16[32,64,128]{2,1,0:T(8,128)(2,1)S(1)}, u32[]{:S(2)}, u32[]{:S(2)}) async-start(bf16[32,64,128]{2,1,0:T(8,128)(2,1)} %get-tuple-element.28), calls=%async_computation.2 | async-start | bytes 1048576 | tf_op jit(solution)/shard_map/all_to_all | solution.py:531
  122.0 13.7 %copy-start.4 = (f32[200]{0:T(256)S(1)}, f32[200]{0:T(256)}, u32[]{:S(2)}) copy-start(f32[200]{0:T(256)} %param.12) | copy-start | bytes 2404
  122.0 13.7 %copy-start.5 = (f32[200]{0:T(256)S(1)}, f32[200]{0:T(256)}, u32[]{:S(2)}) copy-start(f32[200]{0:T(256)} %param.13) | copy-start | bytes 2404
  130.5 11.6 %collective-permute-start = (f32[400,1024]{1,0:T(8,128)S(1)}, f32[400,1024]{1,0:T(8,128)S(1)}, u32[]{:S(2)}, u32[]{:S(2)}) collective-permute-start(f32[400,1024]{1,0:T(8,128)S(1)} %get-tuple-element.40.send_ref), channel_id=1, source_target_pairs={{0,32},{32,0},{64,96},{96,64},{128,160},{160,128},{192,224},{224,1... | collective-permute-start | bytes 4915208 | tf_op jit(solution)/shard_map/ppermute | solution.py:598
  171.3 3.5 %collective-permute-start.1 = (bf16[2,200,1024]{2,1,0:T(8,128)(2,1)S(1)}, bf16[2,200,1024]{2,1,0:T(8,128)(2,1)S(1)}, u32[]{:S(2)}, u32[]{:S(2)}) collective-permute-start(bf16[2,200,1024]{2,1,0:T(8,128)(2,1)S(1)} %get-tuple-element.42), channel_id=1, source_target_pairs={{0,32},{32,0},{64,96},{96,64},{128,160},{160,128},{192,224},{224,1... | collective-permute-start | bytes 2457608 | tf_op jit(solution)/shard_map/ppermute | solution.py:621

commit v5 on v4

--- a/solution.py
+++ b/solution.py
@@ -20,6 +20,10 @@
 
 def iota(shape, axis):
     return lax.broadcasted_iota(I32, shape, axis)
+
+
+def hot(true):
+    return true.astype(F32).astype(BF16)
 
 
 def mm(a, b):
@@ -117,13 +121,13 @@
 
 
 def tiles(count, grid, low, high):
-    return [jnp.where(grid == jnp.where(high == float(h), low, -1.0).astype(BF16), 1.0, 0.0).astype(BF16) for h in range(count)]
+    return [hot(grid == jnp.where(high == float(h), low, -1.0)) for h in range(count)]
 
 
 def columns(source, code, shift):
     rows, words = source.shape[0] // 2, source.shape[1]
     chunk = 256
-    grid = iota((256, chunk), 0).astype(F32).astype(BF16)
+    grid = iota((256, chunk), 0).astype(F32)
     out = []
     for c in range(code.shape[1] // chunk):
         mine = code[:, c * chunk : (c + 1) * chunk]
@@ -164,25 +168,26 @@
     lax.fori_loop(0, groups, one, 0)
 
 
-def index_kernel(shift, docs, asked_ref, low_ref, block_ref, key_ref, flat_ref):
+def index_kernel(shift, docs, pack, asked_ref, low_ref, block_ref, key_ref, flat_ref):
     peers, capacity = asked_ref.shape
     groups, places = flat_ref.shape
     group = peers // groups
     flatten(flat_ref, asked_ref, group)
     lane = iota((1, places), 1)
     chunk = low_ref.shape[1]
-    grid = iota((places, chunk), 1).astype(F32).astype(BF16)
+    grid = iota((places, chunk), 1).astype(F32)
     for g in range(groups):
         code = flat_ref[g : g + 1, :].astype(I32)
         key = jnp.where(code == 0, -1, lax.shift_right_logical(code, 13))
         for s in range(1, group):
-            key = key + jnp.where(lane >= s * capacity, jnp.where(code == 0, 0, docs), 0)
+            more = docs if s % pack else (1 - pack) * docs
+            key = key + jnp.where(lane >= s * capacity, jnp.where(code == 0, 0, more), 0)
         at = at_of(code) & ((2 << shift) - 1)
         low = (at & (chunk - 1)).astype(F32)
         key_ref[:, g * places : (g + 1) * places] = key.astype(F32)
         block_ref[:, g * places : (g + 1) * places] = lax.shift_right_logical(at, chunk.bit_length() - 1).astype(F32)
-        column = jnp.transpose(jnp.broadcast_to(low, (8, places)))[:, 0:1].astype(BF16)
-        low_ref[g * places : (g + 1) * places, :] = jnp.where(grid == column, 1.0, 0.0).astype(BF16)
+        column = jnp.transpose(jnp.broadcast_to(low, (8, places)))[:, 0:1]
+        low_ref[g * places : (g + 1) * places, :] = hot(grid == column)
 
 
 def digamma(value):
@@ -258,7 +263,7 @@
     peers = factor_in.shape[0]
     topics, places = out_ref.shape[0], ratio_ref.shape[1]
     group = places // capacity
-    grid = iota((group * docs, places), 0).astype(F32).astype(BF16)
+    grid = iota((group * docs, places), 0)
     third = (topics - HEAD) // 3
     spare = capacity - HEAD
     for g in range(peers // group):
@@ -270,7 +275,7 @@
             ratio_ref[0:1, i * capacity : i * capacity + HEAD] = ratio[0:1]
             ratio_ref[0:1, i * capacity + HEAD : (i + 1) * capacity] = ratio[1:2, :spare]
         at = slice(g * places, (g + 1) * places)
-        mask = jnp.where(grid == key_ref[:, at].astype(BF16), 1.0, 0.0).astype(BF16)
+        mask = hot(grid == key_ref[:, at].astype(I32))
         top = factor_in[g * group : (g + 1) * group, :docs, :].reshape(group * docs, HEAD)
         bottom = jnp.concatenate(turned, axis=1).astype(BF16)
         ratio = ratio_ref[...]
@@ -504,7 +509,7 @@
     tail = topics - HEAD
     packed = capacity + tail + tail // 3
     groups = 4
-    group = peers // groups
+    pack = 4
     where = jnp.stack([chip, core]).astype(I32)
 
     def local(*dims, dtype=F32):
@@ -575,7 +580,7 @@
     asked_late, factors = lax.optimization_barrier((asked, factors))
     factors = exchange(factors)
     low, block, key = call(
-        functools.partial(index_kernel, shift, docs),
+        functools.partial(index_kernel, shift, docs, pack),
         [local(places, 2 * HEAD, dtype=BF16), local(1, places), local(1, places)],
         asked_late,
         scratch=[flat],
@@ -592,7 +597,7 @@
         table,
         scalars=1,
         far=1,
-        scratch=[local(1, places // groups), pltpu.SemaphoreType.DMA(())],
+        scratch=[local(1, pack * capacity), pltpu.SemaphoreType.DMA(())],
     )
     swap = [(i, i ^ 1) for i in range(time_peers)]
     recv = lax.ppermute(send, "tm", swap)

time: 179 us -> 174 us (0.972)
  Pallas kernels: 48.6 us -> 43.8 us
    pallas_call x10, Pallas kernels: 48.6 us -> 43.8 us  [call(): pl.pallas_call(kernel, out_shape=outs, in_specs=[SMEM] * scalars + [VMEM]...]
where the time goes in v5:
time: 174 us
  blocking collectives  96.8 us (56%)
  Pallas kernels  43.8 us (25%)
  starting transfers between devices  15.1 us (9%)
  waiting for transfers between devices  13.2 us (8%)
  other arithmetic  3.51 us (2%)
    all_to_all x2, blocking collectives, exchange(): return lax.all_to_all(value, 'doc', split_axis=0, concat_axis=0, tiled=True)  71.9 us
    pallas_call x10, Pallas kernels, call(): pl.pallas_call(kernel, out_shape=outs, in_specs=[SMEM] * scalars + [VMEM]...  43.8 us
    all_to_all x1, blocking collectives, per_device(): lax.all_to_all(combined, 'tm', split_axis=0, concat_axis=0, tiled=True, a...  24.9 us
    all_to_all x1, waiting for transfers between devices, exchange(): return lax.all_to_all(value, 'doc', split_axis=0, concat_axis=0, tiled=True)  11.3 us
    all_to_all x1, starting transfers between devices, exchange(): return lax.all_to_all(value, 'doc', split_axis=0, concat_axis=0, tiled=True)  8.35 us
    ppermute x1, starting transfers between devices, per_device(): recv = lax.ppermute(send, 'tm', swap)  5.22 us
  transfers between devices with their start and end apart: 3, of which 2 were waited for; matrix products, arithmetic and copies ran while one was open for 0% of the time, Pallas kernels for 4%

profile of v5, /device:TPU:1, one launch (start us, length us, event | category | flops | bytes accessed | tf_op | source)
XLA Modules:
  0.0 174.1 jit_solution(14596010325588845158)
XLA Ops:
  0.6 0.0 copy-start
  0.7 2.3 %bitcast_reduce_fusion = f32[2,200]{1,0:T(2,128)S(1)} fusion(f32[2,2048,200]{1,2,0:T(8,128)} %param.7), kind=kLoop, calls=%fused_computation.1 | loop fusion | flops 818800 | bytes 3278400 | tf_op jit(solution)/shard_map/reduce_max | solution.py:528
  3.0 0.6 copy-done
  3.5 0.6 fusion.1
  4.1 0.1 reshape.35
  4.2 0.1 reshape.36
  4.3 0.1 pad_add_fusion.chip_ref.where_ref
  4.4 0.0 copy-done.2
  4.4 1.3 shard_map.87
  5.8 0.1 maximum_reduce_fusion
  5.9 0.1 pad.6.clone
  5.9 0.1 pad_maximum_fusion
  6.0 20.8 %all_to_all.20 = f32[32,1,960]{2,1,0:T(1,128)S(1)} all-to-all(f32[32,1,960]{2,1,0:T(1,128)S(1)} %pad_maximum_fusion), channel_id=1, replica_groups=mesh['tm'=8,'doc'=32] {'doc'}, dimensions={0} | all-to-all | bytes 245760 | tf_op jit(solution)/shard_map/all_to_all | solution.py:536
  26.9 0.3 fusion.6
  27.3 11.6 %shard_map.88 = (bf16[400,2048]{1,0:T(8,128)(2,1)}, bf16[32,256,128]{2,1,0:T(8,128)(2,1)}) custom-call(f32[400,2048]{1,0:T(8,128)S(1)} %bitcast.32, f32[1,512]{1,0:T(1,128)S(1)} %bitcast.36, f32[32,160]{1,0:T(8,128)S(1)} %bitcast.33), custom_call_target="tpu_custom_call" | custom-call | tf_op jit(solution)/shard_map/pallas_call | solution.py:51
  38.8 51.0 %all_to_all.21.got_ref = bf16[32,256,128]{2,1,0:T(8,128)(2,1)S(1)} all-to-all(bf16[32,256,128]{2,1,0:T(8,128)(2,1)} %get-tuple-element.24), channel_id=1, replica_groups=mesh['tm'=8,'doc'=32] {'doc'}, dimensions={0} | all-to-all | bytes 4194304 | tf_op jit(solution)/shard_map/all_to_all | solution.py:536
  89.9 8.3 %shard_map.89 = (f32[32,200]{1,0:T(8,128)}, bf16[32,64,128]{2,1,0:T(8,128)(2,1)}) custom-call(bf16[32,256,128]{2,1,0:T(8,128)(2,1)S(1)} %all_to_all.21.got_ref, f32[32,160]{1,0:T(8,128)S(1)} %get-tuple-element.25.doc_rows, f32[32,160]{1,0:T(8,128)S(1)} %get-tuple-element.26.count_rows, s32[32,128]{1,0:T(8,128)S(1)} %copy-done.1, f32[1,200]{1,0:T(1,128)S(1)} %bitcast.37), custom_call_target="tpu_custom_call" | custom-call | tf_op jit(solution)/shard_map/pallas_call | solution.py:51
  98.2 8.4 %all-to-all-start.2 = ((bf16[32,64,128]{2,1,0:T(8,128)(2,1)}), bf16[32,64,128]{2,1,0:T(8,128)(2,1)S(1)}, u32[]{:S(2)}, u32[]{:S(2)}) async-start(bf16[32,64,128]{2,1,0:T(8,128)(2,1)} %get-tuple-element.28), calls=%async_computation.2 | async-start | bytes 1048576 | tf_op jit(solution)/shard_map/all_to_all | solution.py:536
  106.5 1.6 shard_map.90
  108.1 11.3 %all-to-all-done.2.factor_in = bf16[32,64,128]{2,1,0:T(8,128)(2,1)S(1)} async-done(((bf16[32,64,128]{2,1,0:T(8,128)(2,1)}), bf16[32,64,128]{2,1,0:T(8,128)(2,1)S(1)}, u32[]{:S(2)}, u32[]{:S(2)}) %all-to-all-start.2) | async-done | bytes 524320 | tf_op jit(solution)/shard_map/all_to_all | solution.py:536
  119.4 6.7 %shard_map.91 = (f32[400,1024]{1,0:T(8,128)S(1)}, bf16[200,5120]{1,0:T(8,128)(2,1)S(1)}, bf16[400,2048]{1,0:T(8,128)(2,1)S(1)}) custom-call(s32[2]{0:T(128)S(1)} %pad_add_fusion.chip_ref.where_ref, bf16[32,64,128]{2,1,0:T(8,128)(2,1)S(1)} %all-to-all-done.2.factor_in, f32[1,5120]{1,0:T(1,128)S(1)} %get-tuple-element.34.key_ref, ...), custom_call_target="tpu_custom_call" | custom-call | tf_op jit(solution)/shard_map/pallas_call | solution.py:51
  126.0 5.2 %collective-permute-start = (f32[400,1024]{1,0:T(8,128)S(1)}, f32[400,1024]{1,0:T(8,128)S(1)}, u32[]{:S(2)}, u32[]{:S(2)}) collective-permute-start(f32[400,1024]{1,0:T(8,128)S(1)} %get-tuple-element.40.send_ref), channel_id=1, source_target_pairs={{0,32},{32,0},{64,96},{96,64},{128,160},{160,128},{192,224},{224,1... | collective-permute-start | bytes 4915208 | tf_op jit(solution)/shard_map/ppermute | solution.py:603
  131.3 0.0 copy-done.4
  131.3 0.9 shard_map.86.coef_ref
  132.1 5.2 %shard_map.92.keep_ref = f32[400,1024]{1,0:T(8,128)S(1)} custom-call(s32[2]{0:T(128)S(1)} %pad_add_fusion.chip_ref.where_ref, bf16[200,5120]{1,0:T(8,128)(2,1)S(1)} %get-tuple-element.38.factor_ref, bf16[5120,256]{1,0:T(8,128)(2,1)S(1)} %get-tuple-element.35.low_ref, f32[1,5120]{1,0:T(1,128)S(1)} %get-tuple-element.36.block_ref, ...), custom_call_target="tpu_custom_call" | custom-call | tf_op jit(solution)/shard_map/pallas_call | solution.py:51
  137.4 0.0 collective-permute-done.recv_ref
  137.4 1.7 %shard_map.93 = bf16[4,200,1024]{2,1,0:T(8,128)(2,1)S(1)} custom-call(s32[2]{0:T(128)S(1)} %pad_add_fusion.chip_ref.where_ref, f32[200,32]{1,0:T(8,128)S(1)} %shard_map.86.coef_ref, f32[400,1024]{1,0:T(8,128)S(1)} %shard_map.92.keep_ref, f32[400,1024]{1,0:T(8,128)S(1)} %collective-permute-done.recv_ref), custom_call_target="tpu_custom_call" | custom-call | tf_op jit(solution)/shard_map/pallas_call | solution.py:51
  139.1 24.9 %all_to_all.22.far_ref = bf16[4,200,1024]{2,1,0:T(8,128)(2,1)S(1)} all-to-all(bf16[4,200,1024]{2,1,0:T(8,128)(2,1)S(1)} %shard_map.93), channel_id=1, replica_groups={{0,64,128,192},{32,96,160,224},{1,65,129,193},{33,97,161,225},{2,66,130..., dimensions={0} | all-to-all | bytes 3276800 | tf_op jit(solution)/shard_map/all_to_all | solution.py:608
  164.1 2.6 %shard_map.94 = (f32[2,200,1024]{2,1,0:T(8,128)S(1)}, bf16[2,200,1024]{2,1,0:T(8,128)(2,1)S(1)}) custom-call(s32[2]{0:T(128)S(1)} %pad_add_fusion.chip_ref.where_ref, f32[200,32]{1,0:T(8,128)S(1)} %shard_map.86.coef_ref, f32[400,1024]{1,0:T(8,128)S(1)} %shard_map.92.keep_ref, f32[400,1024]{1,0:T(8,128)S(1)} %collective-permute-done.recv_ref, ...), custom_call_target="tpu_custom_call" | custom-call | tf_op jit(solution)/shard_map/pallas_call | solution.py:51
  166.6 1.5 collective-permute-start.1
  168.1 2.0 %collective-permute-done.1.other_ref = bf16[2,200,1024]{2,1,0:T(8,128)(2,1)S(1)} collective-permute-done((bf16[2,200,1024]{2,1,0:T(8,128)(2,1)S(1)}, bf16[2,200,1024]{2,1,0:T(8,128)(2,1)S(1)}, u32[]{:S(2)}, u32[]{:S(2)}) %collective-permute-start.1) | collective-permute-done | bytes 819232 | tf_op jit(solution)/shard_map/ppermute | solution.py:626
  170.1 4.0 %shard_map.95 = f32[2,200,2048]{2,1,0:T(8,128)} custom-call(s32[2]{0:T(128)S(1)} %pad_add_fusion.chip_ref.where_ref, f32[200,32]{1,0:T(8,128)S(1)} %shard_map.86.coef_ref, f32[400,1024]{1,0:T(8,128)S(1)} %shard_map.92.keep_ref, f32[400,1024]{1,0:T(8,128)S(1)} %get-tuple-element.40.send_ref, f32[2,200,1024]{2,1,0:T(8,128)S(1)} %get-tuple-element.41.own_ref, ...), custom_call_target="tpu_custom_call" | custom-call | tf_op jit(solution)/shard_map/pallas_call | solution.py:51
  (16 shorter events, 0.1 us)
Async XLA Ops:
  0.6 2.9 %copy-start = (f32[2,2048,200]{1,2,0:T(8,128)S(1)}, f32[2,2048,200]{1,2,0:T(8,128)}, u32[]{:S(2)}) copy-start(f32[2,2048,200]{1,2,0:T(8,128)} %param.7) | copy-start | bytes 9830404
  3.5 0.8 copy-start.1
  3.5 0.8 copy-start.2
  3.5 0.8 copy-start.6
  38.8 51.1 %copy-start.3 = (f32[200]{0:T(256)S(1)}, f32[200]{0:T(256)}, u32[]{:S(2)}) copy-start(f32[200]{0:T(256)} %param.11) | copy-start | bytes 2404
  98.2 21.2 %all-to-all-start.2 = ((bf16[32,64,128]{2,1,0:T(8,128)(2,1)}), bf16[32,64,128]{2,1,0:T(8,128)(2,1)S(1)}, u32[]{:S(2)}, u32[]{:S(2)}) async-start(bf16[32,64,128]{2,1,0:T(8,128)(2,1)} %get-tuple-element.28), calls=%async_computation.2 | async-start | bytes 1048576 | tf_op jit(solution)/shard_map/all_to_all | solution.py:536
  119.4 11.9 %copy-start.4 = (f32[200]{0:T(256)S(1)}, f32[200]{0:T(256)}, u32[]{:S(2)}) copy-start(f32[200]{0:T(256)} %param.12) | copy-start | bytes 2404
  119.4 11.9 %copy-start.5 = (f32[200]{0:T(256)S(1)}, f32[200]{0:T(256)}, u32[]{:S(2)}) copy-start(f32[200]{0:T(256)} %param.13) | copy-start | bytes 2404
  126.0 11.3 %collective-permute-start = (f32[400,1024]{1,0:T(8,128)S(1)}, f32[400,1024]{1,0:T(8,128)S(1)}, u32[]{:S(2)}, u32[]{:S(2)}) collective-permute-start(f32[400,1024]{1,0:T(8,128)S(1)} %get-tuple-element.40.send_ref), channel_id=1, source_target_pairs={{0,32},{32,0},{64,96},{96,64},{128,160},{160,128},{192,224},{224,1... | collective-permute-start | bytes 4915208 | tf_op jit(solution)/shard_map/ppermute | solution.py:603
  166.6 3.5 %collective-permute-start.1 = (bf16[2,200,1024]{2,1,0:T(8,128)(2,1)S(1)}, bf16[2,200,1024]{2,1,0:T(8,128)(2,1)S(1)}, u32[]{:S(2)}, u32[]{:S(2)}) collective-permute-start(bf16[2,200,1024]{2,1,0:T(8,128)(2,1)S(1)} %get-tuple-element.42), channel_id=1, source_target_pairs={{0,32},{32,0},{64,96},{96,64},{128,160},{160,128},{192,224},{224,1... | collective-permute-start | bytes 2457608 | tf_op jit(solution)/shard_map/ppermute | solution.py:626

commit v6 on v5

--- a/solution.py
+++ b/solution.py
@@ -58,7 +58,41 @@
     )(*args)
 
 
-def place_kernel(peers, capacity, shift, per, slice_ref, where_ref, ids_ref, counts_ref, code_ref, doc_ref, count_ref):
+HEAD = 128
+
+
+def open_kernel(
+    peers,
+    capacity,
+    shift,
+    per,
+    where_ref,
+    slice_hbm,
+    ids_hbm,
+    counts_hbm,
+    beta_hbm,
+    beta_ref,
+    out_ref,
+    doc_ref,
+    count_ref,
+    slice_ref,
+    ids_ref,
+    counts_ref,
+    small_sems,
+    sems,
+):
+    small = []
+    for k, (source, target) in enumerate(((ids_hbm, ids_ref), (counts_hbm, counts_ref), (slice_hbm, slice_ref))):
+        small.append(pltpu.make_async_copy(source, target, small_sems.at[k]))
+        small[k].start()
+    size = beta_ref.shape[0] // sems.shape[0]
+    loads = []
+    for c in range(sems.shape[0]):
+        at = pl.ds(c * size, size)
+        loads.append(pltpu.make_async_copy(beta_hbm.at[at], beta_ref.at[at], sems.at[c]))
+        loads[c].start()
+    for load in small:
+        load.wait()
     docs, width = ids_ref.shape
     ids = ids_ref[...]
     owner = lax.shift_right_logical(ids, shift)
@@ -93,12 +127,29 @@
         )
     placed = mmg(jnp.concatenate(left, axis=1), jnp.concatenate(right, axis=1), NT)
     low_p, high_p, doc_p, count_p = (placed[i * peers : (i + 1) * peers] for i in range(4))
-    code_ref[...] = doc_p * 8192.0 + high_p * 256.0 + low_p
+    code = doc_p * 8192.0 + high_p * 256.0 + low_p
     doc_ref[...] = jnp.where(high_p > 0.5, doc_p, -1.0)
     count_ref[...] = count_p
-
-
-HEAD = 128
+    both = []
+    left_side = iota((size, HEAD), 1) < HEAD // 2
+    for c, load in enumerate(loads):
+        load.wait()
+        rows = beta_ref[c * size : (c + 1) * size, :]
+        top = jnp.max(rows, axis=1, keepdims=True)
+        mass = jnp.sum(jnp.exp(rows - top), axis=1, keepdims=True)
+        both.append(jnp.where(left_side, top, mass))
+    full = beta_ref.shape[0] // HEAD
+    last = beta_ref.shape[0] - full * HEAD
+    both.append(jnp.zeros((HEAD - last, HEAD), F32))
+    both = jnp.transpose(jnp.concatenate(both, axis=0))
+    both = [both[0:1], both[HEAD // 2 : HEAD // 2 + 1]]
+    common = jnp.concatenate([b[:, k * HEAD : (k + 1) * HEAD] for b in both for k in range(full)], axis=0)
+    rest = [b[:, full * HEAD : full * HEAD + last] for b in both]
+    rest.append(jnp.zeros((1, 2 * HEAD - capacity - 2 * last), F32))
+    rest = jnp.concatenate(rest, axis=1)
+    for s in range(peers):
+        second = jnp.concatenate([code[s : s + 1, HEAD:], rest], axis=1)
+        out_ref[s] = jnp.concatenate([code[s : s + 1, :HEAD], second, common], axis=0)
 
 
 def at_of(code):
@@ -118,6 +169,32 @@
     for s in range(rows_ref.shape[0]):
         g, i = divmod(s, group)
         flat_ref[g : g + 1, i * capacity : (i + 1) * capacity] = rows_ref[s : s + 1, :]
+
+
+def flatten_codes(flat_ref, message_ref, capacity):
+    groups = flat_ref.shape[0]
+    group = message_ref.shape[0] // groups
+    for s in range(message_ref.shape[0]):
+        g, i = divmod(s, group)
+        at = i * capacity
+        flat_ref[g : g + 1, at : at + HEAD] = message_ref[s, 0:1, :]
+        flat_ref[g : g + 1, at + HEAD : at + capacity] = message_ref[s, 1:2, : capacity - HEAD]
+
+
+def log_norm_of(message_ref, rows, spare):
+    full = rows // HEAD
+    last = rows - full * HEAD
+
+    def merge(top, mass):
+        highest = jnp.max(top, axis=0)
+        return highest + jnp.log(jnp.sum(mass * jnp.exp(top - highest[None]), axis=0))
+
+    most = merge(message_ref[:, 2 : 2 + full, :], message_ref[:, 2 + full : 2 + 2 * full, :])
+    second = message_ref[:, 1, :]
+    end = merge(second[:, spare : spare + last], second[:, spare + last : spare + 2 * last])[None]
+    end = jnp.concatenate([end, jnp.zeros((1, HEAD - last), F32)], axis=1)
+    turned = jnp.transpose(jnp.concatenate([most, end, jnp.zeros((8 - full - 1, HEAD), F32)], axis=0))
+    return jnp.concatenate([turned[:, k : k + 1] for k in range(full)] + [turned[:last, full : full + 1]], axis=0)
 
 
 def tiles(count, grid, low, high):
@@ -138,18 +215,18 @@
     return jnp.concatenate(out, axis=1)
 
 
-def fetch_kernel(shift, beta_ref, norm_ref, asked_ref, table_ref, out_ref, flat_ref):
+def fetch_kernel(shift, capacity, beta_ref, message_ref, table_ref, out_ref, flat_ref):
     rows, words = beta_ref.shape
     topics = rows // 2
     tail = topics - HEAD
-    peers, capacity = asked_ref.shape
+    peers = message_ref.shape[0]
     groups = flat_ref.shape[0]
     group = peers // groups
-    norm = jnp.transpose(jnp.broadcast_to(norm_ref[...], (8, norm_ref.shape[1])))[:, 0:1]
+    norm = log_norm_of(message_ref, rows, capacity - HEAD)
     step = 40
     for r in range(0, rows, step):
         table_ref[r : r + step, :] = jnp.exp(beta_ref[r : r + step, :] - norm[r : r + step]).astype(BF16)
-    flatten(flat_ref, asked_ref, group)
+    flatten_codes(flat_ref, message_ref, capacity)
     third = tail // 3
     spare = capacity - HEAD
 
@@ -168,11 +245,10 @@
     lax.fori_loop(0, groups, one, 0)
 
 
-def index_kernel(shift, docs, pack, asked_ref, low_ref, block_ref, key_ref, flat_ref):
-    peers, capacity = asked_ref.shape
+def index_kernel(shift, docs, pack, capacity, message_ref, low_ref, block_ref, key_ref, flat_ref):
     groups, places = flat_ref.shape
-    group = peers // groups
-    flatten(flat_ref, asked_ref, group)
+    group = places // capacity
+    flatten_codes(flat_ref, message_ref, capacity)
     lane = iota((1, places), 1)
     chunk = low_ref.shape[1]
     grid = iota((places, chunk), 1).astype(F32)
@@ -516,20 +592,23 @@
         return pltpu.VMEM(dims, dtype)
 
     beta = jnp.swapaxes(beta_mean, 1, 2)
-    code, doc, count = call(
-        functools.partial(place_kernel, peers, capacity, shift, slice_dev),
-        [local(peers, capacity)] * 3,
+    beta, outgoing, doc, count = call(
+        functools.partial(open_kernel, peers, capacity, shift, slice_dev),
+        [local(rows, vocab_shard), local(peers, 8, HEAD), local(peers, capacity), local(peers, capacity)],
+        where,
         doc_slice,
-        where,
         word_ids,
         word_counts,
-        scalars=2,
-    )
-    top = jnp.max(beta, axis=2)
-    mass = jnp.sum(jnp.exp(beta - top[:, :, None]), axis=2)
-    stats = jnp.concatenate([top.reshape(1, 1, -1), mass.reshape(1, 1, -1)], axis=2)
-    outgoing = jnp.concatenate(
-        [code.reshape(peers, 1, capacity), jnp.broadcast_to(stats, (peers, 1, stats.shape[2]))], axis=2
+        beta.reshape(rows, vocab_shard),
+        scalars=1,
+        far=4,
+        scratch=[
+            pltpu.SMEM((docs,), I32),
+            local(docs, width, dtype=I32),
+            local(docs, width, dtype=I32),
+            pltpu.SemaphoreType.DMA((3,)),
+            pltpu.SemaphoreType.DMA((5,)),
+        ],
     )
 
     def exchange(value):
@@ -545,19 +624,12 @@
         scalars=1,
         scratch=[local(NCOEF, 2 * HEAD)],
     )
-    asked = arrived[:, 0, :capacity]
-    tops = arrived[:, 0, capacity : capacity + rows]
-    masses = arrived[:, 0, capacity + rows :]
-    highest = jnp.max(tops, axis=0)
-    log_norm = highest + jnp.log(jnp.sum(masses * jnp.exp(tops - highest), axis=0))
-    log_norm = jnp.pad(log_norm, (0, 4 * HEAD - rows)).reshape(1, -1)
     flat = local(groups, places // groups)
     table, fetched = call(
-        functools.partial(fetch_kernel, shift),
+        functools.partial(fetch_kernel, shift, capacity),
         [pltpu.HBM((rows, vocab_shard), BF16), pltpu.HBM((peers, packed, HEAD), BF16)],
-        beta.reshape(rows, vocab_shard),
-        log_norm,
-        asked,
+        beta,
+        arrived,
         scratch=[flat],
     )
     got = exchange(fetched)
@@ -577,12 +649,12 @@
             local(1, places),
         ],
     )
-    asked_late, factors = lax.optimization_barrier((asked, factors))
+    arrived, factors = lax.optimization_barrier((arrived, factors))
     factors = exchange(factors)
     low, block, key = call(
-        functools.partial(index_kernel, shift, docs, pack),
+        functools.partial(index_kernel, shift, docs, pack, capacity),
         [local(places, 2 * HEAD, dtype=BF16), local(1, places), local(1, places)],
-        asked_late,
+        arrived,
         scratch=[flat],
     )
     factors, low, block, key = lax.optimization_barrier((factors, low, block, key))

time: 174 us -> 173 us (level)
  other arithmetic: 3.51 us -> 0.08 us
  Pallas kernels: 43.8 us -> 46.9 us
    pallas_call x10, Pallas kernels: 43.8 us -> 46.9 us  [call(): pl.pallas_call(kernel, out_shape=outs, in_specs=[SMEM] * scalars + [VMEM]...]
    reduce_max x1 -> x0, other arithmetic: 2.31 us -> none  [per_device(): top = jnp.max(beta, axis=2)]
where the time goes in v6:
time: 173 us
  blocking collectives  96.8 us (56%)
  Pallas kernels  46.9 us (27%)
  starting transfers between devices  15.1 us (9%)
  waiting for transfers between devices  13.2 us (8%)
    all_to_all x2, blocking collectives, exchange(): return lax.all_to_all(value, 'doc', split_axis=0, concat_axis=0, tiled=True)  71.8 us
    pallas_call x10, Pallas kernels, call(): pl.pallas_call(kernel, out_shape=outs, in_specs=[SMEM] * scalars + [VMEM]...  46.9 us
    all_to_all x1, blocking collectives, per_device(): lax.all_to_all(combined, 'tm', split_axis=0, concat_axis=0, tiled=True, a...  24.9 us
    all_to_all x1, waiting for transfers between devices, exchange(): return lax.all_to_all(value, 'doc', split_axis=0, concat_axis=0, tiled=True)  11.3 us
    all_to_all x1, starting transfers between devices, exchange(): return lax.all_to_all(value, 'doc', split_axis=0, concat_axis=0, tiled=True)  8.36 us
    ppermute x1, starting transfers between devices, per_device(): recv = lax.ppermute(send, 'tm', swap)  5.22 us
  transfers between devices with their start and end apart: 3, of which 2 were waited for; matrix products, arithmetic and copies ran while one was open for 0% of the time, Pallas kernels for 4%

profile of v6, /device:TPU:1, one launch (start us, length us, event | category | flops | bytes accessed | tf_op | source)
XLA Modules:
  0.0 172.8 jit_solution(18354344475710181271)
XLA Ops:
  0.6 0.1 pad_add_fusion.chip_ref.where_ref
  0.7 4.3 %shard_map.87 = (f32[400,2048]{1,0:T(8,128)S(1)}, f32[32,8,128]{2,1,0:T(8,128)S(1)}, f32[32,160]{1,0:T(8,128)S(1)}, f32[32,160]{1,0:T(8,128)S(1)}) custom-call(s32[2]{0:T(128)S(1)} %pad_add_fusion.chip_ref.where_ref, s32[32]{0:T(128)} %slice_hbm.1, s32[32,128]{1,0:T(8,128)} %ids_hbm.1, s32[32,128]{1,0:T(8,128)} %counts_ref.1, f32[400,2048]{1,0:T(8,128)} %bitcast.12), custom_call_target="tpu_custom_call" | custom-call | tf_op jit(solution)/shard_map/pallas_call | solution.py:51
  5.0 20.8 %all_to_all.20.message_ref = f32[32,8,128]{2,1,0:T(8,128)S(1)} all-to-all(f32[32,8,128]{2,1,0:T(8,128)S(1)} %get-tuple-element.24), channel_id=1, replica_groups=mesh['tm'=8,'doc'=32] {'doc'}, dimensions={0} | all-to-all | bytes 262144 | tf_op jit(solution)/shard_map/all_to_all | solution.py:615
  25.8 11.7 %shard_map.88 = (bf16[400,2048]{1,0:T(8,128)(2,1)}, bf16[32,256,128]{2,1,0:T(8,128)(2,1)}) custom-call(f32[400,2048]{1,0:T(8,128)S(1)} %get-tuple-element.25.beta_ref, f32[32,8,128]{2,1,0:T(8,128)S(1)} %all_to_all.20.message_ref), custom_call_target="tpu_custom_call" | custom-call | tf_op jit(solution)/shard_map/pallas_call | solution.py:51
  37.6 0.0 copy-start
  37.6 0.0 copy-start.1
  37.6 51.0 %all_to_all.21.got_ref = bf16[32,256,128]{2,1,0:T(8,128)(2,1)S(1)} all-to-all(bf16[32,256,128]{2,1,0:T(8,128)(2,1)} %get-tuple-element.26), channel_id=1, replica_groups=mesh['tm'=8,'doc'=32] {'doc'}, dimensions={0} | all-to-all | bytes 4194304 | tf_op jit(solution)/shard_map/all_to_all | solution.py:615
  88.6 0.0 copy-done
  88.6 0.0 copy-done.1
  88.6 8.3 %shard_map.89 = (f32[32,200]{1,0:T(8,128)}, bf16[32,64,128]{2,1,0:T(8,128)(2,1)}) custom-call(bf16[32,256,128]{2,1,0:T(8,128)(2,1)S(1)} %all_to_all.21.got_ref, f32[32,160]{1,0:T(8,128)S(1)} %get-tuple-element.27.doc_rows, f32[32,160]{1,0:T(8,128)S(1)} %get-tuple-element.28.count_rows, s32[32,128]{1,0:T(8,128)S(1)} %copy-done, f32[1,200]{1,0:T(1,128)S(1)} %bitcast.9), custom_call_target="tpu_custom_call" | custom-call | tf_op jit(solution)/shard_map/pallas_call | solution.py:51
  96.9 8.4 %all-to-all-start.2 = ((bf16[32,64,128]{2,1,0:T(8,128)(2,1)}), bf16[32,64,128]{2,1,0:T(8,128)(2,1)S(1)}, u32[]{:S(2)}, u32[]{:S(2)}) async-start(bf16[32,64,128]{2,1,0:T(8,128)(2,1)} %get-tuple-element.30), calls=%async_computation.2 | async-start | bytes 1048576 | tf_op jit(solution)/shard_map/all_to_all | solution.py:615
  105.2 1.6 shard_map.90
  106.8 11.3 %all-to-all-done.2.factor_in = bf16[32,64,128]{2,1,0:T(8,128)(2,1)S(1)} async-done(((bf16[32,64,128]{2,1,0:T(8,128)(2,1)}), bf16[32,64,128]{2,1,0:T(8,128)(2,1)S(1)}, u32[]{:S(2)}, u32[]{:S(2)}) %all-to-all-start.2) | async-done | bytes 524320 | tf_op jit(solution)/shard_map/all_to_all | solution.py:615
  118.1 0.0 copy-start.2
  118.1 0.0 copy-start.3
  118.1 6.7 %shard_map.91 = (f32[400,1024]{1,0:T(8,128)S(1)}, bf16[200,5120]{1,0:T(8,128)(2,1)S(1)}, bf16[400,2048]{1,0:T(8,128)(2,1)S(1)}) custom-call(s32[2]{0:T(128)S(1)} %pad_add_fusion.chip_ref.where_ref, bf16[32,64,128]{2,1,0:T(8,128)(2,1)S(1)} %all-to-all-done.2.factor_in, f32[1,5120]{1,0:T(1,128)S(1)} %get-tuple-element.36.key_ref, ...), custom_call_target="tpu_custom_call" | custom-call | tf_op jit(solution)/shard_map/pallas_call | solution.py:51
  124.8 5.2 %collective-permute-start = (f32[400,1024]{1,0:T(8,128)S(1)}, f32[400,1024]{1,0:T(8,128)S(1)}, u32[]{:S(2)}, u32[]{:S(2)}) collective-permute-start(f32[400,1024]{1,0:T(8,128)S(1)} %get-tuple-element.42.send_ref), channel_id=1, source_target_pairs={{0,32},{32,0},{64,96},{96,64},{128,160},{160,128},{192,224},{224,1... | collective-permute-start | bytes 4915208 | tf_op jit(solution)/shard_map/ppermute | solution.py:675
  130.0 0.0 copy-done.2
  130.0 0.0 copy-done.3
  130.0 0.9 shard_map.86.coef_ref
  130.8 5.2 %shard_map.92.keep_ref = f32[400,1024]{1,0:T(8,128)S(1)} custom-call(s32[2]{0:T(128)S(1)} %pad_add_fusion.chip_ref.where_ref, bf16[200,5120]{1,0:T(8,128)(2,1)S(1)} %get-tuple-element.40.factor_ref, bf16[5120,256]{1,0:T(8,128)(2,1)S(1)} %get-tuple-element.37.low_ref, f32[1,5120]{1,0:T(1,128)S(1)} %get-tuple-element.38.block_ref, ...), custom_call_target="tpu_custom_call" | custom-call | tf_op jit(solution)/shard_map/pallas_call | solution.py:51
  136.1 0.0 collective-permute-done.recv_ref
  136.1 1.7 %shard_map.93 = bf16[4,200,1024]{2,1,0:T(8,128)(2,1)S(1)} custom-call(s32[2]{0:T(128)S(1)} %pad_add_fusion.chip_ref.where_ref, f32[200,32]{1,0:T(8,128)S(1)} %shard_map.86.coef_ref, f32[400,1024]{1,0:T(8,128)S(1)} %shard_map.92.keep_ref, f32[400,1024]{1,0:T(8,128)S(1)} %collective-permute-done.recv_ref), custom_call_target="tpu_custom_call" | custom-call | tf_op jit(solution)/shard_map/pallas_call | solution.py:51
  137.9 24.9 %all_to_all.22.far_ref = bf16[4,200,1024]{2,1,0:T(8,128)(2,1)S(1)} all-to-all(bf16[4,200,1024]{2,1,0:T(8,128)(2,1)S(1)} %shard_map.93), channel_id=1, replica_groups={{0,64,128,192},{32,96,160,224},{1,65,129,193},{33,97,161,225},{2,66,130..., dimensions={0} | all-to-all | bytes 3276800 | tf_op jit(solution)/shard_map/all_to_all | solution.py:680
  162.8 2.6 %shard_map.94 = (f32[2,200,1024]{2,1,0:T(8,128)S(1)}, bf16[2,200,1024]{2,1,0:T(8,128)(2,1)S(1)}) custom-call(s32[2]{0:T(128)S(1)} %pad_add_fusion.chip_ref.where_ref, f32[200,32]{1,0:T(8,128)S(1)} %shard_map.86.coef_ref, f32[400,1024]{1,0:T(8,128)S(1)} %shard_map.92.keep_ref, f32[400,1024]{1,0:T(8,128)S(1)} %collective-permute-done.recv_ref, ...), custom_call_target="tpu_custom_call" | custom-call | tf_op jit(solution)/shard_map/pallas_call | solution.py:51
  165.3 1.5 collective-permute-start.1
  166.9 2.0 %collective-permute-done.1.other_ref = bf16[2,200,1024]{2,1,0:T(8,128)(2,1)S(1)} collective-permute-done((bf16[2,200,1024]{2,1,0:T(8,128)(2,1)S(1)}, bf16[2,200,1024]{2,1,0:T(8,128)(2,1)S(1)}, u32[]{:S(2)}, u32[]{:S(2)}) %collective-permute-start.1) | collective-permute-done | bytes 819232 | tf_op jit(solution)/shard_map/ppermute | solution.py:698
  168.8 4.0 %shard_map.95 = f32[2,200,2048]{2,1,0:T(8,128)} custom-call(s32[2]{0:T(128)S(1)} %pad_add_fusion.chip_ref.where_ref, f32[200,32]{1,0:T(8,128)S(1)} %shard_map.86.coef_ref, f32[400,1024]{1,0:T(8,128)S(1)} %shard_map.92.keep_ref, f32[400,1024]{1,0:T(8,128)S(1)} %get-tuple-element.42.send_ref, f32[2,200,1024]{2,1,0:T(8,128)S(1)} %get-tuple-element.43.own_ref, ...), custom_call_target="tpu_custom_call" | custom-call | tf_op jit(solution)/shard_map/pallas_call | solution.py:51
Async XLA Ops:
  37.6 51.0 %copy-start = (s32[32,128]{1,0:T(8,128)S(1)}, s32[32,128]{1,0:T(8,128)}, u32[]{:S(2)}) copy-start(s32[32,128]{1,0:T(8,128)} %counts_ref.1) | copy-start | bytes 49156
  37.6 51.0 %copy-start.1 = (f32[200]{0:T(256)S(1)}, f32[200]{0:T(256)}, u32[]{:S(2)}) copy-start(f32[200]{0:T(256)} %param.11) | copy-start | bytes 2404
  96.9 21.2 %all-to-all-start.2 = ((bf16[32,64,128]{2,1,0:T(8,128)(2,1)}), bf16[32,64,128]{2,1,0:T(8,128)(2,1)S(1)}, u32[]{:S(2)}, u32[]{:S(2)}) async-start(bf16[32,64,128]{2,1,0:T(8,128)(2,1)} %get-tuple-element.30), calls=%async_computation.2 | async-start | bytes 1048576 | tf_op jit(solution)/shard_map/all_to_all | solution.py:615
  118.1 11.9 %copy-start.2 = (f32[200]{0:T(256)S(1)}, f32[200]{0:T(256)}, u32[]{:S(2)}) copy-start(f32[200]{0:T(256)} %param.12) | copy-start | bytes 2404
  118.1 11.9 %copy-start.3 = (f32[200]{0:T(256)S(1)}, f32[200]{0:T(256)}, u32[]{:S(2)}) copy-start(f32[200]{0:T(256)} %param.13) | copy-start | bytes 2404
  124.8 11.3 %collective-permute-start = (f32[400,1024]{1,0:T(8,128)S(1)}, f32[400,1024]{1,0:T(8,128)S(1)}, u32[]{:S(2)}, u32[]{:S(2)}) collective-permute-start(f32[400,1024]{1,0:T(8,128)S(1)} %get-tuple-element.42.send_ref), channel_id=1, source_target_pairs={{0,32},{32,0},{64,96},{96,64},{128,160},{160,128},{192,224},{224,1... | collective-permute-start | bytes 4915208 | tf_op jit(solution)/shard_map/ppermute | solution.py:675
  165.3 3.5 %collective-permute-start.1 = (bf16[2,200,1024]{2,1,0:T(8,128)(2,1)S(1)}, bf16[2,200,1024]{2,1,0:T(8,128)(2,1)S(1)}, u32[]{:S(2)}, u32[]{:S(2)}) collective-permute-start(bf16[2,200,1024]{2,1,0:T(8,128)(2,1)S(1)} %get-tuple-element.44), channel_id=1, source_target_pairs={{0,32},{32,0},{64,96},{96,64},{128,160},{160,128},{192,224},{224,1... | collective-permute-start | bytes 2457608 | tf_op jit(solution)/shard_map/ppermute | solution.py:698
